TPU v7x, 32 devices: a whole 2x2x4 slice. The times are simulated.
32 devices in a mesh: dp: 4 (over x, core), ctx: 4 (over z), tensor: 2 (over y).
Axes of the slice: x: 2, y: 2, z: 4, core: 2. Of those that a mesh axis runs over, the one named last changes fastest.
Arguments:
- out_grad: bfloat16 [4, 1024, 4096], P('dp', ('ctx', 'tensor')), may hold values from -1 to 1
- prev_state: bfloat16 [4, 1024, 4096], P('dp', 'ctx', 'tensor'), may hold values from -6 to 6
- boundary: int32 [4, 1024], P('dp', 'ctx'), may hold values 0 or 1
- angle_code: int32 [64, 32], P('tensor'), may hold values from 0 to 4095
- radius_code: int32 [64, 32], P('tensor'), may hold values from 0 to 1023
- reflect: float32 [64, 4, 64], P('tensor'), may hold values from -6 to 6
Outputs:
- grad_input: bfloat16 [4, 1024, 4096], P('dp', 'ctx', 'tensor')
- grad_transition: float32 [64, 64, 64], P('tensor')
All inputs are finite; a program needn't handle non-finite values. No bound on the sum of `boundary` on one device may be relied on, other than what follows from the above.
Results may differ from a plain program's by a relative error of at most 0.003.
Values may be sent and summed in bfloat16 or wider, within the bound.
No kernel may reach another device: no remote copies, remote signals or barrier semaphores. Data moves between devices by JAX's collectives and lax.ppermute only.
A program may use at most 128 MiB of HBM per device.

v0:
```python
import math

import jax
import jax.numpy as jnp
from jax import lax
from jax.sharding import PartitionSpec as P

SUBLEN = 16


def entering(array, axis, combine, identity):
    peers, position = (lax.axis_size(axis), lax.axis_index(axis))
    everything = jax.tree.map(lambda part: lax.all_gather(part, axis), array)
    start = jax.tree.map(
        lambda part, zero: jnp.broadcast_to(jnp.asarray(zero, part.dtype), part.shape),
        array,
        identity,
    )

    def hop(k, before):
        at = peers - 1 - k
        reached = at > position
        new = combine(before, jax.tree.map(lambda part: part[at], everything))
        return jax.tree.map(lambda a, b: jnp.where(reached, a, b), new, before)

    return lax.fori_loop(0, peers, hop, start)


def transition(angle_code, radius_code, reflect):
    block_count = radius_code.shape[0]
    block_size = 2 * radius_code.shape[1]
    rates = jnp.exp2(-(4.0 + radius_code.astype(jnp.float32) * (10.0 / 1024.0)))
    radius = 1.0 - rates
    angles = angle_code.astype(jnp.float32) * (math.pi / 4096.0)
    cosine = jnp.repeat(radius * jnp.cos(angles), 2, axis=1)[:, :, None]
    sine_part = jnp.repeat(radius * jnp.sin(angles), 2, axis=1)[:, :, None]
    row_index = jnp.arange(block_size)[:, None]
    col_index = jnp.arange(block_size)[None, :]
    on_diagonal = row_index == col_index
    upper_pair = (row_index % 2 == 0) & (col_index == row_index + 1)
    lower_pair = (row_index % 2 == 1) & (col_index == row_index - 1)
    zero_value = jnp.float32(0.0)
    rotation = (
        jnp.where(on_diagonal[None], cosine, zero_value)
        + jnp.where(upper_pair[None], -sine_part, zero_value)
        + jnp.where(lower_pair[None], sine_part, zero_value)
    )
    basis_now = jnp.broadcast_to(
        jnp.eye(block_size, dtype=jnp.float32), (block_count, block_size, block_size)
    )
    for reflect_index in range(4):
        reflector = reflect[:, reflect_index, :]
        norm_sq = jnp.sum(reflector * reflector, axis=1)
        projected = jnp.einsum("bij,bj->bi", basis_now, reflector, precision=lax.Precision.HIGHEST)
        basis_now = (
            basis_now - 2.0 * projected[:, :, None] * reflector[:, None, :] / norm_sq[:, None, None]
        )
    rotated = jnp.einsum("bij,bjk->bik", basis_now, rotation, precision=lax.Precision.HIGHEST)
    return jnp.einsum("bik,blk->bil", rotated, basis_now, precision=lax.Precision.HIGHEST)


def apply_blocks(matrix, vectors):
    return jnp.einsum("bxy,...by->...bx", matrix, vectors, precision=lax.Precision.HIGHEST)


def matrix_blocks(left_side, right_side):
    return jnp.einsum("bxy,byz->bxz", left_side, right_side, precision=lax.Precision.HIGHEST)


def power_stack(matrix, how_many):
    block_count, block_size = (matrix.shape[0], matrix.shape[1])
    stacked = jnp.broadcast_to(
        jnp.eye(block_size, dtype=jnp.float32), (1, block_count, block_size, block_size)
    )
    current = matrix
    while stacked.shape[0] < how_many:
        extended = jnp.einsum("qbxy,byz->qbxz", stacked, current, precision=lax.Precision.HIGHEST)
        stacked = jnp.concatenate([stacked, extended], axis=0)
        current = matrix_blocks(current, current)
    return stacked[:how_many]


def matrix_power(matrix, exponent_count):
    result = None
    base = matrix
    remaining = exponent_count
    while remaining > 0:
        if remaining % 2 == 1:
            result = base
        remaining = remaining // 2
        if remaining > 0:
            base = matrix_blocks(base, base)
    return result


def body(out_grad, prev_state, boundary, angle_code, radius_code, reflect):
    local_grad = lax.all_to_all(out_grad, "tensor", split_axis=2, concat_axis=1, tiled=True)
    transit = transition(angle_code, radius_code, reflect)
    transposed = jnp.swapaxes(transit, 1, 2)
    block_count, block_size = (transit.shape[0], transit.shape[1])
    token_count = local_grad.shape[1]
    sub_count = token_count // SUBLEN
    grad_rows = (
        local_grad[0].astype(jnp.float32).reshape(sub_count, SUBLEN, block_count, block_size)
    )
    retain = jnp.where(boundary[0] == 1, jnp.float32(0.6), jnp.float32(1.0)).reshape(
        sub_count, SUBLEN
    )

    def backstep(state_next, inputs):
        grad_row, keep_row = inputs
        adjoint = grad_row + keep_row[:, None, None] * apply_blocks(transposed, state_next)
        return (adjoint, adjoint)

    zero_state = jnp.zeros((sub_count, block_count, block_size), jnp.float32)
    unused_state, local_adj = lax.scan(
        backstep,
        zero_state,
        (jnp.swapaxes(grad_rows, 0, 1), jnp.swapaxes(retain, 0, 1)),
        reverse=True,
    )
    log_keep = jnp.log(retain)
    tail_logs = jnp.flip(jnp.cumsum(jnp.flip(log_keep, 1), axis=1), 1)
    tail_scale = jnp.exp(tail_logs)
    sub_logs = tail_logs[:, 0]
    total_log = jnp.sum(sub_logs)
    small_powers = power_stack(transposed, SUBLEN + 1)
    block_power = small_powers[SUBLEN]
    device_power = matrix_power(block_power, sub_count)
    starts = local_adj[0]

    def entry_step(entry_now, inputs):
        start_row, sub_log = inputs
        entry_before = start_row + jnp.exp(sub_log) * apply_blocks(block_power, entry_now)
        return (entry_before, entry_now)

    zero_vector = jnp.zeros((block_count, block_size), jnp.float32)
    device_first, unused_entries = lax.scan(
        entry_step, zero_vector, (starts, sub_logs), reverse=True
    )
    device_map = jnp.exp(total_log) * device_power

    def compose(earlier, nearer):
        return (
            nearer[0] + apply_blocks(nearer[1], earlier[0]),
            matrix_blocks(nearer[1], earlier[1]),
        )

    identity_blocks = jnp.broadcast_to(
        jnp.eye(block_size, dtype=jnp.float32), (block_count, block_size, block_size)
    )
    incoming, unused_matrix = entering(
        (device_first, device_map), "ctx", compose, (zero_vector, identity_blocks)
    )
    unused_first, entry_full = lax.scan(entry_step, incoming, (starts, sub_logs), reverse=True)
    small_chosen = jnp.flip(small_powers[1:], 0)
    correction = jnp.einsum(
        "ibxy,jby->ijbx", small_chosen, entry_full, precision=lax.Precision.HIGHEST
    )
    adjoint_all = local_adj + jnp.swapaxes(tail_scale, 0, 1)[:, :, None, None] * correction
    grad_input = (
        jnp.swapaxes(adjoint_all, 0, 1)
        .reshape(1, token_count, block_count * block_size)
        .astype(jnp.bfloat16)
    )
    previous = jnp.swapaxes(
        prev_state[0].astype(jnp.float32).reshape(sub_count, SUBLEN, block_count, block_size), 0, 1
    )
    partial_grad = jnp.einsum(
        "ijbx,ijby->bxy", adjoint_all, previous, precision=lax.Precision.HIGHEST
    )
    summed = lax.psum(partial_grad, ("dp", "ctx"))
    return (grad_input, summed)


def solution(mesh):
    in_specs = (
        P("dp", ("ctx", "tensor"), None),
        P("dp", "ctx", "tensor"),
        P("dp", "ctx"),
        P("tensor", None),
        P("tensor", None),
        P("tensor", None, None),
    )
    out_specs = (P("dp", "ctx", "tensor"), P("tensor", None, None))
    return jax.shard_map(body, mesh=mesh, in_specs=in_specs, out_specs=out_specs, check_vma=False)
```

profile of v0, /device:TPU:0, one launch (start us, length us, event | category | flops | bytes accessed | tf_op | source)
XLA Modules:
  0.0 459.4 jit_solution(16878735421799689898)
XLA Ops:
  7.2 5.0 %copy.70 = bf16[1,128,4096]{1,0,2:T(2,128)(2,1)S(1)} copy(bf16[1,128,4096]{2,1,0:T(8,128)(2,1)} %param.14) | data formatting | bytes 2097152 | tf_op args[0]
  12.7 22.4 %reduce.7 = bf16[4096,128]{1,0:T(8,128)(2,1)S(1)} reduce(bf16[4096,1,128]{2,1,0:T(2,128)(2,1)S(1)} %bitcast.233, bf16[]{:T(256)} %broadcast.175), dimensions={1}, to_apply=%bitcast.152.reduce_sub_computation | reduce | bytes 2097154
  36.3 4.4 all-to-all-start
  45.3 1.9 fusion.54
  47.3 2.4 fusion.67
  49.7 2.9 fusion.68
  53.1 3.0 fusion.48
  56.2 2.8 fusion.69
  59.0 1.9 fusion.93
  60.9 3.1 constant_dynamic-update-slice_fusion.2
  66.3 3.3 convolution_bitcast_fusion.1
  70.8 5.5 %constant_dynamic-update-slice_fusion.1 = (f32[16,32,64,64]{2,3,0,1:T(8,128)}, f32[31,32,64,64]{2,3,0,1:T(8,128)}, f32[2,32,64,64]{2,3,0,1:T(8,128)S(1)}) fusion(f32[16,32,64,64]{2,3,0,1:T(8,128)} %get-tuple-element.647, f32[31,32,64,64]{2,3,0,1:T(8,128)} %get-tuple-element.648, f32[32,64,64]{2,1,0:T(8,128)} %copy-done, ...), kind=kOutput, calls=%fused_computation.99 | convolution fusion | flops 201588736 | bytes 7340032 | tf_op jit(solution)/shard_map/qbxy,byz->qbxz/dot_general | solution.py:77
  76.3 6.3 %constant_dynamic-update-slice_fusion = (f32[16,32,64,64]{2,3,0,1:T(8,128)}, f32[31,32,64,64]{2,3,0,1:T(8,128)}, f32[4,32,64,64]{2,3,0,1:T(8,128)S(1)}) fusion(f32[16,32,64,64]{2,3,0,1:T(8,128)} %get-tuple-element.645, f32[31,32,64,64]{2,3,0,1:T(8,128)} %get-tuple-element.646, f32[2,32,64,64]{2,3,0,1:T(8,128)S(1)} %get-tuple-element.656, ...), kind=kOutput, calls=%fused_computation.98 | convolution fusion | flops 403701760 | bytes 13107200 | tf_op jit(solution)/shard_map/qbxy,byz->qbxz/dot_general | solution.py:77
  82.6 11.0 %bitcast_dynamic-update-slice_fusion.3 = (f32[16,32,64,64]{2,3,0,1:T(8,128)}, f32[31,32,64,64]{2,3,0,1:T(8,128)}) fusion(f32[16,32,64,64]{2,3,0,1:T(8,128)} %get-tuple-element.643, f32[31,32,64,64]{2,3,0,1:T(8,128)} %get-tuple-element.644, f32[4,32,64,64]{2,3,0,1:T(8,128)S(1)} %get-tuple-element.657, f32[2,32,64,64]{2,3,0,1:T(8,128)S(1)} %get-tuple-element.656, ...), kind=kOutput, calls=%fused_computation.35 | convolution fusion | flops 808452096 | bytes 21495808 | tf_op jit(solution)/shard_map/qbxy,byz->qbxz/dot_general | solution.py:77
  93.6 23.3 %constant_dynamic-update-slice_fusion.3 = (f32[31,32,64,64]{2,3,0,1:T(8,128)}, f32[16,32,64,64]{2,3,0,1:T(8,128)}) fusion(f32[31,32,64,64]{2,3,0,1:T(8,128)} %get-tuple-element.642, f32[32,64,64,1]{1,2,3,0:T(8,128)S(1)} %copy-done.5, f32[16,32,64,64]{2,3,0,1:T(8,128)} %get-tuple-element.641), kind=kOutput, calls=%fused_computation.101 | convolution fusion | flops 1610612736 | bytes 50855936 | tf_op jit(solution)/shard_map/qbxy,byz->qbxz/dot_general | solution.py:77
  116.9 3.4 fusion.89
  123.4 2.2 convolution_multiply_fusion.1
  127.9 4.6 %reshape.170 = bf16[16,16,32,64]{3,2,1,0:T(8,128)(2,1)} reshape(bf16[1,256,2048]{2,1,0:T(8,128)(2,1)} %param.15) | data formatting | bytes 2097152 | tf_op jit(solution)/shard_map/reshape | solution.py:167
  132.5 2.9 reshape.204
  135.5 4.9 %bitcast_convert_fusion = f32[1,128,4096]{1,0,2:T(1,128)} fusion(bf16[4096,1,128]{2,1,0:T(2,128)(2,1)} %reshape.204), kind=kLoop, calls=%fused_computation.141 | loop fusion | flops 524288 | bytes 3145728 | tf_op jit(solution)/shard_map/transpose | solution.py:119
  140.4 2.9 copy.71
  143.3 4.9 %reshape.171 = f32[16,16,32,64]{3,2,1,0:T(8,128)} reshape(f32[1,2,128,2048]{3,2,1,0:T(8,128)} %bitcast.232) | data formatting | bytes 4194304 | tf_op jit(solution)/shard_map/transpose | solution.py:119
  148.1 2.4 broadcast_in_dim.115
  150.5 55.6 %while.65 = (s32[]{:T(128)}, f32[16,32,64]{2,0,1:T(8,128)S(1)}, f32[16,16,32,64]{3,1,2,0:T(8,128)}, f32[16,16,32,64]{3,2,0,1:T(8,128)}, f32[16,16]{1,0:T(8,128)S...) while((s32[]{:T(128)}, f32[16,32,64]{2,0,1:T(8,128)S(1)}, ...), condition=%wide.region_5.6_spmd.clone, body=%wide.region_4.5_spmd.clone.sunk | while | flops 25264132 | bytes 1704255 | solution.py:116
  151.6 2.5 bitcast_dynamic-update-slice_fusion.8
  155.1 2.4 bitcast_dynamic-update-slice_fusion.8
  158.5 2.5 bitcast_dynamic-update-slice_fusion.8
  162.0 2.5 bitcast_dynamic-update-slice_fusion.8
  165.5 2.4 bitcast_dynamic-update-slice_fusion.8
  168.9 2.4 bitcast_dynamic-update-slice_fusion.8
  172.4 2.4 bitcast_dynamic-update-slice_fusion.8
  175.9 2.5 bitcast_dynamic-update-slice_fusion.8
  179.4 2.5 bitcast_dynamic-update-slice_fusion.8
  182.8 2.5 bitcast_dynamic-update-slice_fusion.8
  186.3 2.4 bitcast_dynamic-update-slice_fusion.8
  189.8 2.4 bitcast_dynamic-update-slice_fusion.8
  193.2 2.5 bitcast_dynamic-update-slice_fusion.8
  196.7 2.4 bitcast_dynamic-update-slice_fusion.8
  200.2 2.5 bitcast_dynamic-update-slice_fusion.8
  203.7 2.5 bitcast_dynamic-update-slice_fusion.8
  206.2 3.5 copy.83
  209.7 48.8 %while.66 = (s32[]{:T(128)}, f32[32,64]{1,0:T(8,128)S(1)}, f32[16,32,64]{2,1,0:T(8,128)S(1)}, f32[16]{0:T(128)S(1)}, f32[32,64,64]{2,1,0:T(8,128)S(1)}, /*index=5*/s32[]{:T(128)}, s32[]{:T(128)}, s32[]{:T(128)}) while((s32[]{:T(128)}, f32[32,64]{1,0:T(8,128)S(1)}, f32[16,32,64]{2,1,0:T(8,128)S(1)}, f32[16]{0:T(128)S(1)}, ...), condition=%wide.region_8.9_spmd.clone, body=%wide.region_7.8_spmd.clone.sunk | while | flops 1579012 | bytes 581767 | solution.py:138
  211.0 1.7 fusion.142
  214.0 1.7 fusion.142
  217.1 1.7 fusion.142
  220.1 1.7 fusion.142
  223.2 1.7 fusion.142
  226.2 1.7 fusion.142
  229.3 1.7 fusion.142
  232.3 1.7 fusion.142
  258.5 14.7 %all-gather = f32[128,64]{1,0:T(8,128)S(1)} all-gather(f32[32,64]{1,0:T(8,128)S(1)} %get-tuple-element.482), channel_id=2, replica_groups=mesh['dp'=4,'ctx'=4,'tensor'=2] {'ctx'}, dimensions={0}, use_global_device_ids=true | all-gather | bytes 40960 | tf_op jit(solution)/shard_map/all_gather | solution.py:13
  273.2 12.3 %while.67 = (s32[]{:T(128)}, f32[32,64]{1,0:T(8,128)S(1)}, s32[]{:T(128)}, f32[4,32,64]{2,1,0:T(8,128)S(1)}, f32[4,32,64,64]{3,2,1,0:T(8,128)}, /*index=5*/s32[]{:T(128)}, s32[]{:T(128)}, s32[]{:T(128)}, s32[]{:T(128)}) while((s32[]{:T(128)}, f32[32,64]{1,0:T(8,128)S(1)}, s32[]{:T(128)}, f32[4,32,64]{2,1,0:T(8,128)S(1)}, ...), condition=%wide.region_11.12_spmd.clone, body=%wide.region_10.11_spmd.clone.sunk | while | flops 1581064 | bytes 1114280 | solution.py:26
  273.5 3.0 fusion.145
  276.5 3.0 fusion.145
  279.5 3.0 fusion.145
  282.5 3.0 fusion.145
  285.5 48.8 %while.64 = (s32[]{:T(128)}, f32[32,64]{1,0:T(8,128)S(1)}, f32[16,32,64]{2,1,0:T(8,128)S(1)}, f32[16,32,64]{2,1,0:T(8,128)S(1)}, f32[16]{0:T(128)S(1)}, /*index=5*/f32[32,64,64]{2,1,0:T(8,128)S(1)}, s32[]{:T(128)}, s32[]{:T(128)}) while((s32[]{:T(128)}, f32[32,64]{1,0:T(8,128)S(1)}, f32[16,32,64]{2,1,0:T(8,128)S(1)}, ...), condition=%wide.region_13.14_spmd, body=%wide.region_12.13_spmd.sunk | while | flops 1576963 | bytes 598145 | solution.py:155
  334.3 11.8 %fusion.28 = f32[16,16,32,64]{3,1,0,2:T(8,128)S(1)} fusion(f32[16,16,32,64]{3,1,2,0:T(8,128)} %get-tuple-element.481, f32[31,32,64,64]{2,3,0,1:T(8,128)} %get-tuple-element.658, f32[16,16]{1,0:T(8,128)S(1)} %copy.82, f32[16,32,64,1]{2,1,0,3:T(8,128)S(1)} %bitcast.243), kind=kOutput, calls=%fused_computation.43 | convolution fusion | flops 403701760 | bytes 23200768 | tf_op jit(solution)/shard_map/ibxy,jby->ijbx/dot_general | solution.py:157
  346.1 1.9 copy-done.3
  348.0 6.5 %fusion.42 = f32[32,64,64]{2,1,0:T(8,128)} fusion(f32[16,16,32,64]{3,1,0,2:T(8,128)S(1)} %fusion.28, bf16[16,16,32,64]{3,2,1,0:T(8,128)(2,1)S(1)} %copy-done.6), kind=kOutput, calls=%fused_computation.53 | convolution fusion | flops 402653184 | bytes 3670016 | tf_op jit(solution)/shard_map/ijbx,ijby->bxy/dot_general | solution.py:169
  354.5 2.5 convert_bitcast_fusion
  358.5 2.4 convert_element_type.59
  360.9 88.9 %all-reduce.2.cloned.1.call-done = f32[32,64,64]{2,1,0:T(8,128)} async-done(((f32[32,64,64]{2,1,0:T(8,128)}), f32[32,64,64]{2,1,0:T(8,128)}) %all-reduce.2.cloned.1.call-update) | async-done | bytes 524304 | tf_op jit(solution)/shard_map/psum | solution.py:172
  449.8 2.3 copy.211
  (257 shorter events, 93.2 us)
Async XLA Ops:
  12.2 28.6 %copy-start.8 = (s32[32,32]{1,0:T(8,128)S(1)}, s32[32,32]{1,0:T(8,128)}, u32[]{:S(2)}) copy-start(s32[32,32]{1,0:T(8,128)} %param.17) | copy-start | bytes 12292
  12.2 28.6 %copy-start.9 = (s32[32,32]{1,0:T(8,128)S(1)}, s32[32,32]{1,0:T(8,128)}, u32[]{:S(2)}) copy-start(s32[32,32]{1,0:T(8,128)} %param.18) | copy-start | bytes 12292
  12.7 30.6 %copy-start.7 = (f32[32,4,64]{2,1,0:T(4,128)S(1)}, f32[32,4,64]{2,1,0:T(4,128)}, u32[]{:S(2)}) copy-start(f32[32,4,64]{2,1,0:T(4,128)} %param.19) | copy-start | bytes 98308
  36.3 96.2 %all-to-all-start = ((bf16[2,2,131072]{2,1,0:T(2,128)(2,1)}), bf16[2,2,131072]{2,1,0:T(2,128)(2,1)}, u32[]{:S(2)}, u32[]{:S(2)}) async-start(bf16[2,2,131072]{2,1,0:T(2,128)(2,1)} %reshape.203), calls=%async_computation | async-start | bytes 2097152 | tf_op jit(solution)/shard_map/all_to_all | solution.py:97
  40.7 232.5 %all-gather.4.cloned.1.call-start = ((), (), s32[]{:S(2)}) async-start(), calls=%async_computation.2 | async-start | bytes 5242880 | tf_op jit(solution)/shard_map/all_gather | solution.py:13
  59.0 6.2 %copy-start.1 = (f32[32,64,64]{2,1,0:T(8,128)}, f32[32,64,64]{2,1,0:T(8,128)S(1)}, u32[]{:S(2)}) copy-start(f32[32,64,64]{2,1,0:T(8,128)S(1)} %fusion.69) | copy-start | bytes 1572868
  60.9 3.1 copy-start
  63.9 5.6 %copy-start.10 = (s32[1,256]{1,0:T(1,128)S(1)}, s32[1,256]{1,0:T(1,128)}, u32[]{:S(2)}) copy-start(s32[1,256]{1,0:T(1,128)} %param.16) | copy-start | bytes 3076
  70.8 5.5 %copy-start.4 = (f32[1,32,64,64]{2,3,0,1:T(8,128)S(1)}, f32[1,32,64,64]{2,3,0,1:T(8,128)}, u32[]{:S(2)}) copy-start(f32[1,32,64,64]{2,3,0,1:T(8,128)} %broadcast_bitcast_fusion) | copy-start | bytes 1572868
  82.6 11.0 %copy-start.5 = (f32[32,64,64,1]{1,2,3,0:T(8,128)S(1)}, f32[32,64,64,1]{1,2,3,0:T(8,128)}, u32[]{:S(2)}) copy-start(f32[32,64,64,1]{1,2,3,0:T(8,128)} %convolution_bitcast_fusion.1) | copy-start | bytes 1572868
  123.4 4.0 copy-start.2
  125.6 324.2 %all-reduce.2.cloned.1.call-start = ((), (), s32[]{:S(2)}) async-start(), calls=%async_computation.1 | async-start | bytes 2097152 | tf_op jit(solution)/shard_map/psum | solution.py:172
  334.3 13.7 %copy-start.6 = (bf16[16,16,32,64]{3,2,1,0:T(8,128)(2,1)S(1)}, bf16[16,16,32,64]{3,2,1,0:T(8,128)(2,1)}, u32[]{:S(2)}) copy-start(bf16[16,16,32,64]{3,2,1,0:T(8,128)(2,1)} %reshape.170) | copy-start | bytes 3145732
  346.1 1.9 copy-start.3
Sparse Core Ops, SparseCore 0:
  125.8 83.8 all-gather.3
  354.7 95.0 all-reduce.1
where the time goes:
time: 468 us; the launch traced here: 459 us
  matrix products  204 us (44%)
  waiting for transfers between devices  89 us (19%)
  local copies, waits for them, and re-layouts  76.1 us (16%)
  other arithmetic  31.8 us (7%)
  loops' own time  23.7 us (5%)
  between operations  15.6 us (3%)
  blocking collectives  14.7 us (3%)
    dot_general x52, matrix products, apply_blocks(): jnp.einsum('bxy,...by->...bx', matrix, vectors, precision=lax.Precision.H...  106 us
    psum x1, waiting for transfers between devices, body(): summed = lax.psum(partial_grad, ('dp', 'ctx'))  88.9 us
    dot_general x5, matrix products, power_stack(): jnp.einsum('qbxy,byz->qbxz', stacked, current, precision=lax.Precision.HI...  49.2 us
    unnamed x4, other arithmetic  22.4 us
    dynamic_slice x32, local copies, waits for them, and re-layouts, body(): lax.scan(entry_step, zero_vector, (starts, sub_logs), reverse=True)  18.8 us
    unnamed x31, local copies, waits for them, and re-layouts  15.7 us
    dynamic_slice x16, local copies, waits for them, and re-layouts, body(): lax.scan(backstep, zero_state, (jnp.swapaxes(grad_rows, 0, 1), jnp.swapax...  15.5 us
    dot_general x8, matrix products, matrix_blocks(): jnp.einsum('bxy,byz->bxz', left_side, right_side, precision=lax.Precision...  15.4 us
  transfers between devices with their start and end apart: 3, of which 1 were waited for; matrix products, arithmetic and copies ran while one was open for 46% of the time, Pallas kernels for 0%

commit v1 on v0

v1 whole, which is shorter than its diff:
```python
import functools
import math

import jax
import jax.numpy as jnp
from jax import lax
from jax.experimental import pallas as pl
from jax.experimental.pallas import tpu as pltpu
from jax.sharding import PartitionSpec as P

F32 = jnp.float32
BF16 = jnp.bfloat16
LANES = 128
CHUNKS = 8
GROUP = 256
SIZE = 64


def iota(shape, dim):
    return lax.broadcasted_iota(jnp.int32, shape, dim)


def matmul(a, b, dims, precision=None):
    return lax.dot_general(a, b, (dims, ((), ())), precision=precision, preferred_element_type=F32)


def split(x):
    high = x.astype(BF16)
    return high, (x - high.astype(F32)).astype(BF16)


def setup_kernel(length, reflect_ref, angle_ref, radius_ref, keep_ref, high_ref, low_ref, tab_ref, hop_ref, ktab_ref, u_ref):
    step = pl.program_id(0)
    rows = reflect_ref.shape[0]
    blocks = rows // 4

    @pl.when(step == 0)
    def _():
        v = [reflect_ref[pl.ds(k, blocks, stride=4), :] for k in range(4)]
        u = []
        for k in range(4):
            now = v[k]
            for l in range(k):
                now = now - u[l] * jnp.sum(v[l] * v[k], axis=1, keepdims=True)
            u.append(now * (2.0 / jnp.sum(v[k] * v[k], axis=1, keepdims=True)))
        for k in range(4):
            u_ref[pl.ds(k, blocks, stride=4), :] = u[k]
        chunk = keep_ref[pl.ds(0, CHUNKS, stride=length), :]
        for i in range(1, length):
            chunk = chunk * keep_ref[pl.ds(i, CHUNKS, stride=length), :]
        row = iota((CHUNKS, LANES), 0)

        def later(x, k):
            return jnp.where(row < CHUNKS - k, pltpu.roll(x, CHUNKS - k, 0), 1.0)

        def earlier(x, k):
            return jnp.where(row >= k, pltpu.roll(x, k, 0), 1.0)

        two = chunk * later(chunk, 1)
        four = two * later(two, 2)
        before = earlier(chunk, 1)
        before = before * earlier(before, 1)
        before = before * earlier(before, 2)
        before = before * earlier(before, 4)
        eight = four * later(four, 4)
        ktab_ref[0] = chunk
        ktab_ref[1] = two
        ktab_ref[2] = four
        ktab_ref[3] = before
        ktab_ref[4] = jnp.broadcast_to(eight[0:1], (CHUNKS, LANES))

    width = GROUP
    own = iota((16, width), 0) // 4 == iota((16, width), 1) // SIZE
    at = pl.ds(pl.multiple_of(step * 16, 16), 16)
    v16 = reflect_ref[at, :]
    u16 = u_ref[at, :]
    v16 = jnp.where(own, jnp.concatenate([v16] * 4, axis=1), 0.0)
    u16 = jnp.where(own, jnp.concatenate([u16] * 4, axis=1), 0.0)
    column = iota((width, width), 1)
    half = column // LANES
    inside = column % LANES
    source = (inside // 32) * SIZE + (inside % 32) * 2 + half
    order = jnp.where(iota((width, width), 0) == source, 1.0, 0.0).astype(F32)
    v16 = matmul(v16, order, ((1,), (0,)), lax.Precision.HIGHEST)
    basis = order - matmul(u16, v16, ((0,), (0,)), lax.Precision.HIGHEST)
    high, low = split(basis)
    high_ref[0] = high
    low_ref[0] = low

    code = angle_ref[0]
    rate = jnp.exp(-math.log(2.0) * (4.0 + radius_ref[0].astype(F32) * (10.0 / 1024.0)))
    series = jnp.full_like(rate, 1.0 / 8.0)
    for n in range(7, 0, -1):
        series = series * rate + 1.0 / n
    log_radius = -rate * series

    def power(n):
        turn = ((n * code) & 8191).astype(F32) * (math.pi / 4096.0)
        size = jnp.exp(n.astype(F32) * log_radius)
        return size * jnp.cos(turn), -size * jnp.sin(turn)

    row = iota((CHUNKS, LANES), 0)
    n = jnp.where(row == 0, 1, jnp.where(row == 1, length, jnp.where(row == 2, 2 * length, jnp.where(row == 3, 4 * length, 8 * length))))
    re, im = power(n)
    tab_ref[0, 0] = re
    tab_ref[0, 1] = im
    re, im = power(row * length)
    hop_ref[0, 0] = re
    hop_ref[0, 1] = im


def setup(reflect, angle, radius, keep):
    blocks = reflect.shape[0]
    groups = blocks // 4
    tokens = keep.shape[0]
    whole = lambda shape: pl.BlockSpec(shape, lambda g: (0,) * len(shape))
    each = lambda shape: pl.BlockSpec((1,) + shape, lambda g: (g,) + (0,) * len(shape))
    return pl.pallas_call(
        functools.partial(setup_kernel, tokens // CHUNKS),
        grid=(groups,),
        in_specs=[whole((blocks * 4, SIZE)), each((1, LANES)), each((1, LANES)), whole((tokens, LANES))],
        out_specs=[
            each((GROUP, GROUP)),
            each((GROUP, GROUP)),
            each((2, CHUNKS, LANES)),
            each((2, CHUNKS, LANES)),
            whole((5, CHUNKS, LANES)),
        ],
        out_shape=[
            jax.ShapeDtypeStruct((groups, GROUP, GROUP), BF16),
            jax.ShapeDtypeStruct((groups, GROUP, GROUP), BF16),
            jax.ShapeDtypeStruct((groups, 2, CHUNKS, LANES), F32),
            jax.ShapeDtypeStruct((groups, 2, CHUNKS, LANES), F32),
            jax.ShapeDtypeStruct((5, CHUNKS, LANES), F32),
        ],
        scratch_shapes=[pltpu.VMEM((blocks * 4, SIZE), F32)],
        name="setup",
        cost_estimate=pl.CostEstimate(flops=groups * 60_000_000, bytes_accessed=groups * 300_000, transcendentals=groups * 10_000),
    )(reflect.reshape(blocks * 4, SIZE), angle.reshape(groups, 1, LANES), radius.reshape(groups, 1, LANES), keep)


def times(a, b):
    return a[0] * b[0] - a[1] * b[1], a[0] * b[1] + a[1] * b[0]


def first_kernel(length, peers, place_ref, *refs):
    own_ref, others, rest = refs[0], refs[1:peers], refs[peers:]
    high_ref, low_ref, tab_ref, hop_ref, ktab_ref, keep_ref, re_ref, im_ref, head_ref, first_ref, rows_ref = rest
    count = own_ref.shape[0]
    place = place_ref[0]
    rows_ref[pl.ds(pl.multiple_of(place * count, count), count), :] = own_ref[...]
    for k in range(1, peers):
        rows_ref[pl.ds(pl.multiple_of((place ^ k) * count, count), count), :] = others[k - 1][...]
    rows = rows_ref[...]
    out = matmul(rows, high_ref[0], ((1,), (0,))) + matmul(rows, low_ref[0], ((1,), (0,)))
    re_ref[...] = out[:, :LANES]
    im_ref[...] = out[:, LANES:]
    shape = (CHUNKS, LANES)
    unit = (jnp.broadcast_to(tab_ref[0, 0, 0:1], shape), jnp.broadcast_to(tab_ref[0, 1, 0:1], shape))
    at = pl.ds(length - 1, CHUNKS, stride=length)
    state = (re_ref[at, :], im_ref[at, :])
    for i in range(length - 2, -1, -1):
        at = pl.ds(i, CHUNKS, stride=length)
        keep = keep_ref[at, :]
        turned = times(unit, state)
        state = (re_ref[at, :] + keep * turned[0], im_ref[at, :] + keep * turned[1])
    head_ref[0, 0] = state[0]
    head_ref[0, 1] = state[1]
    moved = times((hop_ref[0, 0], hop_ref[0, 1]), state)
    before = ktab_ref[3]
    first_ref[0, 0] = jnp.sum(moved[0] * before, axis=0, keepdims=True)
    first_ref[0, 1] = jnp.sum(moved[1] * before, axis=0, keepdims=True)


def first_pass(place, parts, high, low, tab, hop, ktab, keep):
    peers = len(parts)
    count, channels = parts[0].shape
    groups = channels // GROUP
    tokens = keep.shape[0]
    each = lambda shape: pl.BlockSpec((1,) + shape, lambda g, *_: (g,) + (0,) * len(shape))
    whole = lambda shape: pl.BlockSpec(shape, lambda g, *_: (0,) * len(shape))
    columns = lambda n, w: pl.BlockSpec((n, w), lambda g, *_: (0, g))
    return pl.pallas_call(
        functools.partial(first_kernel, tokens // CHUNKS, peers),
        grid_spec=pltpu.PrefetchScalarGridSpec(
            num_scalar_prefetch=1,
            grid=(groups,),
            in_specs=[columns(count, GROUP)] * peers
            + [
                each((GROUP, GROUP)),
                each((GROUP, GROUP)),
                each((2, CHUNKS, LANES)),
                each((2, CHUNKS, LANES)),
                whole((5, CHUNKS, LANES)),
                whole((tokens, LANES)),
            ],
            out_specs=[columns(tokens, LANES), columns(tokens, LANES), each((2, CHUNKS, LANES)), each((2, 1, LANES))],
            scratch_shapes=[pltpu.VMEM((tokens, GROUP), BF16)],
        ),
        out_shape=[
            jax.ShapeDtypeStruct((tokens, groups * LANES), F32),
            jax.ShapeDtypeStruct((tokens, groups * LANES), F32),
            jax.ShapeDtypeStruct((groups, 2, CHUNKS, LANES), F32),
            jax.ShapeDtypeStruct((groups, 2, 1, LANES), F32),
        ],
        name="first_pass",
        cost_estimate=pl.CostEstimate(flops=groups * 70_000_000, bytes_accessed=groups * 700_000, transcendentals=0),
    )(place, *parts, high, low, tab, hop, ktab, keep)


def second_kernel(length, re_ref, im_ref, head_ref, entry_ref, high_ref, low_ref, tab_ref, ktab_ref, keep_ref, prev_ref, out_ref, grad_ref, zr_ref, zi_ref):
    shape = (CHUNKS, LANES)
    row = iota(shape, 0)
    table = lambda n: (jnp.broadcast_to(tab_ref[0, 0, n : n + 1], shape), jnp.broadcast_to(tab_ref[0, 1, n : n + 1], shape))
    entry = (jnp.broadcast_to(entry_ref[0, 0], shape), jnp.broadcast_to(entry_ref[0, 1], shape))
    moved = times(table(1), entry)
    last = row == CHUNKS - 1
    chunk = ktab_ref[0]
    scan = tuple(head_ref[0, c] + jnp.where(last, chunk * moved[c], 0.0) for c in range(2))
    for n in range(3):
        k = 1 << n
        near = tuple(jnp.where(row < CHUNKS - k, pltpu.roll(x, CHUNKS - k, 0), 0.0) for x in scan)
        moved = times(table(n + 1), near)
        scan = tuple(scan[c] + ktab_ref[n] * moved[c] for c in range(2))
    state = tuple(jnp.where(last, entry[c], pltpu.roll(scan[c], CHUNKS - 1, 0)) for c in range(2))
    unit = table(0)
    for i in range(length - 1, -1, -1):
        at = pl.ds(i, CHUNKS, stride=length)
        keep = keep_ref[at, :]
        turned = times(unit, state)
        state = (re_ref[at, :] + keep * turned[0], im_ref[at, :] + keep * turned[1])
        zr_ref[at, :] = state[0]
        zi_ref[at, :] = state[1]
    z_high, z_low = split(jnp.concatenate([zr_ref[...], zi_ref[...]], axis=1))
    contract = ((1,), (1,))
    adjoint = matmul(z_high, high_ref[0], contract) + matmul(z_high, low_ref[0], contract) + matmul(z_low, high_ref[0], contract)
    a_high, a_low = split(adjoint)
    out_ref[...] = a_high
    prev = prev_ref[...]
    grad = matmul(a_high, prev, ((0,), (0,))) + matmul(a_low, prev, ((0,), (0,)))
    left = iota((SIZE, LANES), 1) < SIZE
    for q in range(2):
        lanes = slice(q * LANES, (q + 1) * LANES)
        grad_ref[q * SIZE : (q + 1) * SIZE, :] = jnp.where(
            left, grad[q * LANES : q * LANES + SIZE, lanes], grad[q * LANES + SIZE : (q + 1) * LANES, lanes]
        )


def second_pass(re, im, head, entry, high, low, tab, ktab, keep, prev):
    tokens, channels = prev.shape
    groups = channels // GROUP
    each = lambda shape: pl.BlockSpec((1,) + shape, lambda g: (g,) + (0,) * len(shape))
    whole = lambda shape: pl.BlockSpec(shape, lambda g: (0,) * len(shape))
    columns = lambda n, w: pl.BlockSpec((n, w), lambda g: (0, g))
    return pl.pallas_call(
        functools.partial(second_kernel, tokens // CHUNKS),
        grid=(groups,),
        in_specs=[
            columns(tokens, LANES),
            columns(tokens, LANES),
            each((2, CHUNKS, LANES)),
            each((2, 1, LANES)),
            each((GROUP, GROUP)),
            each((GROUP, GROUP)),
            each((2, CHUNKS, LANES)),
            whole((5, CHUNKS, LANES)),
            whole((tokens, LANES)),
            columns(tokens, GROUP),
        ],
        out_specs=[columns(tokens, GROUP), pl.BlockSpec((2 * SIZE, LANES), lambda g: (g, 0))],
        out_shape=[
            jax.ShapeDtypeStruct((tokens, channels), BF16),
            jax.ShapeDtypeStruct((groups * 2 * SIZE, LANES), F32),
        ],
        scratch_shapes=[pltpu.VMEM((tokens, LANES), F32), pltpu.VMEM((tokens, LANES), F32)],
        name="second_pass",
        cost_estimate=pl.CostEstimate(flops=groups * 180_000_000, bytes_accessed=groups * 900_000, transcendentals=0),
    )(re, im, head, entry, high, low, tab, ktab, keep, prev)


def unpack_kernel(x_ref, o_ref):
    for n in range(x_ref.shape[0] // SIZE):
        rows = x_ref[n * SIZE : (n + 1) * SIZE, :]
        o_ref[2 * n] = rows[:, :SIZE]
        o_ref[2 * n + 1] = rows[:, SIZE:]


def unpack(x):
    blocks = x.shape[0] // SIZE * 2
    return pl.pallas_call(
        unpack_kernel, out_shape=jax.ShapeDtypeStruct((blocks, SIZE, SIZE), F32), name="unpack"
    )(x)


def swap(x, axis, k):
    n = lax.axis_size(axis)
    return lax.ppermute(x, axis, [(i, i ^ k) for i in range(n)])


def entering(first, total, far, axis):
    peers, place = lax.axis_size(axis), lax.axis_index(axis)
    entry = (jnp.zeros_like(first[0]), jnp.zeros_like(first[1]))
    gap = (jnp.ones_like(first[0]), jnp.zeros_like(first[0]))
    k = 1
    while k < peers:
        rows = first[0].shape[0]
        got = swap(jnp.concatenate([first[0], first[1], jnp.broadcast_to(total, (8, LANES))]), axis, k)
        other = (got[:rows], got[rows : 2 * rows])
        other_total = got[2 * rows : 2 * rows + 1]
        early = (place // k) % 2 == 0
        reach = times(gap, other)
        entry = tuple(jnp.where(early, e + r, e) for e, r in zip(entry, reach))
        if 2 * k < peers:
            step = times(gap, far)
            gap = tuple(jnp.where(early, other_total * s, g) for s, g in zip(step, gap))
            near = tuple(jnp.where(early, a, b) for a, b in zip(first, other))
            late = tuple(jnp.where(early, b, a) for a, b in zip(first, other))
            moved = times(far, late)
            first = tuple(a + jnp.where(early, total, other_total) * b for a, b in zip(near, moved))
            total = total * other_total
            far = times(far, far)
        k *= 2
    return entry


def total_sum(x, axes):
    steps = []
    for axis in axes:
        k = 1
        while k < lax.axis_size(axis):
            steps.append((axis, k))
            k *= 2
    done = []
    for axis, k in steps[:-1]:
        bit = (lax.axis_index(axis) // k) % 2
        m = x.shape[0] // 2
        away = lax.dynamic_slice_in_dim(x, (1 - bit) * m, m, 0)
        x = lax.dynamic_slice_in_dim(x, bit * m, m, 0) + swap(away, axis, k)
        done.append((axis, k, bit))
    axis, k = steps[-1]
    x = x + swap(x, axis, k)
    for axis, k, bit in done[::-1]:
        other = swap(x, axis, k)
        x = jnp.where(bit == 0, jnp.concatenate([x, other]), jnp.concatenate([other, x]))
    return x


def body(out_grad, prev_state, boundary, angle_code, radius_code, reflect):
    peers, place = lax.axis_size("tensor"), lax.axis_index("tensor")
    rows = out_grad[0]
    channels = prev_state.shape[2]
    tokens = prev_state.shape[1]
    part = lambda at: lax.dynamic_slice_in_dim(rows, at * channels, channels, 1)
    parts = [part(place)] + [swap(part(place ^ k), "tensor", k) for k in range(1, peers)]
    keep = jnp.where(boundary[0] == 1, F32(0.6), F32(1.0))
    keep = jnp.broadcast_to(keep[:, None], (tokens, LANES))
    high, low, tab, hop, ktab = setup(reflect, angle_code, radius_code, keep)
    re, im, head, first = first_pass(jnp.reshape(place, (1,)), parts, high, low, tab, hop, ktab, keep)
    far = (tab[:, 0, 4], tab[:, 1, 4])
    entry = entering((first[:, 0, 0], first[:, 1, 0]), ktab[4, :1], far, "ctx")
    entry = jnp.stack(entry, axis=1)[:, :, None, :]
    grad_input, partial = second_pass(re, im, head, entry, high, low, tab, ktab, keep, prev_state[0])
    summed = unpack(total_sum(partial, ("dp", "ctx")))
    return grad_input[None], summed


def solution(mesh):
    in_specs = (
        P("dp", ("ctx", "tensor"), None),
        P("dp", "ctx", "tensor"),
        P("dp", "ctx"),
        P("tensor", None),
        P("tensor", None),
        P("tensor", None, None),
    )
    out_specs = (P("dp", "ctx", "tensor"), P("tensor", None, None))
    return jax.shard_map(body, mesh=mesh, in_specs=in_specs, out_specs=out_specs, check_vma=False)
```

time: 468 us -> 79.8 us (0.17); the launches traced: 459 us -> 79.2 us
  matrix products: 204 us -> 0 us
  local copies, waits for them, and re-layouts: 76.1 us -> 7.5 us
  waiting for transfers between devices: 89 us -> 21.6 us
  other arithmetic: 31.8 us -> 2.25 us
  Pallas kernels: 0 us -> 29 us
  loops' own time: 23.7 us -> 0 us
  between operations: 15.6 us -> 0.83 us
  blocking collectives: 14.7 us -> 0 us
  starting transfers between devices: 4.5 us -> 18.1 us
    dot_general x73 -> x0, matrix products: 204 us -> none  [the longest x52 106 us: apply_blocks(): jnp.einsum('bxy,...by->...bx', matrix, vectors, precision=lax.Precision.H...]
    psum x1 -> x0, waiting for transfers between devices: 88.9 us -> none  [body(): summed = lax.psum(partial_grad, ('dp', 'ctx'))]
    dynamic_slice x48 -> x4, local copies, waits for them, and re-layouts: 34.3 us -> 3.16 us  [the longest x1 2.09 us: body(): part = lambda at: lax.dynamic_slice_in_dim(rows, at * channels, channels, 1)]
    pallas_call x0 -> x4, Pallas kernels: none -> 29 us  [the longest x1 10.7 us: second_pass(): pl.pallas_call(functools.partial(second_kernel, tokens // CHUNKS), grid=(...]
    another operation x4 -> x0, loops' own time: 23.7 us -> none  [the longest x1 11.5 us: body(): lax.scan(entry_step, zero_vector, (starts, sub_logs), reverse=True)]
    unnamed x4 -> x0, other arithmetic: 22.4 us -> none
    ppermute x0 -> x10, waiting for transfers between devices: none -> 21.6 us  [swap(): return lax.ppermute(x, axis, [(i, i ^ k) for i in range(n)])]
    ppermute x0 -> x10, starting transfers between devices: none -> 18.1 us  [swap(): return lax.ppermute(x, axis, [(i, i ^ k) for i in range(n)])]
  transfers between devices with their start and end apart: 3 -> 10, of which waited for: 1 -> 10; matrix products, arithmetic and copies ran while one was open for 46% -> 4% of each run, Pallas kernels for 0% -> 11%
where the time goes in v1:
time: 79.8 us; the launch traced here: 79.2 us
  Pallas kernels  29 us (36%)
  waiting for transfers between devices  21.6 us (27%)
  starting transfers between devices  18.1 us (23%)
  local copies, waits for them, and re-layouts  7.5 us (9%)
  other arithmetic  2.25 us (3%)
  between operations  0.83 us (1%)
    ppermute x10, waiting for transfers between devices, swap(): return lax.ppermute(x, axis, [(i, i ^ k) for i in range(n)])  21.6 us
    ppermute x10, starting transfers between devices, swap(): return lax.ppermute(x, axis, [(i, i ^ k) for i in range(n)])  18.1 us
    pallas_call x1, Pallas kernels, second_pass(): pl.pallas_call(functools.partial(second_kernel, tokens // CHUNKS), grid=(...  10.7 us
    pallas_call x1, Pallas kernels, setup(): pl.pallas_call(functools.partial(setup_kernel, tokens // CHUNKS), grid=(g...  8.55 us
    pallas_call x1, Pallas kernels, first_pass(): pl.pallas_call(functools.partial(first_kernel, tokens // CHUNKS, peers),...  7.49 us
    pallas_call x1, Pallas kernels, unpack(): pl.pallas_call(unpack_kernel, out_shape=jax.ShapeDtypeStruct((blocks, SIZ...  2.21 us
    dynamic_slice x1, local copies, waits for them, and re-layouts, body(): part = lambda at: lax.dynamic_slice_in_dim(rows, at * channels, channels, 1)  2.09 us
  transfers between devices with their start and end apart: 10, of which 10 were waited for; matrix products, arithmetic and copies ran while one was open for 4% of the time, Pallas kernels for 11%

profile of v1, /device:TPU:0, one launch (start us, length us, event | category | flops | bytes accessed | tf_op | source)
XLA Modules:
  0.0 79.2 jit_solution(4611544512767910213)
XLA Ops:
  0.6 0.0 copy-start.3
  0.7 2.1 %dynamic-slice_bitcast_fusion = (bf16[128,2048]{1,0:T(8,128)(2,1)S(1)}, bf16[128,2048]{1,0:T(8,128)(2,1)}) fusion(bf16[1,128,4096]{2,1,0:T(8,128)(2,1)} %param.6, s32[]{:T(128)S(6)} %select_n.147, s32[]{:T(128)S(6)} %select_n.146), kind=kLoop, calls=%fused_computation.1 | loop fusion | bytes 2097160 | tf_op jit(solution)/shard_map/dynamic_slice | solution.py:353
  2.7 0.0 copy-start.4
  2.7 3.0 %collective-permute-start = (bf16[128,2048]{1,0:T(8,128)(2,1)S(1)}, bf16[128,2048]{1,0:T(8,128)(2,1)S(1)}, u32[]{:S(2)}, u32[]{:S(2)}) collective-permute-start(bf16[128,2048]{1,0:T(8,128)(2,1)S(1)} %get-tuple-element.24), channel_id=1, source_target_pairs={{0,1},{1,0},{2,3},{3,2},{4,5},{5,4},{6,7},{7,6},{8,9},{9,8},{10,11... | collective-permute-start | bytes 1572872 | tf_op jit(solution)/shard_map/ppermute | solution.py:297
  5.7 0.0 copy-done.3
  5.7 0.7 reshape.32.angle_ref
  6.4 0.0 copy-done.4
  6.4 0.0 copy-start.5
  6.4 0.7 reshape.33.radius_ref
  7.1 0.0 copy-done.5
  7.1 0.8 broadcast_in_dim.39.keep_ref.refs_7_
  7.9 8.5 %setup.1 = (bf16[8,256,256]{2,1,0:T(8,128)(2,1)}, bf16[8,256,256]{2,1,0:T(8,128)(2,1)}, f32[8,2,8,128]{3,2,1,0:T(8,128)}, f32[8,2,8,128]{3,2,1,0:T(8,128)}, f32[5,8,128]{2,1,0:T(8,128)}) custom-call(f32[128,64]{1,0:T(8,128)} %bitcast.81, s32[8,1,128]{2,1,0:T(1,128)} %reshape.32.angle_ref, s32[8,1,128]{2,1,0:T(1,128)} %reshape.33.radius_ref, ...), custom_call_target="tpu_custom_call" | custom-call | flops 480000000 | bytes 2400000 | tf_op jit(solution)/shard_map/setup/pallas_call | solution.py:118
  16.4 0.7 slice_bitcast_fusion.5
  17.1 0.6 collective-permute-done.refs_1_
  17.7 0.0 copy-start.2
  17.7 0.8 copy-done.2
  18.4 7.5 %first_pass.1 = (f32[256,1024]{1,0:T(8,128)}, f32[256,1024]{1,0:T(8,128)}, f32[8,2,8,128]{3,2,1,0:T(8,128)}, f32[8,2,1,128]{3,2,1,0:T(1,128)}) custom-call(s32[1]{0:T(128)} %bitcast.place_ref, bf16[128,2048]{1,0:T(8,128)(2,1)} %get-tuple-element.25.refs_0_, bf16[128,2048]{1,0:T(8,128)(2,1)} %copy-done.2, ...), custom_call_target="tpu_custom_call" | custom-call | flops 560000000 | bytes 5600000 | tf_op jit(solution)/shard_map/first_pass/pallas_call | solution.py:183
  25.9 0.0 copy-start
  25.9 0.7 copy.8
  26.7 1.9 %collective-permute-start.1 = (f32[24,128]{1,0:T(8,128)S(1)}, f32[24,128]{1,0:T(8,128)S(1)}, u32[]{:S(2)}, u32[]{:S(2)}) collective-permute-start(f32[24,128]{1,0:T(8,128)S(1)} %pad_maximum_fusion), channel_id=1, source_target_pairs={{0,2},{2,0},{4,6},{6,4},{1,3},{3,1},{5,7},{7,5},{8,10},{10,8},{12,... | collective-permute-start | bytes 36872 | tf_op jit(solution)/shard_map/ppermute | solution.py:297
  28.5 0.0 copy-done
  28.6 1.9 %collective-permute-done.1 = f32[24,128]{1,0:T(8,128)S(1)} collective-permute-done((f32[24,128]{1,0:T(8,128)S(1)}, f32[24,128]{1,0:T(8,128)S(1)}, u32[]{:S(2)}, u32[]{:S(2)}) %collective-permute-start.1) | collective-permute-done | bytes 12320 | tf_op jit(solution)/shard_map/ppermute | solution.py:297
  30.4 0.7 fusion
  31.2 2.9 %collective-permute-start.2 = (f32[24,128]{1,0:T(8,128)S(1)}, f32[24,128]{1,0:T(8,128)S(1)}, u32[]{:S(2)}, u32[]{:S(2)}) collective-permute-start(f32[24,128]{1,0:T(8,128)S(1)} %pad_maximum_fusion.1), channel_id=1, source_target_pairs={{0,4},{2,6},{4,0},{6,2},{1,5},{3,7},{5,1},{7,3},{8,12},{10,14},{12... | collective-permute-start | bytes 36872 | tf_op jit(solution)/shard_map/ppermute | solution.py:297
  34.0 1.8 %collective-permute-done.2 = f32[24,128]{1,0:T(8,128)S(1)} collective-permute-done((f32[24,128]{1,0:T(8,128)S(1)}, f32[24,128]{1,0:T(8,128)S(1)}, u32[]{:S(2)}, u32[]{:S(2)}) %collective-permute-start.2) | collective-permute-done | bytes 12320 | tf_op jit(solution)/shard_map/ppermute | solution.py:297
  35.8 0.6 pad_maximum_fusion.2
  36.4 10.7 %second_pass.1 = (bf16[256,2048]{1,0:T(8,128)(2,1)}, f32[1024,128]{1,0:T(8,128)}) custom-call(f32[256,1024]{1,0:T(8,128)} %get-tuple-element.18.re_ref, f32[256,1024]{1,0:T(8,128)} %get-tuple-element.19.im_ref, f32[8,2,8,128]{3,2,1,0:T(8,128)} %get-tuple-element.20.head_ref, f32[8,2,1,128]{3,2,1,0:T(1,128)} %bitcast.76, ...), custom_call_target="tpu_custom_call" | custom-call | flops 1440000000 | bytes 7200000 | tf_op jit(solution)/shard_map/second_pass/pallas_call | solution.py:255
  47.1 0.0 copy-start.1
  47.1 1.0 %constant_dynamic-slice_fusion.2 = f32[512,128]{1,0:T(8,128)S(1)} fusion(f32[1024,128]{1,0:T(8,128)} %get-tuple-element.23, s32[]{:T(128)S(6)} %select_n.174), kind=kLoop, calls=%fused_computation.26 | loop fusion | bytes 524292 | tf_op jit(solution)/shard_map/dynamic_slice | solution.py:337
  48.2 0.1 collective-permute-start.3
  48.3 1.5 %collective-permute-done.3 = f32[512,128]{1,0:T(8,128)S(1)} collective-permute-done((f32[512,128]{1,0:T(8,128)S(1)}, f32[512,128]{1,0:T(8,128)S(1)}, u32[]{:S(2)}, u32[]{:S(2)}) %collective-permute-start.3) | collective-permute-done | bytes 262176 | tf_op jit(solution)/shard_map/ppermute | solution.py:297
  49.8 0.0 copy-done.1
  49.9 1.8 %collective-permute-start.4 = (f32[256,128]{1,0:T(8,128)S(1)}, f32[256,128]{1,0:T(8,128)S(1)}, u32[]{:S(2)}, u32[]{:S(2)}) collective-permute-start(f32[256,128]{1,0:T(8,128)S(1)} %constant_dynamic-slice_fusion.1), channel_id=1, source_target_pairs={{0,16},{8,24},{16,0},{24,8},{1,17},{9,25},{17,1},{25,9},{2,18},{10... | collective-permute-start | bytes 393224 | tf_op jit(solution)/shard_map/ppermute | solution.py:297
  51.6 3.8 %collective-permute-done.4 = f32[256,128]{1,0:T(8,128)S(1)} collective-permute-done((f32[256,128]{1,0:T(8,128)S(1)}, f32[256,128]{1,0:T(8,128)S(1)}, u32[]{:S(2)}, u32[]{:S(2)}) %collective-permute-start.4) | collective-permute-done | bytes 131104 | tf_op jit(solution)/shard_map/ppermute | solution.py:297
  55.5 1.9 %collective-permute-start.5 = (f32[128,128]{1,0:T(8,128)S(1)}, f32[128,128]{1,0:T(8,128)S(1)}, u32[]{:S(2)}, u32[]{:S(2)}) collective-permute-start(f32[128,128]{1,0:T(8,128)S(1)} %constant_dynamic-slice_fusion), channel_id=1, source_target_pairs={{0,2},{2,0},{4,6},{6,4},{1,3},{3,1},{5,7},{7,5},{8,10},{10,8},{12,... | collective-permute-start | bytes 196616 | tf_op jit(solution)/shard_map/ppermute | solution.py:297
  57.4 2.5 %collective-permute-done.5 = f32[128,128]{1,0:T(8,128)S(1)} collective-permute-done((f32[128,128]{1,0:T(8,128)S(1)}, f32[128,128]{1,0:T(8,128)S(1)}, u32[]{:S(2)}, u32[]{:S(2)}) %collective-permute-start.5) | collective-permute-done | bytes 65568 | tf_op jit(solution)/shard_map/ppermute | solution.py:297
  59.8 2.9 %collective-permute-start.6 = (f32[128,128]{1,0:T(8,128)S(1)}, f32[128,128]{1,0:T(8,128)S(1)}, u32[]{:S(2)}, u32[]{:S(2)}) collective-permute-start(f32[128,128]{1,0:T(8,128)S(1)} %dynamic-slice_add_fusion.2), channel_id=1, source_target_pairs={{0,4},{2,6},{4,0},{6,2},{1,5},{3,7},{5,1},{7,3},{8,12},{10,14},{12... | collective-permute-start | bytes 196616 | tf_op jit(solution)/shard_map/ppermute | solution.py:297
  62.7 2.4 %collective-permute-done.6 = f32[128,128]{1,0:T(8,128)S(1)} collective-permute-done((f32[128,128]{1,0:T(8,128)S(1)}, f32[128,128]{1,0:T(8,128)S(1)}, u32[]{:S(2)}, u32[]{:S(2)}) %collective-permute-start.6) | collective-permute-done | bytes 65568 | tf_op jit(solution)/shard_map/ppermute | solution.py:297
  65.1 1.8 %collective-permute-start.7 = (f32[128,128]{1,0:T(8,128)S(1)}, f32[128,128]{1,0:T(8,128)S(1)}, u32[]{:S(2)}, u32[]{:S(2)}) collective-permute-start(f32[128,128]{1,0:T(8,128)S(1)} %add.101), channel_id=1, source_target_pairs={{0,2},{2,0},{4,6},{6,4},{1,3},{3,1},{5,7},{7,5},{8,10},{10,8},{12,... | collective-permute-start | bytes 196616 | tf_op jit(solution)/shard_map/ppermute | solution.py:297
  66.9 2.5 %collective-permute-done.7 = f32[128,128]{1,0:T(8,128)S(1)} collective-permute-done((f32[128,128]{1,0:T(8,128)S(1)}, f32[128,128]{1,0:T(8,128)S(1)}, u32[]{:S(2)}, u32[]{:S(2)}) %collective-permute-start.7) | collective-permute-done | bytes 65568 | tf_op jit(solution)/shard_map/ppermute | solution.py:297
  69.4 1.8 %collective-permute-start.8 = (f32[256,128]{1,0:T(8,128)S(1)}, f32[256,128]{1,0:T(8,128)S(1)}, u32[]{:S(2)}, u32[]{:S(2)}) collective-permute-start(f32[256,128]{1,0:T(8,128)S(1)} %maximum_select_fusion.2), channel_id=1, source_target_pairs={{0,16},{8,24},{16,0},{24,8},{1,17},{9,25},{17,1},{25,9},{2,18},{10... | collective-permute-start | bytes 393224 | tf_op jit(solution)/shard_map/ppermute | solution.py:297
  71.3 3.2 %collective-permute-done.8 = f32[256,128]{1,0:T(8,128)S(1)} collective-permute-done((f32[256,128]{1,0:T(8,128)S(1)}, f32[256,128]{1,0:T(8,128)S(1)}, u32[]{:S(2)}, u32[]{:S(2)}) %collective-permute-start.8) | collective-permute-done | bytes 131104 | tf_op jit(solution)/shard_map/ppermute | solution.py:297
  74.5 0.1 collective-permute-start.9
  74.6 1.5 %collective-permute-done.9 = f32[512,128]{1,0:T(8,128)S(1)} collective-permute-done((f32[512,128]{1,0:T(8,128)S(1)}, f32[512,128]{1,0:T(8,128)S(1)}, u32[]{:S(2)}, u32[]{:S(2)}) %collective-permute-start.9) | collective-permute-done | bytes 262176 | tf_op jit(solution)/shard_map/ppermute | solution.py:297
  76.1 0.8 %maximum_select_fusion.x_ref = f32[1024,128]{1,0:T(8,128)} fusion(f32[512,128]{1,0:T(8,128)S(1)} %collective-permute-done.9, f32[512,128]{1,0:T(8,128)S(1)} %maximum_select_fusion.1, pred[]{:T(512)S(6)} %eq.34), kind=kLoop, calls=%fused_computation | loop fusion | flops 393216 | bytes 1048577 | tf_op jit(solution)/shard_map/jit(_where)/select_n | solution.py:344
  76.9 2.2 %unpack.1 = f32[32,64,64]{2,1,0:T(8,128)} custom-call(f32[1024,128]{1,0:T(8,128)} %maximum_select_fusion.x_ref), custom_call_target="tpu_custom_call" | custom-call | tf_op jit(solution)/shard_map/unpack/pallas_call | solution.py:290
  (17 shorter events, 0.2 us)
Async XLA Ops:
  0.6 5.1 %copy-start.3 = (s32[32,32]{1,0:T(8,128)S(1)}, s32[32,32]{1,0:T(8,128)}, u32[]{:S(2)}) copy-start(s32[32,32]{1,0:T(8,128)} %param.9) | copy-start | bytes 12292
  2.7 3.7 %copy-start.4 = (s32[32,32]{1,0:T(8,128)S(1)}, s32[32,32]{1,0:T(8,128)}, u32[]{:S(2)}) copy-start(s32[32,32]{1,0:T(8,128)} %param.10) | copy-start | bytes 12292
  2.7 14.9 %collective-permute-start = (bf16[128,2048]{1,0:T(8,128)(2,1)S(1)}, bf16[128,2048]{1,0:T(8,128)(2,1)S(1)}, u32[]{:S(2)}, u32[]{:S(2)}) collective-permute-start(bf16[128,2048]{1,0:T(8,128)(2,1)S(1)} %get-tuple-element.24), channel_id=1, source_target_pairs={{0,1},{1,0},{2,3},{3,2},{4,5},{5,4},{6,7},{7,6},{8,9},{9,8},{10,11... | collective-permute-start | bytes 1572872 | tf_op jit(solution)/shard_map/ppermute | solution.py:297
  6.4 0.7 copy-start.5
  17.7 0.8 copy-start.2
  25.9 2.6 %copy-start = (f32[8,2,8,128]{3,2,1,0:T(8,128)S(1)}, f32[8,2,8,128]{3,2,1,0:T(8,128)}, u32[]{:S(2)}) copy-start(f32[8,2,8,128]{3,2,1,0:T(8,128)} %get-tuple-element.15.refs_4_.tab_ref) | copy-start | bytes 196612
  26.7 3.8 %collective-permute-start.1 = (f32[24,128]{1,0:T(8,128)S(1)}, f32[24,128]{1,0:T(8,128)S(1)}, u32[]{:S(2)}, u32[]{:S(2)}) collective-permute-start(f32[24,128]{1,0:T(8,128)S(1)} %pad_maximum_fusion), channel_id=1, source_target_pairs={{0,2},{2,0},{4,6},{6,4},{1,3},{3,1},{5,7},{7,5},{8,10},{10,8},{12,... | collective-permute-start | bytes 36872 | tf_op jit(solution)/shard_map/ppermute | solution.py:297
  31.2 4.7 %collective-permute-start.2 = (f32[24,128]{1,0:T(8,128)S(1)}, f32[24,128]{1,0:T(8,128)S(1)}, u32[]{:S(2)}, u32[]{:S(2)}) collective-permute-start(f32[24,128]{1,0:T(8,128)S(1)} %pad_maximum_fusion.1), channel_id=1, source_target_pairs={{0,4},{2,6},{4,0},{6,2},{1,5},{3,7},{5,1},{7,3},{8,12},{10,14},{12... | collective-permute-start | bytes 36872 | tf_op jit(solution)/shard_map/ppermute | solution.py:297
  47.1 2.6 %copy-start.1 = (f32[1024,128]{1,0:T(8,128)S(1)}, f32[1024,128]{1,0:T(8,128)}, u32[]{:S(2)}) copy-start(f32[1024,128]{1,0:T(8,128)} %get-tuple-element.23) | copy-start | bytes 1572868
  48.2 1.6 %collective-permute-start.3 = (f32[512,128]{1,0:T(8,128)S(1)}, f32[512,128]{1,0:T(8,128)S(1)}, u32[]{:S(2)}, u32[]{:S(2)}) collective-permute-start(f32[512,128]{1,0:T(8,128)S(1)} %constant_dynamic-slice_fusion.2), channel_id=1, source_target_pairs={{0,8},{8,0},{16,24},{24,16},{1,9},{9,1},{17,25},{25,17},{2,10},{10... | collective-permute-start | bytes 786440 | tf_op jit(solution)/shard_map/ppermute | solution.py:297
  49.9 5.6 %collective-permute-start.4 = (f32[256,128]{1,0:T(8,128)S(1)}, f32[256,128]{1,0:T(8,128)S(1)}, u32[]{:S(2)}, u32[]{:S(2)}) collective-permute-start(f32[256,128]{1,0:T(8,128)S(1)} %constant_dynamic-slice_fusion.1), channel_id=1, source_target_pairs={{0,16},{8,24},{16,0},{24,8},{1,17},{9,25},{17,1},{25,9},{2,18},{10... | collective-permute-start | bytes 393224 | tf_op jit(solution)/shard_map/ppermute | solution.py:297
  55.5 4.3 %collective-permute-start.5 = (f32[128,128]{1,0:T(8,128)S(1)}, f32[128,128]{1,0:T(8,128)S(1)}, u32[]{:S(2)}, u32[]{:S(2)}) collective-permute-start(f32[128,128]{1,0:T(8,128)S(1)} %constant_dynamic-slice_fusion), channel_id=1, source_target_pairs={{0,2},{2,0},{4,6},{6,4},{1,3},{3,1},{5,7},{7,5},{8,10},{10,8},{12,... | collective-permute-start | bytes 196616 | tf_op jit(solution)/shard_map/ppermute | solution.py:297
  59.8 5.2 %collective-permute-start.6 = (f32[128,128]{1,0:T(8,128)S(1)}, f32[128,128]{1,0:T(8,128)S(1)}, u32[]{:S(2)}, u32[]{:S(2)}) collective-permute-start(f32[128,128]{1,0:T(8,128)S(1)} %dynamic-slice_add_fusion.2), channel_id=1, source_target_pairs={{0,4},{2,6},{4,0},{6,2},{1,5},{3,7},{5,1},{7,3},{8,12},{10,14},{12... | collective-permute-start | bytes 196616 | tf_op jit(solution)/shard_map/ppermute | solution.py:297
  65.1 4.3 %collective-permute-start.7 = (f32[128,128]{1,0:T(8,128)S(1)}, f32[128,128]{1,0:T(8,128)S(1)}, u32[]{:S(2)}, u32[]{:S(2)}) collective-permute-start(f32[128,128]{1,0:T(8,128)S(1)} %add.101), channel_id=1, source_target_pairs={{0,2},{2,0},{4,6},{6,4},{1,3},{3,1},{5,7},{7,5},{8,10},{10,8},{12,... | collective-permute-start | bytes 196616 | tf_op jit(solution)/shard_map/ppermute | solution.py:297
  69.4 5.0 %collective-permute-start.8 = (f32[256,128]{1,0:T(8,128)S(1)}, f32[256,128]{1,0:T(8,128)S(1)}, u32[]{:S(2)}, u32[]{:S(2)}) collective-permute-start(f32[256,128]{1,0:T(8,128)S(1)} %maximum_select_fusion.2), channel_id=1, source_target_pairs={{0,16},{8,24},{16,0},{24,8},{1,17},{9,25},{17,1},{25,9},{2,18},{10... | collective-permute-start | bytes 393224 | tf_op jit(solution)/shard_map/ppermute | solution.py:297
  74.5 1.6 %collective-permute-start.9 = (f32[512,128]{1,0:T(8,128)S(1)}, f32[512,128]{1,0:T(8,128)S(1)}, u32[]{:S(2)}, u32[]{:S(2)}) collective-permute-start(f32[512,128]{1,0:T(8,128)S(1)} %maximum_select_fusion.1), channel_id=1, source_target_pairs={{0,8},{8,0},{16,24},{24,16},{1,9},{9,1},{17,25},{25,17},{2,10},{10... | collective-permute-start | bytes 786440 | tf_op jit(solution)/shard_map/ppermute | solution.py:297

commit v2 on v0

v2 whole, which is shorter than its diff:
```python
import functools
import math

import jax
import jax.numpy as jnp
from jax import lax
from jax.experimental import pallas as pl
from jax.experimental.pallas import tpu as pltpu
from jax.sharding import PartitionSpec as P


F32 = jnp.float32
BF16 = jnp.bfloat16
LANES = 128
CHUNKS = 8
GROUP = 256
SIZE = 64
TILE = (CHUNKS, LANES)
LIMIT = 16 << 20
NN = ((1,), (0,))
NT = ((1,), (1,))
TN = ((0,), (0,))


def iota(shape, dim):
    return lax.broadcasted_iota(jnp.int32, shape, dim)


def matmul(a, b, dims=NN, precision=None):
    return lax.dot_general(a, b, (dims, ((), ())), precision=precision, preferred_element_type=F32)


def split(x):
    high = x.astype(BF16)
    return high, (x - high.astype(F32)).astype(BF16)


def split3(x):
    high = x.astype(BF16)
    rest = x - high.astype(F32)
    middle = rest.astype(BF16)
    return high, middle, (rest - middle.astype(F32)).astype(BF16)


def times(a, b):
    return a[0] * b[0] - a[1] * b[1], a[0] * b[1] + a[1] * b[0]


def later(x, k, fill):
    return jnp.where(iota(TILE, 0) < CHUNKS - k, pltpu.roll(x, CHUNKS - k, 0), fill)


def earlier(x, k, fill):
    return jnp.where(iota(TILE, 0) >= k, pltpu.roll(x, k, 0), fill)


def power(tab_ref, g, n):
    return tuple(jnp.broadcast_to(tab_ref[g, c, n : n + 1], TILE) for c in range(2))


def entries(tab_ref, ktab_ref, g, head, entry):
    last = iota(TILE, 0) == CHUNKS - 1
    moved = times(power(tab_ref, g, 1), entry)
    scan = tuple(jnp.where(last, ktab_ref[0] * m, 0.0) for m in moved)
    if head is not None:
        scan = tuple(h + s for h, s in zip(head, scan))
    for n in range(3):
        near = tuple(later(x, 1 << n, 0.0) for x in scan)
        moved = times(power(tab_ref, g, 1 << n), near)
        scan = tuple(s + ktab_ref[n] * m for s, m in zip(scan, moved))
    return tuple(jnp.where(last, e, pltpu.roll(s, CHUNKS - 1, 0)) for e, s in zip(entry, scan))


def fold(x):
    block = (iota((SIZE, GROUP), 1) % LANES) // 32
    out = x[:SIZE]
    for j in range(1, 4):
        out = jnp.where(block == j, x[j * SIZE : (j + 1) * SIZE], out)
    return out


def walk(length, groups, units, states, keep_ref, load, store):
    for i in range(length - 1, -1, -1):
        at = pl.ds(i, CHUNKS, stride=length)
        keep = keep_ref[at, :]
        for n in range(groups):
            re, im = states[n]
            step_re, step_im = keep * units[n][0], keep * units[n][1]
            if load is None:
                states[n] = (step_re * re - step_im * im, step_re * im + step_im * re)
            else:
                a, b = load(n, at)
                states[n] = ((a + step_re * re) - step_im * im, (b + step_re * im) + step_im * re)
            if store is not None:
                store(n, at, states[n])
    return states


def prepare_kernel(length, reflect_ref, angle_ref, radius_ref, keep_ref, prev_hbm,
                   high_ref, low_ref, tab_ref, ktab_ref, far_ref, turned_ref, decay_ref, weight_ref, u_ref, prev_ref, prev_sem):
    fetch = pltpu.make_async_copy(prev_hbm, prev_ref, prev_sem)
    fetch.start()
    rows = reflect_ref.shape[0]
    blocks = rows // 4
    groups = blocks // 4

    chunk = keep_ref[pl.ds(0, CHUNKS, stride=length), :]
    for i in range(1, length):
        chunk = chunk * keep_ref[pl.ds(i, CHUNKS, stride=length), :]
    two = chunk * later(chunk, 1, 1.0)
    four = two * later(two, 2, 1.0)
    before = earlier(chunk, 1, 1.0)
    before = before * earlier(before, 1, 1.0)
    before = before * earlier(before, 2, 1.0)
    before = before * earlier(before, 4, 1.0)
    eight = four * later(four, 4, 1.0)
    ktab_ref[0] = chunk
    ktab_ref[1] = two
    ktab_ref[2] = four
    ktab_ref[3] = before
    ktab_ref[4] = jnp.broadcast_to(eight[0:1], TILE)

    row = iota(TILE, 0)
    n = jnp.where(row == 0, 1, row * length)
    for g in range(groups):
        code = angle_ref[g : g + 1, :]
        rate = jnp.exp(-math.log(2.0) * (4.0 + radius_ref[g : g + 1, :].astype(F32) * (10.0 / 1024.0)))
        series = jnp.full_like(rate, 1.0 / 8.0)
        for k in range(7, 0, -1):
            series = series * rate + 1.0 / k
        turn = ((n * code) & 8191).astype(F32) * (math.pi / 4096.0)
        size = jnp.exp(n.astype(F32) * (-rate * series))
        re, im = size * jnp.cos(turn), -size * jnp.sin(turn)
        tab_ref[g, 0] = re
        tab_ref[g, 1] = im
        half = (re[4:5], im[4:5])
        whole = times(half, half)
        far_ref[0, g : g + 1, :] = whole[0]
        far_ref[1, g : g + 1, :] = whole[1]

    v = [reflect_ref[pl.ds(k, blocks, stride=4), :] for k in range(4)]
    u = []
    for k in range(4):
        now = v[k]
        for l in range(k):
            now = now - u[l] * jnp.sum(v[l] * v[k], axis=1, keepdims=True)
        u.append(now * (2.0 / jnp.sum(v[k] * v[k], axis=1, keepdims=True)))
        u_ref[pl.ds(k, blocks, stride=4), :] = u[k]
    to = iota((SIZE, SIZE), 1)
    sort = jnp.where(iota((SIZE, SIZE), 0) == (to % 32) * 2 + to // 32, 1.0, 0.0).astype(F32)
    sorted_v = matmul(reflect_ref[...], sort, NN, lax.Precision.HIGHEST)
    wide = (rows, GROUP)
    block = (iota(wide, 0) // 4) % 4
    wide_v = jnp.concatenate([sorted_v[:, :32]] * 4 + [sorted_v[:, 32:]] * 4, axis=1)
    wide_v = split3(jnp.where(block == (iota(wide, 1) % LANES) // 32, wide_v, 0.0))
    wide_u = split3(jnp.where(block == iota(wide, 1) // SIZE, jnp.concatenate([u_ref[...]] * 4, axis=1), 0.0))
    to = iota((GROUP, GROUP), 1)
    order = jnp.where(iota((GROUP, GROUP), 0) == ((to % LANES) // 32) * SIZE + (to % 32) * 2 + to // LANES, 1.0, 0.0).astype(F32)
    for g in range(groups):
        at = slice(g * 16, (g + 1) * 16)
        left = jnp.concatenate([wide_u[n][at] for n in (0, 0, 1, 0, 1, 2)], axis=0)
        right = jnp.concatenate([wide_v[n][at] for n in (0, 1, 0, 2, 1, 0)], axis=0)
        high, low = split(order - matmul(left, right, TN))
        high_ref[g] = high
        low_ref[g] = low

    one, zero = jnp.ones(TILE, F32), jnp.zeros(TILE, F32)
    for first in range(0, groups, 4):
        some = range(first, min(first + 4, groups))
        states = [entries(tab_ref, ktab_ref, g, None, (one, zero)) for g in some]
        units = [power(tab_ref, g, 0) for g in some]

        def store(k, at, state):
            decay_ref[first + k, 0, at, :] = state[0]
            decay_ref[first + k, 1, at, :] = state[1]

        walk(length, len(some), units, states, keep_ref, None, store)
    fetch.wait()
    for g in range(groups):
        columns = slice(g * GROUP, (g + 1) * GROUP)
        turned = prev_ref[:, columns].T
        turned_ref[columns, :] = turned
        high, low = split(jnp.concatenate([decay_ref[g, 0], decay_ref[g, 1]], axis=1))
        weight_ref[g] = fold(matmul(turned, high) + matmul(turned, low))


VMEM = pl.BlockSpec(memory_space=pltpu.VMEM)
SMEM = pl.BlockSpec(memory_space=pltpu.SMEM)


def call(kernel, out_shape, args, specs, scratch=(), flops=0):
    shapes = [jax.ShapeDtypeStruct(s, t) for s, t in out_shape]
    moved = sum(a.size * a.dtype.itemsize for a in args) + sum(s.size * s.dtype.itemsize for s in shapes)
    return pl.pallas_call(
        kernel,
        out_shape=shapes,
        in_specs=specs,
        out_specs=[VMEM] * len(shapes),
        scratch_shapes=list(scratch),
        compiler_params=pltpu.CompilerParams(vmem_limit_bytes=LIMIT),
        cost_estimate=pl.CostEstimate(flops=int(flops), bytes_accessed=int(moved), transcendentals=0),
    )(*args)


def prepare(reflect, angle, radius, keep, prev):
    blocks = reflect.shape[0]
    groups = blocks // 4
    tokens, channels = prev.shape
    out = [
        ((groups, GROUP, GROUP), BF16),
        ((groups, GROUP, GROUP), BF16),
        ((groups, 2) + TILE, F32),
        ((5,) + TILE, F32),
        ((2, groups, LANES), F32),
        ((channels, tokens), BF16),
        ((groups, 2, tokens, LANES), F32),
        ((groups, SIZE, GROUP), F32),
    ]
    args = (reflect.reshape(blocks * 4, SIZE), angle.reshape(groups, LANES), radius.reshape(groups, LANES), keep, prev)
    return call(functools.partial(prepare_kernel, tokens // CHUNKS), out, args, [VMEM] * 4 + [pl.BlockSpec(memory_space=pl.ANY)],
                [pltpu.VMEM((blocks * 4, SIZE), F32), pltpu.VMEM((tokens, channels), BF16), pltpu.SemaphoreType.DMA], groups * 2 * 2 * 256**3)


def scan_kernel(length, base, count, peers, begin, finish, *refs):
    refs = list(refs)
    take = lambda n: [refs.pop(0) for _ in range(n)]
    tab_ref, ktab_ref, keep_ref = take(3)
    if begin:
        place_ref, own_ref, high_ref, low_ref = take(4)
        others = take(peers - 1)
    if begin and not finish:
        (ahead_ref,) = take(1)
    if finish:
        (turned_ref,) = take(1)
    if begin:
        out_ref, head_ref, first_ref = take(3) if not finish else take(1) + [None] + take(1)
    else:
        in_ref, head_ref, out_ref = take(3)
    if finish:
        (grad_ref,) = take(1)
    heads = []
    if begin:
        rows_ref, = take(1)
        spaced_ref = take(1)[0] if finish else out_ref
        size = own_ref.shape[0]
        width = count * GROUP
        place = place_ref[0]
        channels = high_ref.shape[0] * GROUP
        at = pl.ds(pl.multiple_of(place * size, size), size)
        rows_ref[at, :] = own_ref[:, pl.ds(pl.multiple_of(place * channels + base * GROUP, GROUP), width)]
        for k in range(1, peers):
            rows_ref[pl.ds(pl.multiple_of((place ^ k) * size, size), size), :] = others[k - 1][...]
        for n in range(count):
            rows = rows_ref[:, n * GROUP : (n + 1) * GROUP]
            out = matmul(rows, high_ref[base + n]) + matmul(rows, low_ref[base + n])
            spaced_ref[n, 0] = out[:, :LANES]
            spaced_ref[n, 1] = out[:, LANES:]
    else:
        spaced_ref = in_ref
    load = lambda n, at: (spaced_ref[n, 0, at, :], spaced_ref[n, 1, at, :])
    units = [power(tab_ref, base + n, 0) for n in range(count)]
    zero = jnp.zeros(TILE, F32)
    if begin and not finish:
        groups = base + count
        for c in range(2):
            first_ref[c * groups : c * groups + base, :] = ahead_ref[c]
        first_ref[2 * groups :, :] = ktab_ref[4]
    if begin:
        heads = walk(length, count, units, [(zero, zero)] * count, keep_ref, load, None)
        before = ktab_ref[3]
        for n in range(count):
            if head_ref is not None:
                head_ref[n, 0] = heads[n][0]
                head_ref[n, 1] = heads[n][1]
            hop = tuple(jnp.where(iota(TILE, 0) == 0, one, tab_ref[base + n, c]) for c, one in ((0, 1.0), (1, 0.0)))
            moved = times(hop, heads[n])
            for c in range(2):
                value = jnp.sum(moved[c] * before, axis=0, keepdims=True)
                if finish:
                    first_ref[c, n : n + 1, :] = value
                else:
                    first_ref[c * groups + base + n : c * groups + base + n + 1, :] = value
    else:
        heads = [(head_ref[n, 0], head_ref[n, 1]) for n in range(count)]
    if finish:
        states = [entries(tab_ref, ktab_ref, base + n, heads[n], (zero, zero)) for n in range(count)]

        def store(n, at, state):
            out_ref[n, 0, at, :] = state[0]
            out_ref[n, 1, at, :] = state[1]

        walk(length, count, units, states, keep_ref, load, store)
        for n in range(count):
            high, low = split(jnp.concatenate([out_ref[n, 0], out_ref[n, 1]], axis=1))
            turned = turned_ref[(base + n) * GROUP : (base + n + 1) * GROUP, :]
            grad_ref[n] = fold(matmul(turned, high) + matmul(turned, low))


def scan_both(base, count, place, rows, parts, high, low, tab, ktab, keep, turned):
    tokens = keep.shape[0]
    peers = len(parts) + 1
    out = [((count, 2, tokens, LANES), F32), ((2, count, LANES), F32), ((count, SIZE, GROUP), F32)]
    return call(functools.partial(scan_kernel, tokens // CHUNKS, base, count, peers, True, True), out,
                (tab, ktab, keep, place, rows, high, low, *parts, turned), [VMEM] * 3 + [SMEM] + [VMEM] * (peers + 3),
                [pltpu.VMEM((tokens, count * GROUP), BF16), pltpu.VMEM((count, 2, tokens, LANES), F32)], count * 4 * 2 * 256**3)


def scan_first(base, count, place, rows, parts, high, low, tab, ktab, keep, ahead):
    tokens = keep.shape[0]
    peers = len(parts) + 1
    out = [((count, 2, tokens, LANES), F32), ((count, 2) + TILE, F32), ((2 * (base + count) + CHUNKS, LANES), F32)]
    return call(functools.partial(scan_kernel, tokens // CHUNKS, base, count, peers, True, False), out,
                (tab, ktab, keep, place, rows, high, low, *parts, ahead), [VMEM] * 3 + [SMEM] + [VMEM] * (peers + 3),
                [pltpu.VMEM((tokens, count * GROUP), BF16)], count * 2 * 2 * 256**3)


def scan_second(base, count, spaced, head, tab, ktab, keep, turned):
    tokens = keep.shape[0]
    out = [((count, 2, tokens, LANES), F32), ((count, SIZE, GROUP), F32)]
    return call(functools.partial(scan_kernel, tokens // CHUNKS, base, count, 0, False, True), out,
                (tab, ktab, keep, turned, spaced, head), [VMEM] * 6, (), count * 2 * 2 * 256**3)


def merge_kernel(side_ref, a_ref, b_ref, weight_ref, entry_ref, own_ref, away_ref):
    half = a_ref.shape[0]
    side = side_ref[0]
    for n in range(half):
        for out_ref, which in ((own_ref, side), (away_ref, 1 - side)):
            here = jnp.where(which == 0, a_ref[n], b_ref[n])
            at = which * half + n
            re, im = entry_ref[0, pl.ds(at, 1), :], entry_ref[1, pl.ds(at, 1), :]
            weight = weight_ref[at]
            w_re, w_im = weight[:, :LANES], weight[:, LANES:]
            out_ref[n * SIZE : (n + 1) * SIZE, :LANES] = here[:, :LANES] + (re * w_re - im * w_im)
            out_ref[n * SIZE : (n + 1) * SIZE, LANES:] = here[:, LANES:] + (re * w_im + im * w_re)


def merge(side, a, b, weight, entry):
    rows = a.shape[0] * SIZE
    return call(merge_kernel, [((rows, GROUP), F32)] * 2, (side, a, b, weight, entry), [SMEM] + [VMEM] * 4)


def state_kernel(half, a_ref, b_ref, decay_ref, entry_ref, high_ref, low_ref, out_ref):
    g = pl.program_id(0)
    re, im = entry_ref[0, pl.ds(g, 1), :], entry_ref[1, pl.ds(g, 1), :]
    d_re, d_im = decay_ref[0, 0], decay_ref[0, 1]
    first = g < half
    z_re = jnp.where(first, a_ref[0, 0], b_ref[0, 0]) + (re * d_re - im * d_im)
    z_im = jnp.where(first, a_ref[0, 1], b_ref[0, 1]) + (re * d_im + im * d_re)
    z_high, z_low = split(jnp.concatenate([z_re, z_im], axis=1))
    out = matmul(z_high, high_ref[0], NT) + matmul(z_high, low_ref[0], NT) + matmul(z_low, high_ref[0], NT)
    out_ref[...] = out.astype(BF16)


def states(a, b, decay, entry, high, low):
    half, _, tokens, _ = a.shape
    groups = 2 * half
    each = lambda shape: pl.BlockSpec((1,) + shape, lambda g: (g, 0, 0, 0)[: len(shape) + 1])
    return pl.pallas_call(
        functools.partial(state_kernel, half),
        grid=(groups,),
        in_specs=[
            pl.BlockSpec((1, 2, tokens, LANES), lambda g: (jnp.minimum(g, half - 1), 0, 0, 0)),
            pl.BlockSpec((1, 2, tokens, LANES), lambda g: (jnp.maximum(g - half, 0), 0, 0, 0)),
            each((2, tokens, LANES)),
            pl.BlockSpec(entry.shape, lambda g: (0, 0, 0)),
            each((GROUP, GROUP)),
            each((GROUP, GROUP)),
        ],
        out_specs=pl.BlockSpec((tokens, GROUP), lambda g: (0, g)),
        out_shape=jax.ShapeDtypeStruct((tokens, groups * GROUP), BF16),
        name="states",
        compiler_params=pltpu.CompilerParams(vmem_limit_bytes=LIMIT),
        cost_estimate=pl.CostEstimate(flops=groups * 3 * 2 * 256**3, bytes_accessed=groups * 900_000, transcendentals=0),
    )(a, b, decay, entry, high, low)


def final_kernel(side_ref, own_ref, other_ref, high_ref, low_ref, out_ref):
    half = high_ref.shape[0] // 2
    side = side_ref[0]
    for x_ref, which in ((own_ref, side), (other_ref, 1 - side)):
        for n in range(half):
            at = which * half + n
            x_high, x_low = split(x_ref[n * SIZE : (n + 1) * SIZE, :])
            high = high_ref[at]
            out = matmul(high, x_high, NT) + matmul(high, x_low, NT) + matmul(low_ref[at], x_high, NT)
            for j in range(4):
                out_ref[at * 4 + j] = out[j * SIZE : (j + 1) * SIZE]


def final(side, own, other, high, low):
    blocks = high.shape[0] * 4
    return call(final_kernel, [((blocks, SIZE, SIZE), F32)], (side, own, other, high, low), [SMEM] + [VMEM] * 4)[0]


def swap(x, axis, k):
    n = lax.axis_size(axis)
    return lax.ppermute(x, axis, [(i, i ^ k) for i in range(n)])


def entering(sent, far, axis, early_bits):
    peers = lax.axis_size(axis)
    rows = far[0].shape[0]
    first, total = (sent[:rows], sent[rows : 2 * rows]), sent[2 * rows : 2 * rows + 1]
    entry = (jnp.zeros_like(first[0]), jnp.zeros_like(first[1]))
    gap = (jnp.ones_like(first[0]), jnp.zeros_like(first[0]))
    k = 1
    for early in early_bits:
        if k > 1:
            sent = jnp.concatenate([first[0], first[1], jnp.broadcast_to(total, (8, LANES))])
        got = swap(sent, axis, k)
        other = (got[:rows], got[rows : 2 * rows])
        other_total = got[2 * rows : 2 * rows + 1]
        reach = times(gap, other)
        entry = tuple(jnp.where(early, e + r, e) for e, r in zip(entry, reach))
        if 2 * k < peers:
            step = times(gap, far)
            gap = tuple(jnp.where(early, other_total * s, g) for s, g in zip(step, gap))
            near = tuple(jnp.where(early, a, b) for a, b in zip(first, other))
            late = tuple(jnp.where(early, b, a) for a, b in zip(first, other))
            moved = times(far, late)
            first = tuple(a + jnp.where(early, total, other_total) * b for a, b in zip(near, moved))
            total = total * other_total
            far = times(far, far)
        k *= 2
    return jnp.stack(entry)


def exchanges(axes):
    steps = []
    for axis in axes:
        k = 1
        while k < lax.axis_size(axis):
            steps.append((axis, k))
            k *= 2
    return steps


def bits(steps):
    return [(lax.axis_index(axis).astype(jnp.uint32) // jnp.uint32(k)) & jnp.uint32(1) for axis, k in steps]


def piece(x, start, size):
    return lax.dynamic_slice(x, (start, jnp.uint32(0)), (size, x.shape[1]))


def total_sum(own, away, steps, starts):
    x = own + swap(away, *steps[0])
    for (axis, k), (here, there, _) in zip(steps[1:-1], starts):
        m = x.shape[0] // 2
        x = piece(x, here, m) + swap(piece(x, there, m), axis, k)
    x = x + swap(x, *steps[-1])
    for (axis, k), (_, _, lower) in list(zip(steps[1:-1], starts))[::-1]:
        other = swap(x, axis, k)
        x = jnp.where(lower, jnp.concatenate([x, other]), jnp.concatenate([other, x]))
    return x, swap(x, *steps[0])


def inner(out_grad, prev_state, boundary, angle_code, radius_code, reflect):
    peers, place = lax.axis_size("tensor"), lax.axis_index("tensor")
    rows = out_grad[0]
    channels = prev_state.shape[2]
    tokens = prev_state.shape[1]
    groups = channels // GROUP
    half = groups // 2
    width = half * GROUP
    place = place.astype(jnp.uint32)

    def away(k, h):
        start = (place ^ jnp.uint32(k)) * jnp.uint32(channels) + jnp.uint32(h * width)
        return lax.dynamic_slice(rows, (jnp.uint32(0), start), (rows.shape[0], width))

    parts = [[swap(away(k, h), "tensor", k) for k in range(1, peers)] for h in range(2)]
    steps = exchanges(("dp", "ctx"))
    size = half * SIZE
    starts = []
    for bit in bits(steps)[1:-1]:
        size //= 2
        starts.append((bit * jnp.uint32(size), (jnp.uint32(1) - bit) * jnp.uint32(size), bit == 0))
    side = jnp.reshape(lax.axis_index("dp") & 1, (1,))
    place = jnp.reshape(place.astype(jnp.int32), (1,))
    early = [bit == 0 for bit in bits(exchanges(("ctx",)))]
    boundary, reflect, side, place, starts, early = lax.optimization_barrier((boundary, reflect, side, place, starts, early))
    keep = jnp.where(boundary[0] == 1, jnp.float32(0.6), jnp.float32(1.0))
    keep = jnp.broadcast_to(keep[:, None], (tokens, LANES))
    high, low, tab, ktab, far, turned, decay, weight = prepare(reflect, angle_code, radius_code, keep, prev_state[0])
    z_a, first_a, grad_a = scan_both(0, half, place, rows, parts[0], high, low, tab, ktab, keep, turned)
    spaced, head, sent = scan_first(half, half, place, rows, parts[1], high, low, tab, ktab, keep, first_a)
    entry = entering(sent, (far[0], far[1]), "ctx", early)
    z_b, grad_b = scan_second(half, half, spaced, head, tab, ktab, keep, turned)
    own, other = merge(side, grad_a, grad_b, weight, entry)
    grad_input = states(z_a, z_b, decay, entry, high, low)
    own, other = total_sum(own, other, steps, starts)
    return grad_input[None], final(side, own, other, high, low)


def solution(mesh):
    in_specs = (
        P("dp", ("ctx", "tensor"), None),
        P("dp", "ctx", "tensor"),
        P("dp", "ctx"),
        P("tensor", None),
        P("tensor", None),
        P("tensor", None, None),
    )
    out_specs = (P("dp", "ctx", "tensor"), P("tensor", None, None))
    return jax.shard_map(inner, mesh=mesh, in_specs=in_specs, out_specs=out_specs, check_vma=False)
```

time: 468 us -> 59.9 us (0.13); the launches traced: 459 us -> 59.6 us
  matrix products: 204 us -> 0 us
  local copies, waits for them, and re-layouts: 76.1 us -> 4.92 us
  waiting for transfers between devices: 89 us -> 18.5 us
  other arithmetic: 31.8 us -> 0.82 us
  loops' own time: 23.7 us -> 0 us
  Pallas kernels: 0 us -> 16.7 us
  between operations: 15.6 us -> 0.82 us
  blocking collectives: 14.7 us -> 0 us
  starting transfers between devices: 4.5 us -> 17.8 us
    dot_general x73 -> x0, matrix products: 204 us -> none  [the longest x52 106 us: apply_blocks(): jnp.einsum('bxy,...by->...bx', matrix, vectors, precision=lax.Precision.H...]
    psum x1 -> x0, waiting for transfers between devices: 88.9 us -> none  [body(): summed = lax.psum(partial_grad, ('dp', 'ctx'))]
    dynamic_slice x48 -> x3, local copies, waits for them, and re-layouts: 34.3 us -> 1.19 us  [the longest x1 1.15 us: away(): lax.dynamic_slice(rows, (jnp.uint32(0), start), (rows.shape[0], width))]
    another operation x4 -> x0, loops' own time: 23.7 us -> none  [the longest x1 11.5 us: body(): lax.scan(entry_step, zero_vector, (starts, sub_logs), reverse=True)]
    unnamed x4 -> x0, other arithmetic: 22.4 us -> none
    ppermute x0 -> x11, waiting for transfers between devices: none -> 18.5 us  [swap(): return lax.ppermute(x, axis, [(i, i ^ k) for i in range(n)])]
    ppermute x0 -> x11, starting transfers between devices: none -> 17.8 us  [swap(): return lax.ppermute(x, axis, [(i, i ^ k) for i in range(n)])]
    pallas_call x0 -> x7, Pallas kernels: none -> 16.7 us  [the longest x6 12.5 us: call(): pl.pallas_call(kernel, out_shape=shapes, in_specs=specs, out_specs=[VMEM]...]
  transfers between devices with their start and end apart: 3 -> 11, of which waited for: 1 -> 8; matrix products, arithmetic and copies ran while one was open for 46% -> 4% of each run, Pallas kernels for 0% -> 22%
where the time goes in v2:
time: 59.9 us; the launch traced here: 59.6 us
  waiting for transfers between devices  18.5 us (31%)
  starting transfers between devices  17.8 us (30%)
  Pallas kernels  16.7 us (28%)
  local copies, waits for them, and re-layouts  4.92 us (8%)
  other arithmetic  0.82 us (1%)
  between operations  0.82 us (1%)
    ppermute x11, waiting for transfers between devices, swap(): return lax.ppermute(x, axis, [(i, i ^ k) for i in range(n)])  18.5 us
    ppermute x11, starting transfers between devices, swap(): return lax.ppermute(x, axis, [(i, i ^ k) for i in range(n)])  17.8 us
    pallas_call x6, Pallas kernels, call(): pl.pallas_call(kernel, out_shape=shapes, in_specs=specs, out_specs=[VMEM]...  12.5 us
    pallas_call x1, Pallas kernels, states(): pl.pallas_call(functools.partial(state_kernel, half), grid=(groups,), in_...  4.22 us
    unnamed x6, local copies, waits for them, and re-layouts  2.07 us
  transfers between devices with their start and end apart: 11, of which 8 were waited for; matrix products, arithmetic and copies ran while one was open for 4% of the time, Pallas kernels for 22%

profile of v2, /device:TPU:0, one launch (start us, length us, event | category | flops | bytes accessed | tf_op | source)
XLA Modules:
  0.0 59.6 jit_solution(1138033233491909651)
XLA Ops:
  0.6 0.0 copy-start
  0.6 1.2 %dynamic-slice_bitcast_fusion = (bf16[128,1024]{1,0:T(8,128)(2,1)S(1)}, bf16[128,1024]{1,0:T(8,128)(2,1)S(1)}) fusion(bf16[1,128,4096]{2,1,0:T(8,128)(2,1)} %param.6, u32[]{:T(128)S(6)} %add.39, u32[]{:T(128)S(6)} %mul.79), kind=kLoop, calls=%fused_computation.1 | loop fusion | bytes 1048584 | tf_op jit(solution)/shard_map/dynamic_slice | solution.py:471
  1.8 3.1 %collective-permute-start = (bf16[128,1024]{1,0:T(8,128)(2,1)S(1)}, bf16[128,1024]{1,0:T(8,128)(2,1)S(1)}, u32[]{:S(2)}, u32[]{:S(2)}) collective-permute-start(bf16[128,1024]{1,0:T(8,128)(2,1)S(1)} %get-tuple-element.63), channel_id=1, source_target_pairs={{0,1},{1,0},{2,3},{3,2},{4,5},{5,4},{6,7},{7,6},{8,9},{9,8},{10,11... | collective-permute-start | bytes 786440 | tf_op jit(solution)/shard_map/ppermute | solution.py:398
  4.9 0.1 collective-permute-start.1
  4.9 0.8 %reshape.35.angle_ref = s32[8,128]{1,0:T(8,128)S(1)} reshape(s32[32,32]{1,0:T(8,128)} %param.9) | data formatting | bytes 8192 | tf_op jit(solution)/shard_map/reshape | solution.py:219
  5.7 0.8 %reshape.36.radius_ref = s32[8,128]{1,0:T(8,128)S(1)} reshape(s32[32,32]{1,0:T(8,128)} %param.10) | data formatting | bytes 8192 | tf_op jit(solution)/shard_map/reshape | solution.py:219
  6.5 0.7 %compare_select_fusion = f32[1,256]{1,0:T(1,128)S(1)} fusion(s32[1,256]{1,0:T(1,128)} %param.8), kind=kLoop, calls=%fused_computation.30 | loop fusion | flops 512 | bytes 2048 | tf_op jit(solution)/shard_map/jit(_where)/select_n | solution.py:484
  7.2 0.1 broadcast_in_dim.29.keep_ref.refs_2_
  7.3 0.0 copy-start.1
  7.3 1.2 %copy-done.1 = bf16[1,256,2048]{2,1,0:T(8,128)(2,1)S(1)} copy-done((bf16[1,256,2048]{2,1,0:T(8,128)(2,1)S(1)}, bf16[1,256,2048]{2,1,0:T(8,128)(2,1)}, u32[]{:S(2)}) %copy-start.1) | copy-done | bytes 1048600
  8.5 0.0 copy-start.2
  8.5 0.8 %copy-done.2 = f32[32,4,64]{2,1,0:T(4,128)S(1)} copy-done((f32[32,4,64]{2,1,0:T(4,128)S(1)}, f32[32,4,64]{2,1,0:T(4,128)}, u32[]{:S(2)}) %copy-start.2) | copy-done | bytes 32792
  9.4 4.3 %shard_map.77 = (bf16[8,256,256]{2,1,0:T(8,128)(2,1)S(1)}, bf16[8,256,256]{2,1,0:T(8,128)(2,1)S(1)}, f32[8,2,8,128]{3,2,1,0:T(8,128)S(1)}, f32[5,8,128]{2,1,0:T(...) custom-call(f32[128,64]{1,0:T(8,128)S(1)} %bitcast.78, ...), custom_call_target="tpu_custom_call" | custom-call | flops 536870912 | bytes 7081984 | tf_op jit(solution)/shard_map/pallas_call | solution.py:194
  13.7 0.0 collective-permute-done.refs_7_
  13.7 0.0 copy-done
  13.7 2.8 %shard_map.78 = (f32[4,2,256,128]{3,2,1,0:T(8,128)S(1)}, f32[2,4,128]{2,1,0:T(4,128)S(1)}, f32[4,64,256]{2,1,0:T(8,128)S(1)}) custom-call(f32[8,2,8,128]{3,2,1,0:T(8,128)S(1)} %get-tuple-element.34.refs_0_, f32[5,8,128]{2,1,0:T(8,128)S(1)} %get-tuple-element.35.refs_1_, f32[256,128]{1,0:T(8,128)S(1)} %broadcast_in_dim.29.keep_ref.refs_2_, s32[1]{0:T(128)} %bitcast.1.refs_3_, ...), custom_call_target="tpu_custom_call" | custom-call | flops 536870912 | bytes 5988356 | tf_op jit(solution)/shard_map/pallas_call | solution.py:194
  16.5 0.3 collective-permute-done.1.refs_7_
  16.8 1.6 %shard_map.79 = (f32[4,2,256,128]{3,2,1,0:T(8,128)S(1)}, f32[4,2,8,128]{3,2,1,0:T(8,128)S(1)}, f32[24,128]{1,0:T(8,128)S(1)}) custom-call(f32[8,2,8,128]{3,2,1,0:T(8,128)S(1)} %get-tuple-element.34.refs_0_, f32[5,8,128]{2,1,0:T(8,128)S(1)} %get-tuple-element.35.refs_1_, f32[256,128]{1,0:T(8,128)S(1)} %broadcast_in_dim.29.keep_ref.refs_2_, s32[1]{0:T(128)} %bitcast.1.refs_3_, ...), custom_call_target="tpu_custom_call" | custom-call | flops 268435456 | bytes 4722692 | tf_op jit(solution)/shard_map/pallas_call | solution.py:194
  18.4 1.9 %collective-permute-start.2 = (f32[24,128]{1,0:T(8,128)S(1)}, f32[24,128]{1,0:T(8,128)S(1)}, u32[]{:S(2)}, u32[]{:S(2)}) collective-permute-start(f32[24,128]{1,0:T(8,128)S(1)} %get-tuple-element.48), channel_id=1, source_target_pairs={{0,2},{2,0},{4,6},{6,4},{1,3},{3,1},{5,7},{7,5},{8,10},{10,8},{12,... | collective-permute-start | bytes 36872 | tf_op jit(solution)/shard_map/ppermute | solution.py:398
  20.2 1.9 %collective-permute-done.2 = f32[24,128]{1,0:T(8,128)S(1)} collective-permute-done((f32[24,128]{1,0:T(8,128)S(1)}, f32[24,128]{1,0:T(8,128)S(1)}, u32[]{:S(2)}, u32[]{:S(2)}) %collective-permute-start.2) | collective-permute-done | bytes 12320 | tf_op jit(solution)/shard_map/ppermute | solution.py:398
  22.1 2.9 %collective-permute-start.3 = (f32[24,128]{1,0:T(8,128)S(1)}, f32[24,128]{1,0:T(8,128)S(1)}, u32[]{:S(2)}, u32[]{:S(2)}) collective-permute-start(f32[24,128]{1,0:T(8,128)S(1)} %pad_maximum_fusion), channel_id=1, source_target_pairs={{0,4},{2,6},{4,0},{6,2},{1,5},{3,7},{5,1},{7,3},{8,12},{10,14},{12... | collective-permute-start | bytes 36872 | tf_op jit(solution)/shard_map/ppermute | solution.py:398
  25.0 1.8 %shard_map.80 = (f32[4,2,256,128]{3,2,1,0:T(8,128)S(1)}, f32[4,64,256]{2,1,0:T(8,128)S(1)}) custom-call(f32[8,2,8,128]{3,2,1,0:T(8,128)S(1)} %get-tuple-element.34.refs_0_, f32[5,8,128]{2,1,0:T(8,128)S(1)} %get-tuple-element.35.refs_1_, f32[256,128]{1,0:T(8,128)S(1)} %broadcast_in_dim.29.keep_ref.refs_2_, ...), custom_call_target="tpu_custom_call" | custom-call | flops 268435456 | bytes 3657728 | tf_op jit(solution)/shard_map/pallas_call | solution.py:194
  26.9 0.0 collective-permute-done.3
  26.9 0.1 shard_map.81
  27.0 0.1 collective-permute-start.4
  27.1 1.5 %collective-permute-done.4 = f32[256,256]{1,0:T(8,128)S(1)} collective-permute-done((f32[256,256]{1,0:T(8,128)S(1)}, f32[256,256]{1,0:T(8,128)S(1)}, u32[]{:S(2)}, u32[]{:S(2)}) %collective-permute-start.4) | collective-permute-done | bytes 262176 | tf_op jit(solution)/shard_map/ppermute | solution.py:398
  28.7 1.7 %collective-permute-start.5 = (f32[128,256]{1,0:T(8,128)S(1)}, f32[128,256]{1,0:T(8,128)S(1)}, u32[]{:S(2)}, u32[]{:S(2)}) collective-permute-start(f32[128,256]{1,0:T(8,128)S(1)} %constant_dynamic-slice_fusion.1), channel_id=1, source_target_pairs={{0,16},{8,24},{16,0},{24,8},{1,17},{9,25},{17,1},{25,9},{2,18},{10... | collective-permute-start | bytes 393224 | tf_op jit(solution)/shard_map/ppermute | solution.py:398
  30.4 3.9 %collective-permute-done.5 = f32[128,256]{1,0:T(8,128)S(1)} collective-permute-done((f32[128,256]{1,0:T(8,128)S(1)}, f32[128,256]{1,0:T(8,128)S(1)}, u32[]{:S(2)}, u32[]{:S(2)}) %collective-permute-start.5) | collective-permute-done | bytes 131104 | tf_op jit(solution)/shard_map/ppermute | solution.py:398
  34.3 1.8 %collective-permute-start.6 = (f32[64,256]{1,0:T(8,128)S(1)}, f32[64,256]{1,0:T(8,128)S(1)}, u32[]{:S(2)}, u32[]{:S(2)}) collective-permute-start(f32[64,256]{1,0:T(8,128)S(1)} %constant_dynamic-slice_fusion), channel_id=1, source_target_pairs={{0,2},{2,0},{4,6},{6,4},{1,3},{3,1},{5,7},{7,5},{8,10},{10,8},{12,... | collective-permute-start | bytes 196616 | tf_op jit(solution)/shard_map/ppermute | solution.py:398
  36.1 2.5 %collective-permute-done.6 = f32[64,256]{1,0:T(8,128)S(1)} collective-permute-done((f32[64,256]{1,0:T(8,128)S(1)}, f32[64,256]{1,0:T(8,128)S(1)}, u32[]{:S(2)}, u32[]{:S(2)}) %collective-permute-start.6) | collective-permute-done | bytes 65568 | tf_op jit(solution)/shard_map/ppermute | solution.py:398
  38.7 2.8 %collective-permute-start.7 = (f32[64,256]{1,0:T(8,128)S(1)}, f32[64,256]{1,0:T(8,128)S(1)}, u32[]{:S(2)}, u32[]{:S(2)}) collective-permute-start(f32[64,256]{1,0:T(8,128)S(1)} %dynamic-slice_add_fusion.1), channel_id=1, source_target_pairs={{0,4},{2,6},{4,0},{6,2},{1,5},{3,7},{5,1},{7,3},{8,12},{10,14},{12... | collective-permute-start | bytes 196616 | tf_op jit(solution)/shard_map/ppermute | solution.py:398
  41.5 2.4 %collective-permute-done.7 = f32[64,256]{1,0:T(8,128)S(1)} collective-permute-done((f32[64,256]{1,0:T(8,128)S(1)}, f32[64,256]{1,0:T(8,128)S(1)}, u32[]{:S(2)}, u32[]{:S(2)}) %collective-permute-start.7) | collective-permute-done | bytes 65568 | tf_op jit(solution)/shard_map/ppermute | solution.py:398
  43.9 1.8 %collective-permute-start.8 = (f32[64,256]{1,0:T(8,128)S(1)}, f32[64,256]{1,0:T(8,128)S(1)}, u32[]{:S(2)}, u32[]{:S(2)}) collective-permute-start(f32[64,256]{1,0:T(8,128)S(1)} %add.51), channel_id=1, source_target_pairs={{0,2},{2,0},{4,6},{6,4},{1,3},{3,1},{5,7},{7,5},{8,10},{10,8},{12,... | collective-permute-start | bytes 196616 | tf_op jit(solution)/shard_map/ppermute | solution.py:398
  45.7 2.6 %collective-permute-done.8 = f32[64,256]{1,0:T(8,128)S(1)} collective-permute-done((f32[64,256]{1,0:T(8,128)S(1)}, f32[64,256]{1,0:T(8,128)S(1)}, u32[]{:S(2)}, u32[]{:S(2)}) %collective-permute-start.8) | collective-permute-done | bytes 65568 | tf_op jit(solution)/shard_map/ppermute | solution.py:398
  48.3 1.7 %collective-permute-start.9 = (f32[128,256]{1,0:T(8,128)S(1)}, f32[128,256]{1,0:T(8,128)S(1)}, u32[]{:S(2)}, u32[]{:S(2)}) collective-permute-start(f32[128,256]{1,0:T(8,128)S(1)} %maximum_select_fusion.1), channel_id=1, source_target_pairs={{0,16},{8,24},{16,0},{24,8},{1,17},{9,25},{17,1},{25,9},{2,18},{10... | collective-permute-start | bytes 393224 | tf_op jit(solution)/shard_map/ppermute | solution.py:398
  50.0 3.3 %collective-permute-done.9 = f32[128,256]{1,0:T(8,128)S(1)} collective-permute-done((f32[128,256]{1,0:T(8,128)S(1)}, f32[128,256]{1,0:T(8,128)S(1)}, u32[]{:S(2)}, u32[]{:S(2)}) %collective-permute-start.9) | collective-permute-done | bytes 131104 | tf_op jit(solution)/shard_map/ppermute | solution.py:398
  53.3 0.1 collective-permute-start.10
  53.4 4.2 %states.1 = bf16[256,2048]{1,0:T(8,128)(2,1)} custom-call(f32[4,2,256,128]{3,2,1,0:T(8,128)S(1)} %get-tuple-element.40.a_ref, f32[4,2,256,128]{3,2,1,0:T(8,128)S(1)} %get-tuple-element.44.b_ref, f32[8,2,256,128]{3,2,1,0:T(8,128)S(1)} %get-tuple-element.45.decay_ref, f32[2,8,128]{2,1,0:T(8,128)S(1)} %pad_maximum_fusion.1.entry_ref, ...), custom_call_target="tpu_custom_call" | custom-call | flops 805306368 | bytes 7200000 | tf_op jit(solution)/shard_map/states/pallas_call | solution.py:359
  57.6 0.0 collective-permute-done.10.other_ref
  57.6 1.9 %shard_map.82 = f32[32,64,64]{2,1,0:T(8,128)} custom-call(s32[1]{0:T(128)} %bitcast.side_ref, f32[256,256]{1,0:T(8,128)S(1)} %maximum_select_fusion.own_ref, f32[256,256]{1,0:T(8,128)S(1)} %collective-permute-done.10.other_ref, bf16[8,256,256]{2,1,0:T(8,128)(2,1)S(1)} %get-tuple-element.37.refs_5_.high_ref, ...), custom_call_target="tpu_custom_call" | custom-call | bytes 3145732 | tf_op jit(solution)/shard_map/pallas_call | solution.py:194
  (14 shorter events, 0.2 us)
Async XLA Ops:
  0.6 13.1 %copy-start = (bf16[1,128,4096]{2,1,0:T(8,128)(2,1)S(1)}, bf16[1,128,4096]{2,1,0:T(8,128)(2,1)}, u32[]{:S(2)}) copy-start(bf16[1,128,4096]{2,1,0:T(8,128)(2,1)} %param.6) | copy-start | bytes 3145732
  1.8 11.9 %collective-permute-start = (bf16[128,1024]{1,0:T(8,128)(2,1)S(1)}, bf16[128,1024]{1,0:T(8,128)(2,1)S(1)}, u32[]{:S(2)}, u32[]{:S(2)}) collective-permute-start(bf16[128,1024]{1,0:T(8,128)(2,1)S(1)} %get-tuple-element.63), channel_id=1, source_target_pairs={{0,1},{1,0},{2,3},{3,2},{4,5},{5,4},{6,7},{7,6},{8,9},{9,8},{10,11... | collective-permute-start | bytes 786440 | tf_op jit(solution)/shard_map/ppermute | solution.py:398
  4.9 11.9 %collective-permute-start.1 = (bf16[128,1024]{1,0:T(8,128)(2,1)S(1)}, bf16[128,1024]{1,0:T(8,128)(2,1)S(1)}, u32[]{:S(2)}, u32[]{:S(2)}) collective-permute-start(bf16[128,1024]{1,0:T(8,128)(2,1)S(1)} %get-tuple-element.62), channel_id=1, source_target_pairs={{0,1},{1,0},{2,3},{3,2},{4,5},{5,4},{6,7},{7,6},{8,9},{9,8},{10,11... | collective-permute-start | bytes 786440 | tf_op jit(solution)/shard_map/ppermute | solution.py:398
  7.3 1.2 %copy-start.1 = (bf16[1,256,2048]{2,1,0:T(8,128)(2,1)S(1)}, bf16[1,256,2048]{2,1,0:T(8,128)(2,1)}, u32[]{:S(2)}) copy-start(bf16[1,256,2048]{2,1,0:T(8,128)(2,1)} %param.7) | copy-start | bytes 3145732
  8.5 0.8 %copy-start.2 = (f32[32,4,64]{2,1,0:T(4,128)S(1)}, f32[32,4,64]{2,1,0:T(4,128)}, u32[]{:S(2)}) copy-start(f32[32,4,64]{2,1,0:T(4,128)} %param.11) | copy-start | bytes 98308
  18.4 3.8 %collective-permute-start.2 = (f32[24,128]{1,0:T(8,128)S(1)}, f32[24,128]{1,0:T(8,128)S(1)}, u32[]{:S(2)}, u32[]{:S(2)}) collective-permute-start(f32[24,128]{1,0:T(8,128)S(1)} %get-tuple-element.48), channel_id=1, source_target_pairs={{0,2},{2,0},{4,6},{6,4},{1,3},{3,1},{5,7},{7,5},{8,10},{10,8},{12,... | collective-permute-start | bytes 36872 | tf_op jit(solution)/shard_map/ppermute | solution.py:398
  22.1 4.7 %collective-permute-start.3 = (f32[24,128]{1,0:T(8,128)S(1)}, f32[24,128]{1,0:T(8,128)S(1)}, u32[]{:S(2)}, u32[]{:S(2)}) collective-permute-start(f32[24,128]{1,0:T(8,128)S(1)} %pad_maximum_fusion), channel_id=1, source_target_pairs={{0,4},{2,6},{4,0},{6,2},{1,5},{3,7},{5,1},{7,3},{8,12},{10,14},{12... | collective-permute-start | bytes 36872 | tf_op jit(solution)/shard_map/ppermute | solution.py:398
  27.0 1.6 %collective-permute-start.4 = (f32[256,256]{1,0:T(8,128)S(1)}, f32[256,256]{1,0:T(8,128)S(1)}, u32[]{:S(2)}, u32[]{:S(2)}) collective-permute-start(f32[256,256]{1,0:T(8,128)S(1)} %get-tuple-element.57), channel_id=1, source_target_pairs={{0,8},{8,0},{16,24},{24,16},{1,9},{9,1},{17,25},{25,17},{2,10},{10... | collective-permute-start | bytes 786440 | tf_op jit(solution)/shard_map/ppermute | solution.py:398
  28.7 5.6 %collective-permute-start.5 = (f32[128,256]{1,0:T(8,128)S(1)}, f32[128,256]{1,0:T(8,128)S(1)}, u32[]{:S(2)}, u32[]{:S(2)}) collective-permute-start(f32[128,256]{1,0:T(8,128)S(1)} %constant_dynamic-slice_fusion.1), channel_id=1, source_target_pairs={{0,16},{8,24},{16,0},{24,8},{1,17},{9,25},{17,1},{25,9},{2,18},{10... | collective-permute-start | bytes 393224 | tf_op jit(solution)/shard_map/ppermute | solution.py:398
  34.3 4.3 %collective-permute-start.6 = (f32[64,256]{1,0:T(8,128)S(1)}, f32[64,256]{1,0:T(8,128)S(1)}, u32[]{:S(2)}, u32[]{:S(2)}) collective-permute-start(f32[64,256]{1,0:T(8,128)S(1)} %constant_dynamic-slice_fusion), channel_id=1, source_target_pairs={{0,2},{2,0},{4,6},{6,4},{1,3},{3,1},{5,7},{7,5},{8,10},{10,8},{12,... | collective-permute-start | bytes 196616 | tf_op jit(solution)/shard_map/ppermute | solution.py:398
  38.7 5.3 %collective-permute-start.7 = (f32[64,256]{1,0:T(8,128)S(1)}, f32[64,256]{1,0:T(8,128)S(1)}, u32[]{:S(2)}, u32[]{:S(2)}) collective-permute-start(f32[64,256]{1,0:T(8,128)S(1)} %dynamic-slice_add_fusion.1), channel_id=1, source_target_pairs={{0,4},{2,6},{4,0},{6,2},{1,5},{3,7},{5,1},{7,3},{8,12},{10,14},{12... | collective-permute-start | bytes 196616 | tf_op jit(solution)/shard_map/ppermute | solution.py:398
  43.9 4.3 %collective-permute-start.8 = (f32[64,256]{1,0:T(8,128)S(1)}, f32[64,256]{1,0:T(8,128)S(1)}, u32[]{:S(2)}, u32[]{:S(2)}) collective-permute-start(f32[64,256]{1,0:T(8,128)S(1)} %add.51), channel_id=1, source_target_pairs={{0,2},{2,0},{4,6},{6,4},{1,3},{3,1},{5,7},{7,5},{8,10},{10,8},{12,... | collective-permute-start | bytes 196616 | tf_op jit(solution)/shard_map/ppermute | solution.py:398
  48.3 5.0 %collective-permute-start.9 = (f32[128,256]{1,0:T(8,128)S(1)}, f32[128,256]{1,0:T(8,128)S(1)}, u32[]{:S(2)}, u32[]{:S(2)}) collective-permute-start(f32[128,256]{1,0:T(8,128)S(1)} %maximum_select_fusion.1), channel_id=1, source_target_pairs={{0,16},{8,24},{16,0},{24,8},{1,17},{9,25},{17,1},{25,9},{2,18},{10... | collective-permute-start | bytes 393224 | tf_op jit(solution)/shard_map/ppermute | solution.py:398
  53.3 4.3 %collective-permute-start.10 = (f32[256,256]{1,0:T(8,128)S(1)}, f32[256,256]{1,0:T(8,128)S(1)}, u32[]{:S(2)}, u32[]{:S(2)}) collective-permute-start(f32[256,256]{1,0:T(8,128)S(1)} %maximum_select_fusion.own_ref), channel_id=1, source_target_pairs={{0,8},{8,0},{16,24},{24,16},{1,9},{9,1},{17,25},{25,17},{2,10},{10... | collective-permute-start | bytes 786440 | tf_op jit(solution)/shard_map/ppermute | solution.py:398

commit v3 on v2

--- a/solution.py
+++ b/solution.py
@@ -96,40 +96,28 @@
     return states
 
 
-def prepare_kernel(length, reflect_ref, angle_ref, radius_ref, keep_ref, prev_hbm,
-                   high_ref, low_ref, tab_ref, ktab_ref, far_ref, turned_ref, decay_ref, weight_ref, u_ref, prev_ref, prev_sem):
-    fetch = pltpu.make_async_copy(prev_hbm, prev_ref, prev_sem)
-    fetch.start()
+def basis_kernel(length, code_ref, reflect_ref, high_ref, low_ref, tab_ref, far_ref, u_ref, wide_ref):
     rows = reflect_ref.shape[0]
     blocks = rows // 4
     groups = blocks // 4
 
-    chunk = keep_ref[pl.ds(0, CHUNKS, stride=length), :]
-    for i in range(1, length):
-        chunk = chunk * keep_ref[pl.ds(i, CHUNKS, stride=length), :]
-    two = chunk * later(chunk, 1, 1.0)
-    four = two * later(two, 2, 1.0)
-    before = earlier(chunk, 1, 1.0)
-    before = before * earlier(before, 1, 1.0)
-    before = before * earlier(before, 2, 1.0)
-    before = before * earlier(before, 4, 1.0)
-    eight = four * later(four, 4, 1.0)
-    ktab_ref[0] = chunk
-    ktab_ref[1] = two
-    ktab_ref[2] = four
-    ktab_ref[3] = before
-    ktab_ref[4] = jnp.broadcast_to(eight[0:1], TILE)
-
+    wide_ref[...] = jnp.concatenate([code_ref[...]] * 4, axis=1)
+    codes = wide_ref[pl.ds(0, groups, stride=4), :]
+    block = iota(codes.shape, 1) // 32
+    for j in range(1, 4):
+        codes = jnp.where(block == j, wide_ref[pl.ds(j, groups, stride=4), :], codes)
+
+    rates = jnp.exp(-math.log(2.0) * (4.0 + (codes & 1023).astype(F32) * (10.0 / 1024.0)))
+    series = jnp.full_like(rates, 1.0 / 8.0)
+    for k in range(7, 0, -1):
+        series = series * rates + 1.0 / k
+    logs = -rates * series
+    angles = codes >> 10
     row = iota(TILE, 0)
     n = jnp.where(row == 0, 1, row * length)
     for g in range(groups):
-        code = angle_ref[g : g + 1, :]
-        rate = jnp.exp(-math.log(2.0) * (4.0 + radius_ref[g : g + 1, :].astype(F32) * (10.0 / 1024.0)))
-        series = jnp.full_like(rate, 1.0 / 8.0)
-        for k in range(7, 0, -1):
-            series = series * rate + 1.0 / k
-        turn = ((n * code) & 8191).astype(F32) * (math.pi / 4096.0)
-        size = jnp.exp(n.astype(F32) * (-rate * series))
+        turn = ((n * angles[g : g + 1, :]) & 8191).astype(F32) * (math.pi / 4096.0)
+        size = jnp.exp(n.astype(F32) * logs[g : g + 1, :])
         re, im = size * jnp.cos(turn), -size * jnp.sin(turn)
         tab_ref[g, 0] = re
         tab_ref[g, 1] = im
@@ -164,6 +152,28 @@
         high_ref[g] = high
         low_ref[g] = low
 
+
+def weight_kernel(length, boundary_ref, tab_ref, prev_ref, keep_ref, ktab_ref, turned_ref, decay_ref, weight_ref):
+    groups = tab_ref.shape[0]
+    keep = jnp.where(boundary_ref[...] == 1, 0.6, 1.0).astype(F32)
+    keep_ref[...] = jnp.broadcast_to(keep, (LANES, keep.shape[1])).T
+
+    chunk = keep_ref[pl.ds(0, CHUNKS, stride=length), :]
+    for i in range(1, length):
+        chunk = chunk * keep_ref[pl.ds(i, CHUNKS, stride=length), :]
+    two = chunk * later(chunk, 1, 1.0)
+    four = two * later(two, 2, 1.0)
+    before = earlier(chunk, 1, 1.0)
+    before = before * earlier(before, 1, 1.0)
+    before = before * earlier(before, 2, 1.0)
+    before = before * earlier(before, 4, 1.0)
+    eight = four * later(four, 4, 1.0)
+    ktab_ref[0] = chunk
+    ktab_ref[1] = two
+    ktab_ref[2] = four
+    ktab_ref[3] = before
+    ktab_ref[4] = jnp.broadcast_to(eight[0:1], TILE)
+
     one, zero = jnp.ones(TILE, F32), jnp.zeros(TILE, F32)
     for first in range(0, groups, 4):
         some = range(first, min(first + 4, groups))
@@ -175,7 +185,6 @@
             decay_ref[first + k, 1, at, :] = state[1]
 
         walk(length, len(some), units, states, keep_ref, None, store)
-    fetch.wait()
     for g in range(groups):
         columns = slice(g * GROUP, (g + 1) * GROUP)
         turned = prev_ref[:, columns].T
@@ -186,6 +195,7 @@
 
 VMEM = pl.BlockSpec(memory_space=pltpu.VMEM)
 SMEM = pl.BlockSpec(memory_space=pltpu.SMEM)
+HBM = pl.BlockSpec(memory_space=pltpu.HBM)
 
 
 def call(kernel, out_shape, args, specs, scratch=(), flops=0):
@@ -202,26 +212,34 @@
     )(*args)
 
 
-def prepare(reflect, angle, radius, keep, prev):
+def basis(code, reflect, length):
     blocks = reflect.shape[0]
     groups = blocks // 4
-    tokens, channels = prev.shape
     out = [
         ((groups, GROUP, GROUP), BF16),
         ((groups, GROUP, GROUP), BF16),
         ((groups, 2) + TILE, F32),
+        ((2, groups, LANES), F32),
+    ]
+    args = (code, reflect.reshape(blocks * 4, SIZE))
+    scratch = [pltpu.VMEM((blocks * 4, SIZE), F32), pltpu.VMEM((blocks, LANES), jnp.int32)]
+    return call(functools.partial(basis_kernel, length), out, args, [VMEM] * 2, scratch, groups * 2 * 2 * 256**3)
+
+
+def weights(boundary, tab, prev):
+    groups = tab.shape[0]
+    tokens, channels = prev.shape
+    out = [
+        ((tokens, LANES), F32),
         ((5,) + TILE, F32),
-        ((2, groups, LANES), F32),
         ((channels, tokens), BF16),
         ((groups, 2, tokens, LANES), F32),
         ((groups, SIZE, GROUP), F32),
     ]
-    args = (reflect.reshape(blocks * 4, SIZE), angle.reshape(groups, LANES), radius.reshape(groups, LANES), keep, prev)
-    return call(functools.partial(prepare_kernel, tokens // CHUNKS), out, args, [VMEM] * 4 + [pl.BlockSpec(memory_space=pl.ANY)],
-                [pltpu.VMEM((blocks * 4, SIZE), F32), pltpu.VMEM((tokens, channels), BF16), pltpu.SemaphoreType.DMA], groups * 2 * 2 * 256**3)
-
-
-def scan_kernel(length, base, count, peers, begin, finish, *refs):
+    return call(functools.partial(weight_kernel, tokens // CHUNKS), out, (boundary, tab, prev), [VMEM] * 3, (), groups * 2 * 2 * 256**3)
+
+
+def scan_kernel(length, base, count, peers, begin, finish, aheads, *refs):
     refs = list(refs)
     take = lambda n: [refs.pop(0) for _ in range(n)]
     tab_ref, ktab_ref, keep_ref = take(3)
@@ -229,7 +247,7 @@
         place_ref, own_ref, high_ref, low_ref = take(4)
         others = take(peers - 1)
     if begin and not finish:
-        (ahead_ref,) = take(1)
+        ahead = take(aheads)
     if finish:
         (turned_ref,) = take(1)
     if begin:
@@ -262,8 +280,12 @@
     zero = jnp.zeros(TILE, F32)
     if begin and not finish:
         groups = base + count
-        for c in range(2):
-            first_ref[c * groups : c * groups + base, :] = ahead_ref[c]
+        at = 0
+        for ref in ahead:
+            size = ref.shape[1]
+            for c in range(2):
+                first_ref[c * groups + at : c * groups + at + size, :] = ref[c]
+            at += size
         first_ref[2 * groups :, :] = ktab_ref[4]
     if begin:
         heads = walk(length, count, units, [(zero, zero)] * count, keep_ref, load, None)
@@ -300,7 +322,7 @@
     tokens = keep.shape[0]
     peers = len(parts) + 1
     out = [((count, 2, tokens, LANES), F32), ((2, count, LANES), F32), ((count, SIZE, GROUP), F32)]
-    return call(functools.partial(scan_kernel, tokens // CHUNKS, base, count, peers, True, True), out,
+    return call(functools.partial(scan_kernel, tokens // CHUNKS, base, count, peers, True, True, 0), out,
                 (tab, ktab, keep, place, rows, high, low, *parts, turned), [VMEM] * 3 + [SMEM] + [VMEM] * (peers + 3),
                 [pltpu.VMEM((tokens, count * GROUP), BF16), pltpu.VMEM((count, 2, tokens, LANES), F32)], count * 4 * 2 * 256**3)
 
@@ -309,24 +331,25 @@
     tokens = keep.shape[0]
     peers = len(parts) + 1
     out = [((count, 2, tokens, LANES), F32), ((count, 2) + TILE, F32), ((2 * (base + count) + CHUNKS, LANES), F32)]
-    return call(functools.partial(scan_kernel, tokens // CHUNKS, base, count, peers, True, False), out,
-                (tab, ktab, keep, place, rows, high, low, *parts, ahead), [VMEM] * 3 + [SMEM] + [VMEM] * (peers + 3),
+    return call(functools.partial(scan_kernel, tokens // CHUNKS, base, count, peers, True, False, len(ahead)), out,
+                (tab, ktab, keep, place, rows, high, low, *parts, *ahead), [VMEM] * 3 + [SMEM] + [VMEM] * (peers + 2 + len(ahead)),
                 [pltpu.VMEM((tokens, count * GROUP), BF16)], count * 2 * 2 * 256**3)
 
 
 def scan_second(base, count, spaced, head, tab, ktab, keep, turned):
     tokens = keep.shape[0]
     out = [((count, 2, tokens, LANES), F32), ((count, SIZE, GROUP), F32)]
-    return call(functools.partial(scan_kernel, tokens // CHUNKS, base, count, 0, False, True), out,
+    return call(functools.partial(scan_kernel, tokens // CHUNKS, base, count, 0, False, True, 0), out,
                 (tab, ktab, keep, turned, spaced, head), [VMEM] * 6, (), count * 2 * 2 * 256**3)
 
 
-def merge_kernel(side_ref, a_ref, b_ref, weight_ref, entry_ref, own_ref, away_ref):
-    half = a_ref.shape[0]
+def merge_kernel(half, side_ref, entry_ref, weight_ref, *refs):
+    parts, (own_ref, away_ref) = refs[:-2], refs[-2:]
+    blocks = [part.at[n] for part in parts for n in range(part.shape[0])]
     side = side_ref[0]
     for n in range(half):
         for out_ref, which in ((own_ref, side), (away_ref, 1 - side)):
-            here = jnp.where(which == 0, a_ref[n], b_ref[n])
+            here = jnp.where(which == 0, blocks[n][...], blocks[half + n][...])
             at = which * half + n
             re, im = entry_ref[0, pl.ds(at, 1), :], entry_ref[1, pl.ds(at, 1), :]
             weight = weight_ref[at]
@@ -335,62 +358,93 @@
             out_ref[n * SIZE : (n + 1) * SIZE, LANES:] = here[:, LANES:] + (re * w_im + im * w_re)
 
 
-def merge(side, a, b, weight, entry):
-    rows = a.shape[0] * SIZE
-    return call(merge_kernel, [((rows, GROUP), F32)] * 2, (side, a, b, weight, entry), [SMEM] + [VMEM] * 4)
-
-
-def state_kernel(half, a_ref, b_ref, decay_ref, entry_ref, high_ref, low_ref, out_ref):
+def merge(half, side, entry, weight, parts):
+    return call(functools.partial(merge_kernel, half), [((half * SIZE, GROUP), F32)] * 2,
+                (side, entry, weight, *parts), [SMEM] + [VMEM] * (2 + len(parts)))
+
+
+def state_kernel(base, sizes, entry_ref, decay_ref, high_ref, low_ref, *refs):
+    parts, out_ref = refs[: len(sizes)], refs[-1]
     g = pl.program_id(0)
-    re, im = entry_ref[0, pl.ds(g, 1), :], entry_ref[1, pl.ds(g, 1), :]
+    re, im = entry_ref[0, pl.ds(base + g, 1), :], entry_ref[1, pl.ds(base + g, 1), :]
     d_re, d_im = decay_ref[0, 0], decay_ref[0, 1]
-    first = g < half
-    z_re = jnp.where(first, a_ref[0, 0], b_ref[0, 0]) + (re * d_re - im * d_im)
-    z_im = jnp.where(first, a_ref[0, 1], b_ref[0, 1]) + (re * d_im + im * d_re)
+    z_re, z_im = parts[0][0, 0], parts[0][0, 1]
+    if len(parts) > 1:
+        first = g < sizes[0]
+        z_re, z_im = jnp.where(first, z_re, parts[1][0, 0]), jnp.where(first, z_im, parts[1][0, 1])
+    z_re = z_re + (re * d_re - im * d_im)
+    z_im = z_im + (re * d_im + im * d_re)
     z_high, z_low = split(jnp.concatenate([z_re, z_im], axis=1))
     out = matmul(z_high, high_ref[0], NT) + matmul(z_high, low_ref[0], NT) + matmul(z_low, high_ref[0], NT)
     out_ref[...] = out.astype(BF16)
 
 
-def states(a, b, decay, entry, high, low):
-    half, _, tokens, _ = a.shape
-    groups = 2 * half
-    each = lambda shape: pl.BlockSpec((1,) + shape, lambda g: (g, 0, 0, 0)[: len(shape) + 1])
+def states(base, parts, decay, entry, high, low, filled=None):
+    groups = high.shape[0]
+    tokens = parts[0].shape[2]
+    sizes = [part.shape[0] for part in parts]
+    each = lambda shape: pl.BlockSpec((1,) + shape, lambda g: (g + base, 0, 0, 0)[: len(shape) + 1])
+    shape = (1, 2, tokens, LANES)
+    picks = [pl.BlockSpec(shape, lambda g: (jnp.minimum(g, sizes[0] - 1), 0, 0, 0))]
+    picks += [pl.BlockSpec(shape, lambda g: (jnp.maximum(g - sizes[0], 0), 0, 0, 0)) for _ in parts[1:]]
+    args = [entry, decay, high, low, *parts]
+    specs = [pl.BlockSpec(entry.shape, lambda g: (0, 0, 0)), each((2, tokens, LANES)), each((GROUP, GROUP)), each((GROUP, GROUP)), *picks]
+    alias = {}
+    if filled is not None:
+        alias = {len(args): 0}
+        args.append(filled)
+        specs.append(pl.BlockSpec(memory_space=pl.ANY))
     return pl.pallas_call(
-        functools.partial(state_kernel, half),
-        grid=(groups,),
-        in_specs=[
-            pl.BlockSpec((1, 2, tokens, LANES), lambda g: (jnp.minimum(g, half - 1), 0, 0, 0)),
-            pl.BlockSpec((1, 2, tokens, LANES), lambda g: (jnp.maximum(g - half, 0), 0, 0, 0)),
-            each((2, tokens, LANES)),
-            pl.BlockSpec(entry.shape, lambda g: (0, 0, 0)),
-            each((GROUP, GROUP)),
-            each((GROUP, GROUP)),
-        ],
-        out_specs=pl.BlockSpec((tokens, GROUP), lambda g: (0, g)),
+        functools.partial(state_kernel, base, sizes),
+        grid=(sum(sizes),),
+        in_specs=specs,
+        out_specs=pl.BlockSpec((tokens, GROUP), lambda g: (0, g + base)),
         out_shape=jax.ShapeDtypeStruct((tokens, groups * GROUP), BF16),
+        input_output_aliases=alias,
         name="states",
         compiler_params=pltpu.CompilerParams(vmem_limit_bytes=LIMIT),
-        cost_estimate=pl.CostEstimate(flops=groups * 3 * 2 * 256**3, bytes_accessed=groups * 900_000, transcendentals=0),
-    )(a, b, decay, entry, high, low)
-
-
-def final_kernel(side_ref, own_ref, other_ref, high_ref, low_ref, out_ref):
+        cost_estimate=pl.CostEstimate(flops=sum(sizes) * 3 * 2 * 256**3, bytes_accessed=sum(sizes) * 900_000, transcendentals=0),
+    )(*args)
+
+
+def final_kernel(flip, side_ref, x_ref, high_ref, low_ref, *refs):
+    out_hbm, out_ref, sems = refs[-3:]
     half = high_ref.shape[0] // 2
-    side = side_ref[0]
-    for x_ref, which in ((own_ref, side), (other_ref, 1 - side)):
-        for n in range(half):
-            at = which * half + n
-            x_high, x_low = split(x_ref[n * SIZE : (n + 1) * SIZE, :])
-            high = high_ref[at]
-            out = matmul(high, x_high, NT) + matmul(high, x_low, NT) + matmul(low_ref[at], x_high, NT)
-            for j in range(4):
-                out_ref[at * 4 + j] = out[j * SIZE : (j + 1) * SIZE]
-
-
-def final(side, own, other, high, low):
+    which = 1 - side_ref[0] if flip else side_ref[0]
+    copies = []
+    for n in range(half):
+        at = which * half + n
+        x = x_ref[n * SIZE : (n + 1) * SIZE, :]
+        out = matmul(high_ref[at], x, NT) + matmul(low_ref[at], x, NT)
+        for j in range(4):
+            out_ref[4 * n + j] = out[j * SIZE : (j + 1) * SIZE]
+        copies.append(pltpu.make_async_copy(out_ref.at[pl.ds(4 * n, 4)], out_hbm.at[pl.ds(at * 4, 4)], sems.at[n]))
+        copies[-1].start()
+    for copy in copies:
+        copy.wait()
+
+
+def final(flip, side, x, high, low, filled=None):
+    half = high.shape[0] // 2
     blocks = high.shape[0] * 4
-    return call(final_kernel, [((blocks, SIZE, SIZE), F32)], (side, own, other, high, low), [SMEM] + [VMEM] * 4)[0]
+    args = [side, x, high, low]
+    specs = [SMEM] + [VMEM] * 3
+    alias = {}
+    if filled is not None:
+        alias = {len(args): 0}
+        args.append(filled)
+        specs.append(HBM)
+    return pl.pallas_call(
+        functools.partial(final_kernel, flip),
+        out_shape=jax.ShapeDtypeStruct((blocks, SIZE, SIZE), F32),
+        in_specs=specs,
+        out_specs=HBM,
+        scratch_shapes=[pltpu.VMEM((4 * half, SIZE, SIZE), F32), pltpu.SemaphoreType.DMA((half,))],
+        input_output_aliases=alias,
+        name="final",
+        compiler_params=pltpu.CompilerParams(vmem_limit_bytes=LIMIT),
+        cost_estimate=pl.CostEstimate(flops=half * 2 * 2 * 256 * 256 * 64, bytes_accessed=half * 400_000, transcendentals=0),
+    )(*args)
 
 
 def swap(x, axis, k):
@@ -449,11 +503,11 @@
     for (axis, k), (here, there, _) in zip(steps[1:-1], starts):
         m = x.shape[0] // 2
         x = piece(x, here, m) + swap(piece(x, there, m), axis, k)
-    x = x + swap(x, *steps[-1])
+    x = (x + swap(x, *steps[-1])).astype(BF16)
     for (axis, k), (_, _, lower) in list(zip(steps[1:-1], starts))[::-1]:
         other = swap(x, axis, k)
         x = jnp.where(lower, jnp.concatenate([x, other]), jnp.concatenate([other, x]))
-    return x, swap(x, *steps[0])
+    return x
 
 
 def inner(out_grad, prev_state, boundary, angle_code, radius_code, reflect):
@@ -463,14 +517,18 @@
     tokens = prev_state.shape[1]
     groups = channels // GROUP
     half = groups // 2
-    width = half * GROUP
+    counts = [max(1, groups * 5 // 8)]
+    counts.append(groups - counts[0])
+    bases = [sum(counts[:n]) for n in range(len(counts))]
     place = place.astype(jnp.uint32)
 
-    def away(k, h):
-        start = (place ^ jnp.uint32(k)) * jnp.uint32(channels) + jnp.uint32(h * width)
-        return lax.dynamic_slice(rows, (jnp.uint32(0), start), (rows.shape[0], width))
-
-    parts = [[swap(away(k, h), "tensor", k) for k in range(1, peers)] for h in range(2)]
+    def away(k, base, count):
+        start = (place ^ jnp.uint32(k)) * jnp.uint32(channels) + jnp.uint32(base * GROUP)
+        return lax.dynamic_slice(rows, (jnp.uint32(0), start), (rows.shape[0], count * GROUP))
+
+    parts = []
+    for at in zip(bases, counts):
+        parts.append([swap(away(k, *at), "tensor", k) for k in range(1, peers)])
     steps = exchanges(("dp", "ctx"))
     size = half * SIZE
     starts = []
@@ -480,18 +538,26 @@
     side = jnp.reshape(lax.axis_index("dp") & 1, (1,))
     place = jnp.reshape(place.astype(jnp.int32), (1,))
     early = [bit == 0 for bit in bits(exchanges(("ctx",)))]
-    boundary, reflect, side, place, starts, early = lax.optimization_barrier((boundary, reflect, side, place, starts, early))
-    keep = jnp.where(boundary[0] == 1, jnp.float32(0.6), jnp.float32(1.0))
-    keep = jnp.broadcast_to(keep[:, None], (tokens, LANES))
-    high, low, tab, ktab, far, turned, decay, weight = prepare(reflect, angle_code, radius_code, keep, prev_state[0])
-    z_a, first_a, grad_a = scan_both(0, half, place, rows, parts[0], high, low, tab, ktab, keep, turned)
-    spaced, head, sent = scan_first(half, half, place, rows, parts[1], high, low, tab, ktab, keep, first_a)
+    code = angle_code * 1024 + radius_code
+    code, side, place, starts, early = lax.optimization_barrier((code, side, place, starts, early))
+    high, low, tab, far = basis(code, reflect, tokens // CHUNKS)
+    keep, ktab, turned, decay, weight = weights(boundary, tab, prev_state[0])
+    done = []
+    for base, count, part in zip(bases[:-1], counts[:-1], parts[:-1]):
+        done.append(scan_both(base, count, place, rows, part, high, low, tab, ktab, keep, turned))
+    base, count = bases[-1], counts[-1]
+    spaced, head, sent = scan_first(base, count, place, rows, parts[-1], high, low, tab, ktab, keep, [d[1] for d in done])
     entry = entering(sent, (far[0], far[1]), "ctx", early)
-    z_b, grad_b = scan_second(half, half, spaced, head, tab, ktab, keep, turned)
-    own, other = merge(side, grad_a, grad_b, weight, entry)
-    grad_input = states(z_a, z_b, decay, entry, high, low)
-    own, other = total_sum(own, other, steps, starts)
-    return grad_input[None], final(side, own, other, high, low)
+    z_last, grad_last = scan_second(base, count, spaced, head, tab, ktab, keep, turned)
+    own, other = merge(half, side, entry, weight, [d[2] for d in done] + [grad_last])
+    z = [d[0] for d in done] + [z_last]
+    grad_input = states(0, z[:1], decay, entry, high, low)
+    grad_input = states(bases[1], z[1:], decay, entry, high, low, grad_input)
+    own = total_sum(own, other, steps, starts)
+    other = swap(own, *steps[0])
+    grad_transition = final(False, side, own, high, low)
+    grad_transition = final(True, side, other, high, low, grad_transition)
+    return grad_input[None], grad_transition
 
 
 def solution(mesh):

time: 59.9 us -> 62.5 us (1.043)
  waiting for transfers between devices: 18.5 us -> 22.3 us
  local copies, waits for them, and re-layouts: 4.92 us -> 2.91 us
    ppermute x11, waiting for transfers between devices: 18.5 us -> 22.3 us  [swap(): return lax.ppermute(x, axis, [(i, i ^ k) for i in range(n)])]
    pallas_call x1 -> x4, Pallas kernels: 4.22 us -> 7.16 us  [the longest x2 4.85 us: states(): pl.pallas_call(functools.partial(state_kernel, base, sizes), grid=(sum(si...]
    pallas_call x6, Pallas kernels: 12.5 us -> 9.95 us  [call(): pl.pallas_call(kernel, out_shape=shapes, in_specs=specs, out_specs=[VMEM]...]
    reshape x2 -> x0, local copies, waits for them, and re-layouts: 1.57 us -> none  [the longest x1 0.79 us: prepare(): radius.reshape(groups, LANES)]
    unnamed x6 -> x8, local copies, waits for them, and re-layouts: 2.07 us -> 0.85 us
    dynamic_slice x1 -> x2, local copies, waits for them, and re-layouts: 1.15 us -> 2.02 us  [away(): lax.dynamic_slice(rows, (jnp.uint32(0), start), (rows.shape[0], count * G...]
    add x1, other arithmetic: 0.01 us -> 0.81 us  [inner(): code = angle_code * 1024 + radius_code]
    select_n x1 -> x0, other arithmetic: 0.68 us -> none  [inner(): keep = jnp.where(boundary[0] == 1, jnp.float32(0.6), jnp.float32(1.0))]
  transfers between devices with their start and end apart: 11 -> 11, of which waited for: 8 -> 9; matrix products, arithmetic and copies ran while one was open for 4% -> 3% of each run, Pallas kernels for 22% -> 24%
where the time goes in v3:
time: 62.5 us; the launch traced here: 62.2 us
  waiting for transfers between devices  22.3 us (36%)
  starting transfers between devices  18.2 us (29%)
  Pallas kernels  17.1 us (27%)
  local copies, waits for them, and re-layouts  2.91 us (5%)
  other arithmetic  0.96 us (2%)
  between operations  0.84 us (1%)
    ppermute x11, waiting for transfers between devices, swap(): return lax.ppermute(x, axis, [(i, i ^ k) for i in range(n)])  22.3 us
    ppermute x11, starting transfers between devices, swap(): return lax.ppermute(x, axis, [(i, i ^ k) for i in range(n)])  18.2 us
    pallas_call x6, Pallas kernels, call(): pl.pallas_call(kernel, out_shape=shapes, in_specs=specs, out_specs=[VMEM]...  9.95 us
    pallas_call x2, Pallas kernels, states(): pl.pallas_call(functools.partial(state_kernel, base, sizes), grid=(sum(si...  4.85 us
    pallas_call x2, Pallas kernels, final(): pl.pallas_call(functools.partial(final_kernel, flip), out_shape=jax.Shape...  2.31 us
    dynamic_slice x2, local copies, waits for them, and re-layouts, away(): lax.dynamic_slice(rows, (jnp.uint32(0), start), (rows.shape[0], count * G...  2.02 us
  transfers between devices with their start and end apart: 11, of which 9 were waited for; matrix products, arithmetic and copies ran while one was open for 3% of the time, Pallas kernels for 24%

profile of v3, /device:TPU:0, one launch (start us, length us, event | category | flops | bytes accessed | tf_op | source)
XLA Modules:
  0.0 62.2 jit_solution(1226777419634036928)
XLA Ops:
  0.6 0.0 copy-start.3
  0.6 0.0 copy-start.1
  0.7 1.0 %dynamic-slice_bitcast_fusion.1 = bf16[128,768]{1,0:T(8,128)(2,1)S(1)} fusion(bf16[1,128,4096]{2,1,0:T(8,128)(2,1)} %param.6, u32[]{:T(128)S(6)} %add.43), kind=kLoop, calls=%fused_computation.1 | loop fusion | bytes 393220 | tf_op jit(solution)/shard_map/dynamic_slice | solution.py:527
  1.7 3.1 %collective-permute-start = (bf16[128,768]{1,0:T(8,128)(2,1)S(1)}, bf16[128,768]{1,0:T(8,128)(2,1)S(1)}, u32[]{:S(2)}, u32[]{:S(2)}) collective-permute-start(bf16[128,768]{1,0:T(8,128)(2,1)S(1)} %dynamic-slice_bitcast_fusion.1), channel_id=1, source_target_pairs={{0,1},{1,0},{2,3},{3,2},{4,5},{5,4},{6,7},{7,6},{8,9},{9,8},{10,11... | collective-permute-start | bytes 589832 | tf_op jit(solution)/shard_map/ppermute | solution.py:452
  4.8 1.0 %dynamic-slice_bitcast_fusion = bf16[128,1280]{1,0:T(8,128)(2,1)S(1)} fusion(bf16[1,128,4096]{2,1,0:T(8,128)(2,1)} %param.6, u32[]{:T(128)S(6)} %mul.87), kind=kLoop, calls=%fused_computation | loop fusion | bytes 655364 | tf_op jit(solution)/shard_map/dynamic_slice | solution.py:527
  5.7 0.0 copy-start
  5.8 0.1 collective-permute-start.1
  5.8 0.8 %multiply_add_fusion.code_ref = s32[32,32]{1,0:T(8,128)S(1)} fusion(s32[32,32]{1,0:T(8,128)} %param.10, s32[32,32]{1,0:T(8,128)} %param.9), kind=kLoop, calls=%fused_computation.7 | loop fusion | flops 2048 | bytes 12288 | tf_op jit(solution)/shard_map/add | solution.py:541
  6.7 0.0 copy-start.2
  6.7 0.8 %copy-done.2 = f32[32,4,64]{2,1,0:T(4,128)S(1)} copy-done((f32[32,4,64]{2,1,0:T(4,128)S(1)}, f32[32,4,64]{2,1,0:T(4,128)}, u32[]{:S(2)}) %copy-start.2) | copy-done | bytes 32792
  7.5 1.1 %shard_map.77 = (bf16[8,256,256]{2,1,0:T(8,128)(2,1)S(1)}, bf16[8,256,256]{2,1,0:T(8,128)(2,1)S(1)}, f32[8,2,8,128]{3,2,1,0:T(8,128)S(1)}, f32[2,8,128]{2,1,0:T(8,128)S(1)}) custom-call(s32[32,32]{1,0:T(8,128)S(1)} %multiply_add_fusion.code_ref, f32[128,64]{1,0:T(8,128)S(1)} %bitcast.77), custom_call_target="tpu_custom_call" | custom-call | flops 536870912 | bytes 2207744 | tf_op jit(solution)/shard_map/pallas_call | solution.py:204
  8.6 0.0 copy-done.3
  8.6 0.0 copy-done.1
  8.6 3.0 %shard_map.78 = (f32[256,128]{1,0:T(8,128)S(1)}, f32[5,8,128]{2,1,0:T(8,128)S(1)}, bf16[2048,256]{1,0:T(8,128)(2,1)S(1)}, f32[8,2,256,128]{3,2,1,0:T(8,128)S(1)}, f32[8,64,256]{2,1,0:T(8,128)S(1)}) custom-call(s32[1,256]{1,0:T(1,128)S(1)} %copy-done.3, f32[8,2,8,128]{3,2,1,0:T(8,128)S(1)} %get-tuple-element.35.tab_ref.refs_0_, bf16[256,2048]{1,0:T(8,128)(2,1)S(1)} %bitcast.76), custom_call_target="tpu_custom_call" | custom-call | flops 536870912 | bytes 4936704 | tf_op jit(solution)/shard_map/pallas_call | solution.py:204
  11.6 5.1 %collective-permute-done.1.refs_7_ = bf16[128,1280]{1,0:T(8,128)(2,1)S(1)} collective-permute-done((bf16[128,1280]{1,0:T(8,128)(2,1)S(1)}, bf16[128,1280]{1,0:T(8,128)(2,1)S(1)}, u32[]{:S(2)}, u32[]{:S(2)}) %collective-permute-start.1) | collective-permute-done | bytes 327712 | tf_op jit(solution)/shard_map/ppermute | solution.py:452
  16.7 0.0 copy-done
  16.7 3.3 %shard_map.79 = (f32[5,2,256,128]{3,2,1,0:T(8,128)S(1)}, f32[2,5,128]{2,1,0:T(8,128)S(1)}, f32[5,64,256]{2,1,0:T(8,128)S(1)}) custom-call(f32[8,2,8,128]{3,2,1,0:T(8,128)S(1)} %get-tuple-element.35.tab_ref.refs_0_, f32[5,8,128]{2,1,0:T(8,128)S(1)} %get-tuple-element.36.refs_1_, f32[256,128]{1,0:T(8,128)S(1)} %get-tuple-element.37.refs_2_, s32[1]{0:T(128)} %bitcast.1.refs_3_, ...), custom_call_target="tpu_custom_call" | custom-call | flops 671088640 | bytes 6382596 | tf_op jit(solution)/shard_map/pallas_call | solution.py:204
  20.0 0.0 collective-permute-done.refs_7_
  20.0 1.1 %shard_map.80 = (f32[3,2,256,128]{3,2,1,0:T(8,128)S(1)}, f32[3,2,8,128]{3,2,1,0:T(8,128)S(1)}, f32[24,128]{1,0:T(8,128)S(1)}) custom-call(f32[8,2,8,128]{3,2,1,0:T(8,128)S(1)} %get-tuple-element.35.tab_ref.refs_0_, f32[5,8,128]{2,1,0:T(8,128)S(1)} %get-tuple-element.36.refs_1_, f32[256,128]{1,0:T(8,128)S(1)} %get-tuple-element.37.refs_2_, s32[1]{0:T(128)} %bitcast.1.refs_3_, ...), custom_call_target="tpu_custom_call" | custom-call | flops 201326592 | bytes 4387844 | tf_op jit(solution)/shard_map/pallas_call | solution.py:204
  21.1 1.9 %collective-permute-start.2 = (f32[24,128]{1,0:T(8,128)S(1)}, f32[24,128]{1,0:T(8,128)S(1)}, u32[]{:S(2)}, u32[]{:S(2)}) collective-permute-start(f32[24,128]{1,0:T(8,128)S(1)} %get-tuple-element.43), channel_id=1, source_target_pairs={{0,2},{2,0},{4,6},{6,4},{1,3},{3,1},{5,7},{7,5},{8,10},{10,8},{12,... | collective-permute-start | bytes 36872 | tf_op jit(solution)/shard_map/ppermute | solution.py:452
  23.0 1.9 %collective-permute-done.2 = f32[24,128]{1,0:T(8,128)S(1)} collective-permute-done((f32[24,128]{1,0:T(8,128)S(1)}, f32[24,128]{1,0:T(8,128)S(1)}, u32[]{:S(2)}, u32[]{:S(2)}) %collective-permute-start.2) | collective-permute-done | bytes 12320 | tf_op jit(solution)/shard_map/ppermute | solution.py:452
  24.9 2.9 %collective-permute-start.3 = (f32[24,128]{1,0:T(8,128)S(1)}, f32[24,128]{1,0:T(8,128)S(1)}, u32[]{:S(2)}, u32[]{:S(2)}) collective-permute-start(f32[24,128]{1,0:T(8,128)S(1)} %pad_maximum_fusion), channel_id=1, source_target_pairs={{0,4},{2,6},{4,0},{6,2},{1,5},{3,7},{5,1},{7,3},{8,12},{10,14},{12... | collective-permute-start | bytes 36872 | tf_op jit(solution)/shard_map/ppermute | solution.py:452
  27.8 1.4 %shard_map.81 = (f32[3,2,256,128]{3,2,1,0:T(8,128)S(1)}, f32[3,64,256]{2,1,0:T(8,128)S(1)}) custom-call(f32[8,2,8,128]{3,2,1,0:T(8,128)S(1)} %get-tuple-element.35.tab_ref.refs_0_, f32[5,8,128]{2,1,0:T(8,128)S(1)} %get-tuple-element.36.refs_1_, f32[256,128]{1,0:T(8,128)S(1)} %get-tuple-element.37.refs_2_, ...), custom_call_target="tpu_custom_call" | custom-call | flops 201326592 | bytes 3059712 | tf_op jit(solution)/shard_map/pallas_call | solution.py:204
  29.2 0.4 collective-permute-done.3
  29.6 0.1 shard_map.82
  29.7 0.1 collective-permute-start.4
  29.8 1.5 %collective-permute-done.4 = f32[256,256]{1,0:T(8,128)S(1)} collective-permute-done((f32[256,256]{1,0:T(8,128)S(1)}, f32[256,256]{1,0:T(8,128)S(1)}, u32[]{:S(2)}, u32[]{:S(2)}) %collective-permute-start.4) | collective-permute-done | bytes 262176 | tf_op jit(solution)/shard_map/ppermute | solution.py:452
  31.4 1.8 %collective-permute-start.5 = (f32[128,256]{1,0:T(8,128)S(1)}, f32[128,256]{1,0:T(8,128)S(1)}, u32[]{:S(2)}, u32[]{:S(2)}) collective-permute-start(f32[128,256]{1,0:T(8,128)S(1)} %constant_dynamic-slice_fusion.1), channel_id=1, source_target_pairs={{0,16},{8,24},{16,0},{24,8},{1,17},{9,25},{17,1},{25,9},{2,18},{10... | collective-permute-start | bytes 393224 | tf_op jit(solution)/shard_map/ppermute | solution.py:452
  33.1 3.8 %collective-permute-done.5 = f32[128,256]{1,0:T(8,128)S(1)} collective-permute-done((f32[128,256]{1,0:T(8,128)S(1)}, f32[128,256]{1,0:T(8,128)S(1)}, u32[]{:S(2)}, u32[]{:S(2)}) %collective-permute-start.5) | collective-permute-done | bytes 131104 | tf_op jit(solution)/shard_map/ppermute | solution.py:452
  37.0 1.9 %collective-permute-start.6 = (f32[64,256]{1,0:T(8,128)S(1)}, f32[64,256]{1,0:T(8,128)S(1)}, u32[]{:S(2)}, u32[]{:S(2)}) collective-permute-start(f32[64,256]{1,0:T(8,128)S(1)} %constant_dynamic-slice_fusion), channel_id=1, source_target_pairs={{0,2},{2,0},{4,6},{6,4},{1,3},{3,1},{5,7},{7,5},{8,10},{10,8},{12,... | collective-permute-start | bytes 196616 | tf_op jit(solution)/shard_map/ppermute | solution.py:452
  38.9 2.5 %collective-permute-done.6 = f32[64,256]{1,0:T(8,128)S(1)} collective-permute-done((f32[64,256]{1,0:T(8,128)S(1)}, f32[64,256]{1,0:T(8,128)S(1)}, u32[]{:S(2)}, u32[]{:S(2)}) %collective-permute-start.6) | collective-permute-done | bytes 65568 | tf_op jit(solution)/shard_map/ppermute | solution.py:452
  41.4 2.9 %collective-permute-start.7 = (f32[64,256]{1,0:T(8,128)S(1)}, f32[64,256]{1,0:T(8,128)S(1)}, u32[]{:S(2)}, u32[]{:S(2)}) collective-permute-start(f32[64,256]{1,0:T(8,128)S(1)} %dynamic-slice_add_fusion.1), channel_id=1, source_target_pairs={{0,4},{2,6},{4,0},{6,2},{1,5},{3,7},{5,1},{7,3},{8,12},{10,14},{12... | collective-permute-start | bytes 196616 | tf_op jit(solution)/shard_map/ppermute | solution.py:452
  44.2 2.4 %collective-permute-done.7 = f32[64,256]{1,0:T(8,128)S(1)} collective-permute-done((f32[64,256]{1,0:T(8,128)S(1)}, f32[64,256]{1,0:T(8,128)S(1)}, u32[]{:S(2)}, u32[]{:S(2)}) %collective-permute-start.7) | collective-permute-done | bytes 65568 | tf_op jit(solution)/shard_map/ppermute | solution.py:452
  46.6 1.8 %collective-permute-start.8 = (bf16[64,256]{1,0:T(8,128)(2,1)S(1)}, bf16[64,256]{1,0:T(8,128)(2,1)S(1)}, u32[]{:S(2)}, u32[]{:S(2)}) collective-permute-start(bf16[64,256]{1,0:T(8,128)(2,1)S(1)} %add_convert_fusion), channel_id=1, source_target_pairs={{0,2},{2,0},{4,6},{6,4},{1,3},{3,1},{5,7},{7,5},{8,10},{10,8},{12,... | collective-permute-start | bytes 98312 | tf_op jit(solution)/shard_map/ppermute | solution.py:452
  48.5 2.1 %collective-permute-done.8 = bf16[64,256]{1,0:T(8,128)(2,1)S(1)} collective-permute-done((bf16[64,256]{1,0:T(8,128)(2,1)S(1)}, bf16[64,256]{1,0:T(8,128)(2,1)S(1)}, u32[]{:S(2)}, u32[]{:S(2)}) %collective-permute-start.8) | collective-permute-done | bytes 32800 | tf_op jit(solution)/shard_map/ppermute | solution.py:452
  50.6 1.8 %collective-permute-start.9 = (bf16[128,256]{1,0:T(8,128)(2,1)S(1)}, bf16[128,256]{1,0:T(8,128)(2,1)S(1)}, u32[]{:S(2)}, u32[]{:S(2)}) collective-permute-start(bf16[128,256]{1,0:T(8,128)(2,1)S(1)} %maximum_select_fusion.1), channel_id=1, source_target_pairs={{0,16},{8,24},{16,0},{24,8},{1,17},{9,25},{17,1},{25,9},{2,18},{10... | collective-permute-start | bytes 196616 | tf_op jit(solution)/shard_map/ppermute | solution.py:452
  52.4 2.5 %collective-permute-done.9 = bf16[128,256]{1,0:T(8,128)(2,1)S(1)} collective-permute-done((bf16[128,256]{1,0:T(8,128)(2,1)S(1)}, bf16[128,256]{1,0:T(8,128)(2,1)S(1)}, u32[]{:S(2)}, u32[]{:S(2)}) %collective-permute-start.9) | collective-permute-done | bytes 65568 | tf_op jit(solution)/shard_map/ppermute | solution.py:452
  55.0 0.1 collective-permute-start.10
  55.1 2.9 %states.2.refs_1_ = bf16[256,2048]{1,0:T(8,128)(2,1)} custom-call(f32[2,8,128]{2,1,0:T(8,128)S(1)} %pad_maximum_fusion.1.entry_ref, f32[8,2,256,128]{3,2,1,0:T(8,128)S(1)} %get-tuple-element.45.decay_ref, bf16[8,256,256]{2,1,0:T(8,128)(2,1)S(1)} %get-tuple-element.39.refs_5_.high_ref, bf16[8,256,256]{2,1,0:T(8,128)(2,1)S(1)} %get-tuple-element.40.refs_6_.low_ref, ...), custom_call_target="tpu_custom_call" | custom-call | flops 503316480 | bytes 4500000 | tf_op jit(solution)/shard_map/states/pallas_call | solution.py:397
  58.0 1.9 %states.3 = bf16[256,2048]{1,0:T(8,128)(2,1)} custom-call(f32[2,8,128]{2,1,0:T(8,128)S(1)} %pad_maximum_fusion.1.entry_ref, f32[8,2,256,128]{3,2,1,0:T(8,128)S(1)} %get-tuple-element.45.decay_ref, bf16[8,256,256]{2,1,0:T(8,128)(2,1)S(1)} %get-tuple-element.39.refs_5_.high_ref, ...), custom_call_target="tpu_custom_call", output_to_operand_aliasing={{}: (5, {})} | custom-call | flops 301989888 | bytes 2700000 | tf_op jit(solution)/shard_map/states/pallas_call | solution.py:397
  59.9 1.1 %final.2.refs_0_ = f32[32,64,64]{2,1,0:T(8,128)} custom-call(s32[1]{0:T(128)} %bitcast.side_ref, bf16[256,256]{1,0:T(8,128)(2,1)S(1)} %maximum_select_fusion.x_ref, bf16[8,256,256]{2,1,0:T(8,128)(2,1)S(1)} %get-tuple-element.39.refs_5_.high_ref, bf16[8,256,256]{2,1,0:T(8,128)(2,1)S(1)} %get-tuple-element.40.refs_6_.low_ref), custom_call_target="tpu_custom_call" | custom-call | flops 67108864 | bytes 1600000 | tf_op jit(solution)/shard_map/final/pallas_call | solution.py:437
  61.1 0.0 collective-permute-done.10.x_ref
  61.1 1.2 %final.3 = f32[32,64,64]{2,1,0:T(8,128)} custom-call(s32[1]{0:T(128)} %bitcast.side_ref, bf16[256,256]{1,0:T(8,128)(2,1)S(1)} %collective-permute-done.10.x_ref, bf16[8,256,256]{2,1,0:T(8,128)(2,1)S(1)} %get-tuple-element.39.refs_5_.high_ref, bf16[8,256,256]{2,1,0:T(8,128)(2,1)S(1)} %get-tuple-element.40.refs_6_.low_ref, ...), custom_call_target="tpu_custom_call", output_to_operand_aliasing={{}: (4, {})} | custom-call | flops 67108864 | bytes 1600000 | tf_op jit(solution)/shard_map/final/pallas_call | solution.py:437
  (14 shorter events, 0.2 us)
Async XLA Ops:
  0.6 7.9 %copy-start.3 = (s32[1,256]{1,0:T(1,128)S(1)}, s32[1,256]{1,0:T(1,128)}, u32[]{:S(2)}) copy-start(s32[1,256]{1,0:T(1,128)} %boundary_ref.1) | copy-start | bytes 3076
  0.6 7.9 %copy-start.1 = (bf16[1,256,2048]{2,1,0:T(8,128)(2,1)S(1)}, bf16[1,256,2048]{2,1,0:T(8,128)(2,1)}, u32[]{:S(2)}) copy-start(bf16[1,256,2048]{2,1,0:T(8,128)(2,1)} %param.7) | copy-start | bytes 3145732
  1.7 18.3 %collective-permute-start = (bf16[128,768]{1,0:T(8,128)(2,1)S(1)}, bf16[128,768]{1,0:T(8,128)(2,1)S(1)}, u32[]{:S(2)}, u32[]{:S(2)}) collective-permute-start(bf16[128,768]{1,0:T(8,128)(2,1)S(1)} %dynamic-slice_bitcast_fusion.1), channel_id=1, source_target_pairs={{0,1},{1,0},{2,3},{3,2},{4,5},{5,4},{6,7},{7,6},{8,9},{9,8},{10,11... | collective-permute-start | bytes 589832 | tf_op jit(solution)/shard_map/ppermute | solution.py:452
  5.7 10.9 %copy-start = (bf16[1,128,4096]{2,1,0:T(8,128)(2,1)S(1)}, bf16[1,128,4096]{2,1,0:T(8,128)(2,1)}, u32[]{:S(2)}) copy-start(bf16[1,128,4096]{2,1,0:T(8,128)(2,1)} %param.6) | copy-start | bytes 3145732
  5.8 10.9 %collective-permute-start.1 = (bf16[128,1280]{1,0:T(8,128)(2,1)S(1)}, bf16[128,1280]{1,0:T(8,128)(2,1)S(1)}, u32[]{:S(2)}, u32[]{:S(2)}) collective-permute-start(bf16[128,1280]{1,0:T(8,128)(2,1)S(1)} %dynamic-slice_bitcast_fusion), channel_id=1, source_target_pairs={{0,1},{1,0},{2,3},{3,2},{4,5},{5,4},{6,7},{7,6},{8,9},{9,8},{10,11... | collective-permute-start | bytes 983048 | tf_op jit(solution)/shard_map/ppermute | solution.py:452
  6.7 0.8 %copy-start.2 = (f32[32,4,64]{2,1,0:T(4,128)S(1)}, f32[32,4,64]{2,1,0:T(4,128)}, u32[]{:S(2)}) copy-start(f32[32,4,64]{2,1,0:T(4,128)} %param.11) | copy-start | bytes 98308
  21.1 3.8 %collective-permute-start.2 = (f32[24,128]{1,0:T(8,128)S(1)}, f32[24,128]{1,0:T(8,128)S(1)}, u32[]{:S(2)}, u32[]{:S(2)}) collective-permute-start(f32[24,128]{1,0:T(8,128)S(1)} %get-tuple-element.43), channel_id=1, source_target_pairs={{0,2},{2,0},{4,6},{6,4},{1,3},{3,1},{5,7},{7,5},{8,10},{10,8},{12,... | collective-permute-start | bytes 36872 | tf_op jit(solution)/shard_map/ppermute | solution.py:452
  24.9 4.7 %collective-permute-start.3 = (f32[24,128]{1,0:T(8,128)S(1)}, f32[24,128]{1,0:T(8,128)S(1)}, u32[]{:S(2)}, u32[]{:S(2)}) collective-permute-start(f32[24,128]{1,0:T(8,128)S(1)} %pad_maximum_fusion), channel_id=1, source_target_pairs={{0,4},{2,6},{4,0},{6,2},{1,5},{3,7},{5,1},{7,3},{8,12},{10,14},{12... | collective-permute-start | bytes 36872 | tf_op jit(solution)/shard_map/ppermute | solution.py:452
  29.7 1.6 %collective-permute-start.4 = (f32[256,256]{1,0:T(8,128)S(1)}, f32[256,256]{1,0:T(8,128)S(1)}, u32[]{:S(2)}, u32[]{:S(2)}) collective-permute-start(f32[256,256]{1,0:T(8,128)S(1)} %get-tuple-element.57), channel_id=1, source_target_pairs={{0,8},{8,0},{16,24},{24,16},{1,9},{9,1},{17,25},{25,17},{2,10},{10... | collective-permute-start | bytes 786440 | tf_op jit(solution)/shard_map/ppermute | solution.py:452
  31.4 5.6 %collective-permute-start.5 = (f32[128,256]{1,0:T(8,128)S(1)}, f32[128,256]{1,0:T(8,128)S(1)}, u32[]{:S(2)}, u32[]{:S(2)}) collective-permute-start(f32[128,256]{1,0:T(8,128)S(1)} %constant_dynamic-slice_fusion.1), channel_id=1, source_target_pairs={{0,16},{8,24},{16,0},{24,8},{1,17},{9,25},{17,1},{25,9},{2,18},{10... | collective-permute-start | bytes 393224 | tf_op jit(solution)/shard_map/ppermute | solution.py:452
  37.0 4.3 %collective-permute-start.6 = (f32[64,256]{1,0:T(8,128)S(1)}, f32[64,256]{1,0:T(8,128)S(1)}, u32[]{:S(2)}, u32[]{:S(2)}) collective-permute-start(f32[64,256]{1,0:T(8,128)S(1)} %constant_dynamic-slice_fusion), channel_id=1, source_target_pairs={{0,2},{2,0},{4,6},{6,4},{1,3},{3,1},{5,7},{7,5},{8,10},{10,8},{12,... | collective-permute-start | bytes 196616 | tf_op jit(solution)/shard_map/ppermute | solution.py:452
  41.4 5.2 %collective-permute-start.7 = (f32[64,256]{1,0:T(8,128)S(1)}, f32[64,256]{1,0:T(8,128)S(1)}, u32[]{:S(2)}, u32[]{:S(2)}) collective-permute-start(f32[64,256]{1,0:T(8,128)S(1)} %dynamic-slice_add_fusion.1), channel_id=1, source_target_pairs={{0,4},{2,6},{4,0},{6,2},{1,5},{3,7},{5,1},{7,3},{8,12},{10,14},{12... | collective-permute-start | bytes 196616 | tf_op jit(solution)/shard_map/ppermute | solution.py:452
  46.6 4.0 %collective-permute-start.8 = (bf16[64,256]{1,0:T(8,128)(2,1)S(1)}, bf16[64,256]{1,0:T(8,128)(2,1)S(1)}, u32[]{:S(2)}, u32[]{:S(2)}) collective-permute-start(bf16[64,256]{1,0:T(8,128)(2,1)S(1)} %add_convert_fusion), channel_id=1, source_target_pairs={{0,2},{2,0},{4,6},{6,4},{1,3},{3,1},{5,7},{7,5},{8,10},{10,8},{12,... | collective-permute-start | bytes 98312 | tf_op jit(solution)/shard_map/ppermute | solution.py:452
  50.6 4.3 %collective-permute-start.9 = (bf16[128,256]{1,0:T(8,128)(2,1)S(1)}, bf16[128,256]{1,0:T(8,128)(2,1)S(1)}, u32[]{:S(2)}, u32[]{:S(2)}) collective-permute-start(bf16[128,256]{1,0:T(8,128)(2,1)S(1)} %maximum_select_fusion.1), channel_id=1, source_target_pairs={{0,16},{8,24},{16,0},{24,8},{1,17},{9,25},{17,1},{25,9},{2,18},{10... | collective-permute-start | bytes 196616 | tf_op jit(solution)/shard_map/ppermute | solution.py:452
  55.0 6.1 %collective-permute-start.10 = (bf16[256,256]{1,0:T(8,128)(2,1)S(1)}, bf16[256,256]{1,0:T(8,128)(2,1)S(1)}, u32[]{:S(2)}, u32[]{:S(2)}) collective-permute-start(bf16[256,256]{1,0:T(8,128)(2,1)S(1)} %maximum_select_fusion.x_ref), channel_id=1, source_target_pairs={{0,8},{8,0},{16,24},{24,16},{1,9},{9,1},{17,25},{25,17},{2,10},{10... | collective-permute-start | bytes 393224 | tf_op jit(solution)/shard_map/ppermute | solution.py:452

commit v4 on v3

--- a/solution.py
+++ b/solution.py
@@ -365,13 +365,14 @@
 
 def state_kernel(base, sizes, entry_ref, decay_ref, high_ref, low_ref, *refs):
     parts, out_ref = refs[: len(sizes)], refs[-1]
-    g = pl.program_id(0)
-    re, im = entry_ref[0, pl.ds(base + g, 1), :], entry_ref[1, pl.ds(base + g, 1), :]
+    g = pl.program_id(0) + base
+    re, im = entry_ref[0, pl.ds(g, 1), :], entry_ref[1, pl.ds(g, 1), :]
     d_re, d_im = decay_ref[0, 0], decay_ref[0, 1]
     z_re, z_im = parts[0][0, 0], parts[0][0, 1]
-    if len(parts) > 1:
-        first = g < sizes[0]
-        z_re, z_im = jnp.where(first, z_re, parts[1][0, 0]), jnp.where(first, z_im, parts[1][0, 1])
+    start = 0
+    for size, part in zip(sizes[:-1], parts[1:]):
+        start += size
+        z_re, z_im = jnp.where(g < start, z_re, part[0, 0]), jnp.where(g < start, z_im, part[0, 1])
     z_re = z_re + (re * d_re - im * d_im)
     z_im = z_im + (re * d_im + im * d_re)
     z_high, z_low = split(jnp.concatenate([z_re, z_im], axis=1))
@@ -379,16 +380,18 @@
     out_ref[...] = out.astype(BF16)
 
 
-def states(base, parts, decay, entry, high, low, filled=None):
+def states(base, count, parts, decay, entry, high, low, filled=None):
     groups = high.shape[0]
     tokens = parts[0].shape[2]
     sizes = [part.shape[0] for part in parts]
     each = lambda shape: pl.BlockSpec((1,) + shape, lambda g: (g + base, 0, 0, 0)[: len(shape) + 1])
-    shape = (1, 2, tokens, LANES)
-    picks = [pl.BlockSpec(shape, lambda g: (jnp.minimum(g, sizes[0] - 1), 0, 0, 0))]
-    picks += [pl.BlockSpec(shape, lambda g: (jnp.maximum(g - sizes[0], 0), 0, 0, 0)) for _ in parts[1:]]
+
+    def pick(start, size):
+        return pl.BlockSpec((1, 2, tokens, LANES), lambda g: (jnp.minimum(jnp.maximum(g + base - start, 0), size - 1), 0, 0, 0))
+
     args = [entry, decay, high, low, *parts]
-    specs = [pl.BlockSpec(entry.shape, lambda g: (0, 0, 0)), each((2, tokens, LANES)), each((GROUP, GROUP)), each((GROUP, GROUP)), *picks]
+    specs = [pl.BlockSpec(entry.shape, lambda g: (0, 0, 0)), each((2, tokens, LANES)), each((GROUP, GROUP)), each((GROUP, GROUP))]
+    specs += [pick(sum(sizes[:n]), size) for n, size in enumerate(sizes)]
     alias = {}
     if filled is not None:
         alias = {len(args): 0}
@@ -396,15 +399,58 @@
         specs.append(pl.BlockSpec(memory_space=pl.ANY))
     return pl.pallas_call(
         functools.partial(state_kernel, base, sizes),
-        grid=(sum(sizes),),
+        grid=(count,),
         in_specs=specs,
         out_specs=pl.BlockSpec((tokens, GROUP), lambda g: (0, g + base)),
         out_shape=jax.ShapeDtypeStruct((tokens, groups * GROUP), BF16),
         input_output_aliases=alias,
         name="states",
         compiler_params=pltpu.CompilerParams(vmem_limit_bytes=LIMIT),
-        cost_estimate=pl.CostEstimate(flops=sum(sizes) * 3 * 2 * 256**3, bytes_accessed=sum(sizes) * 900_000, transcendentals=0),
+        cost_estimate=pl.CostEstimate(flops=count * 3 * 2 * 256**3, bytes_accessed=count * 900_000, transcendentals=0),
     )(*args)
+
+
+EXTRA = 16
+STEPS = 32000.0
+
+
+def encode(x, code_ref):
+    rows = x.shape[0]
+    most = jnp.maximum(jnp.max(jnp.abs(x), axis=0, keepdims=True), 1e-30)
+    power = jnp.ceil(jnp.log2(most))
+    code = jnp.floor(x * (jnp.exp2(-power) * STEPS) + 0.5)
+    code_ref[:rows, :] = code.astype(jnp.int32).astype(jnp.int16)
+    code_ref[rows:, :] = jnp.broadcast_to(power, (EXTRA, power.shape[1])).astype(jnp.int32).astype(jnp.int16)
+
+
+def decode(code_ref, start=0, rows=None):
+    if rows is None:
+        rows = code_ref.shape[0] - EXTRA
+    power = code_ref[start + rows : start + rows + EXTRA, :].astype(jnp.int32).astype(F32)[:1]
+    return code_ref[start : start + rows, :].astype(jnp.int32).astype(F32) * (jnp.exp2(power) * (1.0 / STEPS))
+
+
+def halve_kernel(bit_ref, own_ref, got_ref, here_ref, code_ref):
+    rows = here_ref.shape[0]
+    bit = bit_ref[0]
+    here, there = (pl.ds(pl.multiple_of(n * rows, rows), rows) for n in (bit, 1 - bit))
+    here_ref[...] = own_ref[here, :] + got_ref[here, :]
+    encode(own_ref[there, :] + got_ref[there, :], code_ref)
+
+
+def halve(bit, own, got):
+    rows, width = own.shape[0] // 2, own.shape[1]
+    out = [((rows, width), F32), ((rows + EXTRA, width), jnp.dtype(jnp.int16))]
+    return call(halve_kernel, out, (bit, own, got), [SMEM, VMEM, VMEM])
+
+
+def add_kernel(own_ref, got_ref, code_ref):
+    own = own_ref[...] if own_ref.dtype == F32 else decode(own_ref)
+    encode(own + decode(got_ref), code_ref)
+
+
+def add(own, got):
+    return call(add_kernel, [(got.shape, got.dtype)], (own, got), [VMEM, VMEM])[0]
 
 
 def final_kernel(flip, side_ref, x_ref, high_ref, low_ref, *refs):
@@ -412,10 +458,12 @@
     half = high_ref.shape[0] // 2
     which = 1 - side_ref[0] if flip else side_ref[0]
     copies = []
+    rows = x_ref.shape[0] // 2 - EXTRA
+    x = jnp.concatenate([decode(x_ref, n * (rows + EXTRA), rows) for n in range(2)], axis=0)
     for n in range(half):
         at = which * half + n
-        x = x_ref[n * SIZE : (n + 1) * SIZE, :]
-        out = matmul(high_ref[at], x, NT) + matmul(low_ref[at], x, NT)
+        x_high, x_low = split(x[n * SIZE : (n + 1) * SIZE, :])
+        out = matmul(high_ref[at], x_high, NT) + matmul(low_ref[at], x_high, NT) + matmul(high_ref[at], x_low, NT)
         for j in range(4):
             out_ref[4 * n + j] = out[j * SIZE : (j + 1) * SIZE]
         copies.append(pltpu.make_async_copy(out_ref.at[pl.ds(4 * n, 4)], out_hbm.at[pl.ds(at * 4, 4)], sems.at[n]))
@@ -443,7 +491,7 @@
         input_output_aliases=alias,
         name="final",
         compiler_params=pltpu.CompilerParams(vmem_limit_bytes=LIMIT),
-        cost_estimate=pl.CostEstimate(flops=half * 2 * 2 * 256 * 256 * 64, bytes_accessed=half * 400_000, transcendentals=0),
+        cost_estimate=pl.CostEstimate(flops=half * 3 * 2 * 256 * 256 * 64, bytes_accessed=half * 400_000, transcendentals=0),
     )(*args)
 
 
@@ -494,20 +542,16 @@
     return [(lax.axis_index(axis).astype(jnp.uint32) // jnp.uint32(k)) & jnp.uint32(1) for axis, k in steps]
 
 
-def piece(x, start, size):
-    return lax.dynamic_slice(x, (start, jnp.uint32(0)), (size, x.shape[1]))
-
-
-def total_sum(own, away, steps, starts):
-    x = own + swap(away, *steps[0])
-    for (axis, k), (here, there, _) in zip(steps[1:-1], starts):
-        m = x.shape[0] // 2
-        x = piece(x, here, m) + swap(piece(x, there, m), axis, k)
-    x = (x + swap(x, *steps[-1])).astype(BF16)
-    for (axis, k), (_, _, lower) in list(zip(steps[1:-1], starts))[::-1]:
-        other = swap(x, axis, k)
-        x = jnp.where(lower, jnp.concatenate([x, other]), jnp.concatenate([other, x]))
-    return x
+def total_sum(own, away, steps, bit, lower):
+    got = swap(away, *steps[0])
+    here, code = halve(bit, own, got)
+    got = swap(code, *steps[1])
+    code = add(here, got)
+    for step in steps[2:]:
+        got = swap(code, *step)
+        code = add(code, got)
+    other = swap(code, *steps[1])
+    return jnp.where(lower, jnp.concatenate([code, other]), jnp.concatenate([other, code]))
 
 
 def inner(out_grad, prev_state, boundary, angle_code, radius_code, reflect):
@@ -530,16 +574,14 @@
     for at in zip(bases, counts):
         parts.append([swap(away(k, *at), "tensor", k) for k in range(1, peers)])
     steps = exchanges(("dp", "ctx"))
-    size = half * SIZE
-    starts = []
-    for bit in bits(steps)[1:-1]:
-        size //= 2
-        starts.append((bit * jnp.uint32(size), (jnp.uint32(1) - bit) * jnp.uint32(size), bit == 0))
+    bit = bits(steps)[1]
+    lower = bit == 0
+    bit = jnp.reshape(bit.astype(jnp.int32), (1,))
     side = jnp.reshape(lax.axis_index("dp") & 1, (1,))
     place = jnp.reshape(place.astype(jnp.int32), (1,))
     early = [bit == 0 for bit in bits(exchanges(("ctx",)))]
     code = angle_code * 1024 + radius_code
-    code, side, place, starts, early = lax.optimization_barrier((code, side, place, starts, early))
+    code, side, place, bit, lower, early = lax.optimization_barrier((code, side, place, bit, lower, early))
     high, low, tab, far = basis(code, reflect, tokens // CHUNKS)
     keep, ktab, turned, decay, weight = weights(boundary, tab, prev_state[0])
     done = []
@@ -551,9 +593,9 @@
     z_last, grad_last = scan_second(base, count, spaced, head, tab, ktab, keep, turned)
     own, other = merge(half, side, entry, weight, [d[2] for d in done] + [grad_last])
     z = [d[0] for d in done] + [z_last]
-    grad_input = states(0, z[:1], decay, entry, high, low)
-    grad_input = states(bases[1], z[1:], decay, entry, high, low, grad_input)
-    own = total_sum(own, other, steps, starts)
+    grad_input = states(0, half, z, decay, entry, high, low)
+    grad_input = states(half, groups - half, z, decay, entry, high, low, grad_input)
+    own = total_sum(own, other, steps, bit, lower)
     other = swap(own, *steps[0])
     grad_transition = final(False, side, own, high, low)
     grad_transition = final(True, side, other, high, low, grad_transition)

time: 62.5 us -> 57.9 us (0.926)
  waiting for transfers between devices: 22.3 us -> 19.2 us
  starting transfers between devices: 18.2 us -> 16.3 us
    ppermute x11 -> x10, waiting for transfers between devices: 22.3 us -> 19.2 us  [swap(): return lax.ppermute(x, axis, [(i, i ^ k) for i in range(n)])]
    ppermute x11 -> x10, starting transfers between devices: 18.2 us -> 16.3 us  [swap(): return lax.ppermute(x, axis, [(i, i ^ k) for i in range(n)])]
    pallas_call x6 -> x10, Pallas kernels: 9.95 us -> 10.3 us  [call(): pl.pallas_call(kernel, out_shape=shapes, in_specs=specs, out_specs=[VMEM]...]
  transfers between devices with their start and end apart: 11 -> 10, of which waited for: 9 -> 8; matrix products, arithmetic and copies ran while one was open for 3% -> 3% of each run, Pallas kernels for 24% -> 25%
where the time goes in v4:
time: 57.9 us; the launch traced here: 57.5 us
  waiting for transfers between devices  19.2 us (33%)
  Pallas kernels  17.5 us (30%)
  starting transfers between devices  16.3 us (28%)
  local copies, waits for them, and re-layouts  2.88 us (5%)
  other arithmetic  0.88 us (2%)
  between operations  0.83 us (1%)
    ppermute x10, waiting for transfers between devices, swap(): return lax.ppermute(x, axis, [(i, i ^ k) for i in range(n)])  19.2 us
    ppermute x10, starting transfers between devices, swap(): return lax.ppermute(x, axis, [(i, i ^ k) for i in range(n)])  16.3 us
    pallas_call x10, Pallas kernels, call(): pl.pallas_call(kernel, out_shape=shapes, in_specs=specs, out_specs=[VMEM]...  10.3 us
    pallas_call x2, Pallas kernels, states(): pl.pallas_call(functools.partial(state_kernel, base, sizes), grid=(count,...  4.55 us
    pallas_call x2, Pallas kernels, final(): pl.pallas_call(functools.partial(final_kernel, flip), out_shape=jax.Shape...  2.6 us
    dynamic_slice x2, local copies, waits for them, and re-layouts, away(): lax.dynamic_slice(rows, (jnp.uint32(0), start), (rows.shape[0], count * G...  2.02 us
  transfers between devices with their start and end apart: 10, of which 8 were waited for; matrix products, arithmetic and copies ran while one was open for 3% of the time, Pallas kernels for 25%

profile of v4, /device:TPU:0, one launch (start us, length us, event | category | flops | bytes accessed | tf_op | source)
XLA Modules:
  0.0 57.5 jit_solution(91507720661378211)
XLA Ops:
  0.6 0.0 copy-start.3
  0.6 0.0 copy-start.1
  0.7 1.0 %dynamic-slice_bitcast_fusion.1 = bf16[128,768]{1,0:T(8,128)(2,1)S(1)} fusion(bf16[1,128,4096]{2,1,0:T(8,128)(2,1)} %param.6, u32[]{:T(128)S(6)} %add.31), kind=kLoop, calls=%fused_computation.1 | loop fusion | bytes 393220 | tf_op jit(solution)/shard_map/dynamic_slice | solution.py:571
  1.7 3.1 %collective-permute-start = (bf16[128,768]{1,0:T(8,128)(2,1)S(1)}, bf16[128,768]{1,0:T(8,128)(2,1)S(1)}, u32[]{:S(2)}, u32[]{:S(2)}) collective-permute-start(bf16[128,768]{1,0:T(8,128)(2,1)S(1)} %dynamic-slice_bitcast_fusion.1), channel_id=1, source_target_pairs={{0,1},{1,0},{2,3},{3,2},{4,5},{5,4},{6,7},{7,6},{8,9},{9,8},{10,11... | collective-permute-start | bytes 589832 | tf_op jit(solution)/shard_map/ppermute | solution.py:500
  4.8 1.0 %dynamic-slice_bitcast_fusion = bf16[128,1280]{1,0:T(8,128)(2,1)S(1)} fusion(bf16[1,128,4096]{2,1,0:T(8,128)(2,1)} %param.6, u32[]{:T(128)S(6)} %mul.71), kind=kLoop, calls=%fused_computation | loop fusion | bytes 655364 | tf_op jit(solution)/shard_map/dynamic_slice | solution.py:571
  5.7 0.0 copy-start
  5.8 0.1 collective-permute-start.1
  5.8 0.8 %multiply_add_fusion.code_ref = s32[32,32]{1,0:T(8,128)S(1)} fusion(s32[32,32]{1,0:T(8,128)} %param.10, s32[32,32]{1,0:T(8,128)} %param.9), kind=kLoop, calls=%fused_computation.3 | loop fusion | flops 2048 | bytes 12288 | tf_op jit(solution)/shard_map/add | solution.py:583
  6.7 0.0 copy-start.2
  6.7 0.8 %copy-done.2 = f32[32,4,64]{2,1,0:T(4,128)S(1)} copy-done((f32[32,4,64]{2,1,0:T(4,128)S(1)}, f32[32,4,64]{2,1,0:T(4,128)}, u32[]{:S(2)}) %copy-start.2) | copy-done | bytes 32792
  7.5 1.1 %shard_map.77 = (bf16[8,256,256]{2,1,0:T(8,128)(2,1)S(1)}, bf16[8,256,256]{2,1,0:T(8,128)(2,1)S(1)}, f32[8,2,8,128]{3,2,1,0:T(8,128)S(1)}, f32[2,8,128]{2,1,0:T(8,128)S(1)}) custom-call(s32[32,32]{1,0:T(8,128)S(1)} %multiply_add_fusion.code_ref, f32[128,64]{1,0:T(8,128)S(1)} %bitcast.78), custom_call_target="tpu_custom_call" | custom-call | flops 536870912 | bytes 2207744 | tf_op jit(solution)/shard_map/pallas_call | solution.py:204
  8.6 0.0 copy-done.3
  8.6 0.0 copy-done.1
  8.6 3.0 %shard_map.78 = (f32[256,128]{1,0:T(8,128)S(1)}, f32[5,8,128]{2,1,0:T(8,128)S(1)}, bf16[2048,256]{1,0:T(8,128)(2,1)S(1)}, f32[8,2,256,128]{3,2,1,0:T(8,128)S(1)}, f32[8,64,256]{2,1,0:T(8,128)S(1)}) custom-call(s32[1,256]{1,0:T(1,128)S(1)} %copy-done.3, f32[8,2,8,128]{3,2,1,0:T(8,128)S(1)} %get-tuple-element.33.tab_ref.refs_0_, bf16[256,2048]{1,0:T(8,128)(2,1)S(1)} %bitcast.77), custom_call_target="tpu_custom_call" | custom-call | flops 536870912 | bytes 4936704 | tf_op jit(solution)/shard_map/pallas_call | solution.py:204
  11.6 5.1 %collective-permute-done.1.refs_7_ = bf16[128,1280]{1,0:T(8,128)(2,1)S(1)} collective-permute-done((bf16[128,1280]{1,0:T(8,128)(2,1)S(1)}, bf16[128,1280]{1,0:T(8,128)(2,1)S(1)}, u32[]{:S(2)}, u32[]{:S(2)}) %collective-permute-start.1) | collective-permute-done | bytes 327712 | tf_op jit(solution)/shard_map/ppermute | solution.py:500
  16.7 0.0 copy-done
  16.7 3.3 %shard_map.79 = (f32[5,2,256,128]{3,2,1,0:T(8,128)S(1)}, f32[2,5,128]{2,1,0:T(8,128)S(1)}, f32[5,64,256]{2,1,0:T(8,128)S(1)}) custom-call(f32[8,2,8,128]{3,2,1,0:T(8,128)S(1)} %get-tuple-element.33.tab_ref.refs_0_, f32[5,8,128]{2,1,0:T(8,128)S(1)} %get-tuple-element.34.refs_1_, f32[256,128]{1,0:T(8,128)S(1)} %get-tuple-element.35.refs_2_, s32[1]{0:T(128)} %bitcast.1.refs_3_, ...), custom_call_target="tpu_custom_call" | custom-call | flops 671088640 | bytes 6382596 | tf_op jit(solution)/shard_map/pallas_call | solution.py:204
  20.0 0.0 collective-permute-done.refs_7_
  20.0 1.1 %shard_map.80 = (f32[3,2,256,128]{3,2,1,0:T(8,128)S(1)}, f32[3,2,8,128]{3,2,1,0:T(8,128)S(1)}, f32[24,128]{1,0:T(8,128)S(1)}) custom-call(f32[8,2,8,128]{3,2,1,0:T(8,128)S(1)} %get-tuple-element.33.tab_ref.refs_0_, f32[5,8,128]{2,1,0:T(8,128)S(1)} %get-tuple-element.34.refs_1_, f32[256,128]{1,0:T(8,128)S(1)} %get-tuple-element.35.refs_2_, s32[1]{0:T(128)} %bitcast.1.refs_3_, ...), custom_call_target="tpu_custom_call" | custom-call | flops 201326592 | bytes 4387844 | tf_op jit(solution)/shard_map/pallas_call | solution.py:204
  21.1 1.9 %collective-permute-start.2 = (f32[24,128]{1,0:T(8,128)S(1)}, f32[24,128]{1,0:T(8,128)S(1)}, u32[]{:S(2)}, u32[]{:S(2)}) collective-permute-start(f32[24,128]{1,0:T(8,128)S(1)} %get-tuple-element.41), channel_id=1, source_target_pairs={{0,2},{2,0},{4,6},{6,4},{1,3},{3,1},{5,7},{7,5},{8,10},{10,8},{12,... | collective-permute-start | bytes 36872 | tf_op jit(solution)/shard_map/ppermute | solution.py:500
  23.0 1.9 %collective-permute-done.2 = f32[24,128]{1,0:T(8,128)S(1)} collective-permute-done((f32[24,128]{1,0:T(8,128)S(1)}, f32[24,128]{1,0:T(8,128)S(1)}, u32[]{:S(2)}, u32[]{:S(2)}) %collective-permute-start.2) | collective-permute-done | bytes 12320 | tf_op jit(solution)/shard_map/ppermute | solution.py:500
  24.9 2.9 %collective-permute-start.3 = (f32[24,128]{1,0:T(8,128)S(1)}, f32[24,128]{1,0:T(8,128)S(1)}, u32[]{:S(2)}, u32[]{:S(2)}) collective-permute-start(f32[24,128]{1,0:T(8,128)S(1)} %pad_maximum_fusion), channel_id=1, source_target_pairs={{0,4},{2,6},{4,0},{6,2},{1,5},{3,7},{5,1},{7,3},{8,12},{10,14},{12... | collective-permute-start | bytes 36872 | tf_op jit(solution)/shard_map/ppermute | solution.py:500
  27.8 1.4 %shard_map.81 = (f32[3,2,256,128]{3,2,1,0:T(8,128)S(1)}, f32[3,64,256]{2,1,0:T(8,128)S(1)}) custom-call(f32[8,2,8,128]{3,2,1,0:T(8,128)S(1)} %get-tuple-element.33.tab_ref.refs_0_, f32[5,8,128]{2,1,0:T(8,128)S(1)} %get-tuple-element.34.refs_1_, f32[256,128]{1,0:T(8,128)S(1)} %get-tuple-element.35.refs_2_, ...), custom_call_target="tpu_custom_call" | custom-call | flops 201326592 | bytes 3059712 | tf_op jit(solution)/shard_map/pallas_call | solution.py:204
  29.2 0.4 collective-permute-done.3
  29.6 0.1 shard_map.82
  29.7 0.1 collective-permute-start.4
  29.8 1.5 %collective-permute-done.4.got_ref = f32[256,256]{1,0:T(8,128)S(1)} collective-permute-done((f32[256,256]{1,0:T(8,128)S(1)}, f32[256,256]{1,0:T(8,128)S(1)}, u32[]{:S(2)}, u32[]{:S(2)}) %collective-permute-start.4) | collective-permute-done | bytes 262176 | tf_op jit(solution)/shard_map/ppermute | solution.py:500
  31.3 0.1 shard_map.83
  31.4 1.8 %collective-permute-start.5 = (s16[144,256]{1,0:T(8,128)(2,1)S(1)}, s16[144,256]{1,0:T(8,128)(2,1)S(1)}, u32[]{:S(2)}, u32[]{:S(2)}) collective-permute-start(s16[144,256]{1,0:T(8,128)(2,1)S(1)} %get-tuple-element.57), channel_id=1, source_target_pairs={{0,16},{8,24},{16,0},{24,8},{1,17},{9,25},{17,1},{25,9},{2,18},{10... | collective-permute-start | bytes 221192 | tf_op jit(solution)/shard_map/ppermute | solution.py:500
  33.2 2.6 %collective-permute-done.5.got_ref = s16[144,256]{1,0:T(8,128)(2,1)S(1)} collective-permute-done((s16[144,256]{1,0:T(8,128)(2,1)S(1)}, s16[144,256]{1,0:T(8,128)(2,1)S(1)}, u32[]{:S(2)}, u32[]{:S(2)}) %collective-permute-start.5) | collective-permute-done | bytes 73760 | tf_op jit(solution)/shard_map/ppermute | solution.py:500
  35.8 0.1 shard_map.84.own_ref
  35.9 1.9 %collective-permute-start.6 = (s16[144,256]{1,0:T(8,128)(2,1)S(1)}, s16[144,256]{1,0:T(8,128)(2,1)S(1)}, u32[]{:S(2)}, u32[]{:S(2)}) collective-permute-start(s16[144,256]{1,0:T(8,128)(2,1)S(1)} %shard_map.84.own_ref), channel_id=1, source_target_pairs={{0,2},{2,0},{4,6},{6,4},{1,3},{3,1},{5,7},{7,5},{8,10},{10,8},{12,... | collective-permute-start | bytes 221192 | tf_op jit(solution)/shard_map/ppermute | solution.py:500
  37.8 2.6 %collective-permute-done.6.got_ref = s16[144,256]{1,0:T(8,128)(2,1)S(1)} collective-permute-done((s16[144,256]{1,0:T(8,128)(2,1)S(1)}, s16[144,256]{1,0:T(8,128)(2,1)S(1)}, u32[]{:S(2)}, u32[]{:S(2)}) %collective-permute-start.6) | collective-permute-done | bytes 73760 | tf_op jit(solution)/shard_map/ppermute | solution.py:500
  40.3 0.1 shard_map.85.own_ref
  40.4 2.9 %collective-permute-start.7 = (s16[144,256]{1,0:T(8,128)(2,1)S(1)}, s16[144,256]{1,0:T(8,128)(2,1)S(1)}, u32[]{:S(2)}, u32[]{:S(2)}) collective-permute-start(s16[144,256]{1,0:T(8,128)(2,1)S(1)} %shard_map.85.own_ref), channel_id=1, source_target_pairs={{0,4},{2,6},{4,0},{6,2},{1,5},{3,7},{5,1},{7,3},{8,12},{10,14},{12... | collective-permute-start | bytes 221192 | tf_op jit(solution)/shard_map/ppermute | solution.py:500
  43.3 2.4 %collective-permute-done.7.got_ref = s16[144,256]{1,0:T(8,128)(2,1)S(1)} collective-permute-done((s16[144,256]{1,0:T(8,128)(2,1)S(1)}, s16[144,256]{1,0:T(8,128)(2,1)S(1)}, u32[]{:S(2)}, u32[]{:S(2)}) %collective-permute-start.7) | collective-permute-done | bytes 73760 | tf_op jit(solution)/shard_map/ppermute | solution.py:500
  45.7 0.1 shard_map.86
  45.8 1.8 %collective-permute-start.8 = (s16[144,256]{1,0:T(8,128)(2,1)S(1)}, s16[144,256]{1,0:T(8,128)(2,1)S(1)}, u32[]{:S(2)}, u32[]{:S(2)}) collective-permute-start(s16[144,256]{1,0:T(8,128)(2,1)S(1)} %shard_map.86), channel_id=1, source_target_pairs={{0,16},{8,24},{16,0},{24,8},{1,17},{9,25},{17,1},{25,9},{2,18},{10... | collective-permute-start | bytes 221192 | tf_op jit(solution)/shard_map/ppermute | solution.py:500
  47.6 2.6 %collective-permute-done.8 = s16[144,256]{1,0:T(8,128)(2,1)S(1)} collective-permute-done((s16[144,256]{1,0:T(8,128)(2,1)S(1)}, s16[144,256]{1,0:T(8,128)(2,1)S(1)}, u32[]{:S(2)}, u32[]{:S(2)}) %collective-permute-start.8) | collective-permute-done | bytes 73760 | tf_op jit(solution)/shard_map/ppermute | solution.py:500
  50.3 0.1 collective-permute-start.9
  50.4 2.3 %states.2.refs_2_ = bf16[256,2048]{1,0:T(8,128)(2,1)} custom-call(f32[2,8,128]{2,1,0:T(8,128)S(1)} %pad_maximum_fusion.1.entry_ref, f32[8,2,256,128]{3,2,1,0:T(8,128)S(1)} %get-tuple-element.43.decay_ref, bf16[8,256,256]{2,1,0:T(8,128)(2,1)S(1)} %get-tuple-element.37.refs_5_.high_ref, bf16[8,256,256]{2,1,0:T(8,128)(2,1)S(1)} %get-tuple-element.38.refs_6_.low_ref, ...), custom_call_target="tpu_custom_call" | custom-call | flops 402653184 | bytes 3600000 | tf_op jit(solution)/shard_map/states/pallas_call | solution.py:400
  52.7 2.3 %states.3 = bf16[256,2048]{1,0:T(8,128)(2,1)} custom-call(f32[2,8,128]{2,1,0:T(8,128)S(1)} %pad_maximum_fusion.1.entry_ref, f32[8,2,256,128]{3,2,1,0:T(8,128)S(1)} %get-tuple-element.43.decay_ref, bf16[8,256,256]{2,1,0:T(8,128)(2,1)S(1)} %get-tuple-element.37.refs_5_.high_ref, ...), custom_call_target="tpu_custom_call", output_to_operand_aliasing={{}: (6, {})} | custom-call | flops 402653184 | bytes 3600000 | tf_op jit(solution)/shard_map/states/pallas_call | solution.py:400
  54.9 1.3 %final.2.refs_0_ = f32[32,64,64]{2,1,0:T(8,128)} custom-call(s32[1]{0:T(128)} %bitcast.side_ref, s16[288,256]{1,0:T(8,128)(2,1)S(1)} %add_select_fusion.x_ref, bf16[8,256,256]{2,1,0:T(8,128)(2,1)S(1)} %get-tuple-element.37.refs_5_.high_ref, bf16[8,256,256]{2,1,0:T(8,128)(2,1)S(1)} %get-tuple-element.38.refs_6_.low_ref), custom_call_target="tpu_custom_call" | custom-call | flops 100663296 | bytes 1600000 | tf_op jit(solution)/shard_map/final/pallas_call | solution.py:485
  56.2 0.0 collective-permute-done.9.x_ref
  56.2 1.3 %final.3 = f32[32,64,64]{2,1,0:T(8,128)} custom-call(s32[1]{0:T(128)} %bitcast.side_ref, s16[288,256]{1,0:T(8,128)(2,1)S(1)} %collective-permute-done.9.x_ref, bf16[8,256,256]{2,1,0:T(8,128)(2,1)S(1)} %get-tuple-element.37.refs_5_.high_ref, bf16[8,256,256]{2,1,0:T(8,128)(2,1)S(1)} %get-tuple-element.38.refs_6_.low_ref, ...), custom_call_target="tpu_custom_call", output_to_operand_aliasing={{}: (4, {})} | custom-call | flops 100663296 | bytes 1600000 | tf_op jit(solution)/shard_map/final/pallas_call | solution.py:485
  (7 shorter events, 0.1 us)
Async XLA Ops:
  0.6 7.9 %copy-start.3 = (s32[1,256]{1,0:T(1,128)S(1)}, s32[1,256]{1,0:T(1,128)}, u32[]{:S(2)}) copy-start(s32[1,256]{1,0:T(1,128)} %boundary_ref.1) | copy-start | bytes 3076
  0.6 7.9 %copy-start.1 = (bf16[1,256,2048]{2,1,0:T(8,128)(2,1)S(1)}, bf16[1,256,2048]{2,1,0:T(8,128)(2,1)}, u32[]{:S(2)}) copy-start(bf16[1,256,2048]{2,1,0:T(8,128)(2,1)} %param.7) | copy-start | bytes 3145732
  1.7 18.3 %collective-permute-start = (bf16[128,768]{1,0:T(8,128)(2,1)S(1)}, bf16[128,768]{1,0:T(8,128)(2,1)S(1)}, u32[]{:S(2)}, u32[]{:S(2)}) collective-permute-start(bf16[128,768]{1,0:T(8,128)(2,1)S(1)} %dynamic-slice_bitcast_fusion.1), channel_id=1, source_target_pairs={{0,1},{1,0},{2,3},{3,2},{4,5},{5,4},{6,7},{7,6},{8,9},{9,8},{10,11... | collective-permute-start | bytes 589832 | tf_op jit(solution)/shard_map/ppermute | solution.py:500
  5.7 10.9 %copy-start = (bf16[1,128,4096]{2,1,0:T(8,128)(2,1)S(1)}, bf16[1,128,4096]{2,1,0:T(8,128)(2,1)}, u32[]{:S(2)}) copy-start(bf16[1,128,4096]{2,1,0:T(8,128)(2,1)} %param.6) | copy-start | bytes 3145732
  5.8 10.9 %collective-permute-start.1 = (bf16[128,1280]{1,0:T(8,128)(2,1)S(1)}, bf16[128,1280]{1,0:T(8,128)(2,1)S(1)}, u32[]{:S(2)}, u32[]{:S(2)}) collective-permute-start(bf16[128,1280]{1,0:T(8,128)(2,1)S(1)} %dynamic-slice_bitcast_fusion), channel_id=1, source_target_pairs={{0,1},{1,0},{2,3},{3,2},{4,5},{5,4},{6,7},{7,6},{8,9},{9,8},{10,11... | collective-permute-start | bytes 983048 | tf_op jit(solution)/shard_map/ppermute | solution.py:500
  6.7 0.8 %copy-start.2 = (f32[32,4,64]{2,1,0:T(4,128)S(1)}, f32[32,4,64]{2,1,0:T(4,128)}, u32[]{:S(2)}) copy-start(f32[32,4,64]{2,1,0:T(4,128)} %param.11) | copy-start | bytes 98308
  21.1 3.8 %collective-permute-start.2 = (f32[24,128]{1,0:T(8,128)S(1)}, f32[24,128]{1,0:T(8,128)S(1)}, u32[]{:S(2)}, u32[]{:S(2)}) collective-permute-start(f32[24,128]{1,0:T(8,128)S(1)} %get-tuple-element.41), channel_id=1, source_target_pairs={{0,2},{2,0},{4,6},{6,4},{1,3},{3,1},{5,7},{7,5},{8,10},{10,8},{12,... | collective-permute-start | bytes 36872 | tf_op jit(solution)/shard_map/ppermute | solution.py:500
  24.9 4.7 %collective-permute-start.3 = (f32[24,128]{1,0:T(8,128)S(1)}, f32[24,128]{1,0:T(8,128)S(1)}, u32[]{:S(2)}, u32[]{:S(2)}) collective-permute-start(f32[24,128]{1,0:T(8,128)S(1)} %pad_maximum_fusion), channel_id=1, source_target_pairs={{0,4},{2,6},{4,0},{6,2},{1,5},{3,7},{5,1},{7,3},{8,12},{10,14},{12... | collective-permute-start | bytes 36872 | tf_op jit(solution)/shard_map/ppermute | solution.py:500
  29.7 1.6 %collective-permute-start.4 = (f32[256,256]{1,0:T(8,128)S(1)}, f32[256,256]{1,0:T(8,128)S(1)}, u32[]{:S(2)}, u32[]{:S(2)}) collective-permute-start(f32[256,256]{1,0:T(8,128)S(1)} %get-tuple-element.55), channel_id=1, source_target_pairs={{0,8},{8,0},{16,24},{24,16},{1,9},{9,1},{17,25},{25,17},{2,10},{10... | collective-permute-start | bytes 786440 | tf_op jit(solution)/shard_map/ppermute | solution.py:500
  31.4 4.4 %collective-permute-start.5 = (s16[144,256]{1,0:T(8,128)(2,1)S(1)}, s16[144,256]{1,0:T(8,128)(2,1)S(1)}, u32[]{:S(2)}, u32[]{:S(2)}) collective-permute-start(s16[144,256]{1,0:T(8,128)(2,1)S(1)} %get-tuple-element.57), channel_id=1, source_target_pairs={{0,16},{8,24},{16,0},{24,8},{1,17},{9,25},{17,1},{25,9},{2,18},{10... | collective-permute-start | bytes 221192 | tf_op jit(solution)/shard_map/ppermute | solution.py:500
  35.9 4.4 %collective-permute-start.6 = (s16[144,256]{1,0:T(8,128)(2,1)S(1)}, s16[144,256]{1,0:T(8,128)(2,1)S(1)}, u32[]{:S(2)}, u32[]{:S(2)}) collective-permute-start(s16[144,256]{1,0:T(8,128)(2,1)S(1)} %shard_map.84.own_ref), channel_id=1, source_target_pairs={{0,2},{2,0},{4,6},{6,4},{1,3},{3,1},{5,7},{7,5},{8,10},{10,8},{12,... | collective-permute-start | bytes 221192 | tf_op jit(solution)/shard_map/ppermute | solution.py:500
  40.4 5.3 %collective-permute-start.7 = (s16[144,256]{1,0:T(8,128)(2,1)S(1)}, s16[144,256]{1,0:T(8,128)(2,1)S(1)}, u32[]{:S(2)}, u32[]{:S(2)}) collective-permute-start(s16[144,256]{1,0:T(8,128)(2,1)S(1)} %shard_map.85.own_ref), channel_id=1, source_target_pairs={{0,4},{2,6},{4,0},{6,2},{1,5},{3,7},{5,1},{7,3},{8,12},{10,14},{12... | collective-permute-start | bytes 221192 | tf_op jit(solution)/shard_map/ppermute | solution.py:500
  45.8 4.4 %collective-permute-start.8 = (s16[144,256]{1,0:T(8,128)(2,1)S(1)}, s16[144,256]{1,0:T(8,128)(2,1)S(1)}, u32[]{:S(2)}, u32[]{:S(2)}) collective-permute-start(s16[144,256]{1,0:T(8,128)(2,1)S(1)} %shard_map.86), channel_id=1, source_target_pairs={{0,16},{8,24},{16,0},{24,8},{1,17},{9,25},{17,1},{25,9},{2,18},{10... | collective-permute-start | bytes 221192 | tf_op jit(solution)/shard_map/ppermute | solution.py:500
  50.3 5.9 %collective-permute-start.9 = (s16[288,256]{1,0:T(8,128)(2,1)S(1)}, s16[288,256]{1,0:T(8,128)(2,1)S(1)}, u32[]{:S(2)}, u32[]{:S(2)}) collective-permute-start(s16[288,256]{1,0:T(8,128)(2,1)S(1)} %add_select_fusion.x_ref), channel_id=1, source_target_pairs={{0,8},{8,0},{16,24},{24,16},{1,9},{9,1},{17,25},{25,17},{2,10},{10... | collective-permute-start | bytes 442376 | tf_op jit(solution)/shard_map/ppermute | solution.py:500

commit v5 on v4

--- a/solution.py
+++ b/solution.py
@@ -343,26 +343,6 @@
                 (tab, ktab, keep, turned, spaced, head), [VMEM] * 6, (), count * 2 * 2 * 256**3)
 
 
-def merge_kernel(half, side_ref, entry_ref, weight_ref, *refs):
-    parts, (own_ref, away_ref) = refs[:-2], refs[-2:]
-    blocks = [part.at[n] for part in parts for n in range(part.shape[0])]
-    side = side_ref[0]
-    for n in range(half):
-        for out_ref, which in ((own_ref, side), (away_ref, 1 - side)):
-            here = jnp.where(which == 0, blocks[n][...], blocks[half + n][...])
-            at = which * half + n
-            re, im = entry_ref[0, pl.ds(at, 1), :], entry_ref[1, pl.ds(at, 1), :]
-            weight = weight_ref[at]
-            w_re, w_im = weight[:, :LANES], weight[:, LANES:]
-            out_ref[n * SIZE : (n + 1) * SIZE, :LANES] = here[:, :LANES] + (re * w_re - im * w_im)
-            out_ref[n * SIZE : (n + 1) * SIZE, LANES:] = here[:, LANES:] + (re * w_im + im * w_re)
-
-
-def merge(half, side, entry, weight, parts):
-    return call(functools.partial(merge_kernel, half), [((half * SIZE, GROUP), F32)] * 2,
-                (side, entry, weight, *parts), [SMEM] + [VMEM] * (2 + len(parts)))
-
-
 def state_kernel(base, sizes, entry_ref, decay_ref, high_ref, low_ref, *refs):
     parts, out_ref = refs[: len(sizes)], refs[-1]
     g = pl.program_id(0) + base
@@ -430,38 +410,57 @@
     return code_ref[start : start + rows, :].astype(jnp.int32).astype(F32) * (jnp.exp2(power) * (1.0 / STEPS))
 
 
-def halve_kernel(bit_ref, own_ref, got_ref, here_ref, code_ref):
-    rows = here_ref.shape[0]
-    bit = bit_ref[0]
+def merge_kernel(half, side_ref, bit_ref, entry_ref, weight_ref, *refs):
+    parts, outs, (own_ref, away_ref) = refs[:-6], refs[-6:-2], refs[-2:]
+    blocks = [part.at[n] for part in parts for n in range(part.shape[0])]
+    side, bit = side_ref[0], bit_ref[0]
+    for n in range(half):
+        for out_ref, which in ((own_ref, side), (away_ref, 1 - side)):
+            here = jnp.where(which == 0, blocks[n][...], blocks[half + n][...])
+            at = which * half + n
+            re, im = entry_ref[0, pl.ds(at, 1), :], entry_ref[1, pl.ds(at, 1), :]
+            weight = weight_ref[at]
+            w_re, w_im = weight[:, :LANES], weight[:, LANES:]
+            out_ref[n * SIZE : (n + 1) * SIZE, :LANES] = here[:, :LANES] + (re * w_re - im * w_im)
+            out_ref[n * SIZE : (n + 1) * SIZE, LANES:] = here[:, LANES:] + (re * w_im + im * w_re)
+    rows = half * SIZE // 2
     here, there = (pl.ds(pl.multiple_of(n * rows, rows), rows) for n in (bit, 1 - bit))
-    here_ref[...] = own_ref[here, :] + got_ref[here, :]
-    encode(own_ref[there, :] + got_ref[there, :], code_ref)
-
-
-def halve(bit, own, got):
-    rows, width = own.shape[0] // 2, own.shape[1]
-    out = [((rows, width), F32), ((rows + EXTRA, width), jnp.dtype(jnp.int16))]
-    return call(halve_kernel, out, (bit, own, got), [SMEM, VMEM, VMEM])
-
-
-def add_kernel(own_ref, got_ref, code_ref):
-    own = own_ref[...] if own_ref.dtype == F32 else decode(own_ref)
-    encode(own + decode(got_ref), code_ref)
-
-
-def add(own, got):
-    return call(add_kernel, [(got.shape, got.dtype)], (own, got), [VMEM, VMEM])[0]
-
-
-def final_kernel(flip, side_ref, x_ref, high_ref, low_ref, *refs):
+    outs[0][...] = own_ref[here, :]
+    outs[1][...] = own_ref[there, :]
+    encode(away_ref[here, :], outs[2])
+    encode(away_ref[there, :], outs[3])
+
+
+def merge(half, side, bit, entry, weight, parts):
+    rows = half * SIZE // 2
+    out = [((rows, GROUP), F32)] * 2 + [((rows + EXTRA, GROUP), jnp.dtype(jnp.int16))] * 2
+    return call(functools.partial(merge_kernel, half), out, (side, bit, entry, weight, *parts),
+                [SMEM] * 2 + [VMEM] * (2 + len(parts)), [pltpu.VMEM((half * SIZE, GROUP), F32)] * 2)
+
+
+def add_kernel(*refs):
+    total = None
+    for ref in refs[:-1]:
+        term = ref[...] if ref.dtype == F32 else decode(ref)
+        total = term if total is None else total + term
+    encode(total, refs[-1])
+
+
+def add(*terms):
+    return call(add_kernel, [(terms[-1].shape, terms[-1].dtype)], terms, [VMEM] * len(terms))[0]
+
+
+def final_kernel(flips, quarters, side_ref, bit_ref, x_ref, high_ref, low_ref, *refs):
     out_hbm, out_ref, sems = refs[-3:]
     half = high_ref.shape[0] // 2
-    which = 1 - side_ref[0] if flip else side_ref[0]
+    count = half * quarters // 2
+    side, bit = (1 - ref[0] if flip else ref[0] for ref, flip in zip((side_ref, bit_ref), flips))
+    start = side * half + bit * count if quarters == 1 else side * half
+    rows = x_ref.shape[0] // quarters - EXTRA
+    x = jnp.concatenate([decode(x_ref, n * (rows + EXTRA), rows) for n in range(quarters)], axis=0)
     copies = []
-    rows = x_ref.shape[0] // 2 - EXTRA
-    x = jnp.concatenate([decode(x_ref, n * (rows + EXTRA), rows) for n in range(2)], axis=0)
-    for n in range(half):
-        at = which * half + n
+    for n in range(count):
+        at = start + n
         x_high, x_low = split(x[n * SIZE : (n + 1) * SIZE, :])
         out = matmul(high_ref[at], x_high, NT) + matmul(low_ref[at], x_high, NT) + matmul(high_ref[at], x_low, NT)
         for j in range(4):
@@ -472,26 +471,26 @@
         copy.wait()
 
 
-def final(flip, side, x, high, low, filled=None):
-    half = high.shape[0] // 2
+def final(flips, quarters, side, bit, x, high, low, filled=None):
+    count = high.shape[0] // 2 * quarters // 2
     blocks = high.shape[0] * 4
-    args = [side, x, high, low]
-    specs = [SMEM] + [VMEM] * 3
+    args = [side, bit, x, high, low]
+    specs = [SMEM] * 2 + [VMEM] * 3
     alias = {}
     if filled is not None:
         alias = {len(args): 0}
         args.append(filled)
         specs.append(HBM)
     return pl.pallas_call(
-        functools.partial(final_kernel, flip),
+        functools.partial(final_kernel, flips, quarters),
         out_shape=jax.ShapeDtypeStruct((blocks, SIZE, SIZE), F32),
         in_specs=specs,
         out_specs=HBM,
-        scratch_shapes=[pltpu.VMEM((4 * half, SIZE, SIZE), F32), pltpu.SemaphoreType.DMA((half,))],
+        scratch_shapes=[pltpu.VMEM((4 * count, SIZE, SIZE), F32), pltpu.SemaphoreType.DMA((count,))],
         input_output_aliases=alias,
         name="final",
         compiler_params=pltpu.CompilerParams(vmem_limit_bytes=LIMIT),
-        cost_estimate=pl.CostEstimate(flops=half * 3 * 2 * 256 * 256 * 64, bytes_accessed=half * 400_000, transcendentals=0),
+        cost_estimate=pl.CostEstimate(flops=count * 3 * 2 * 256 * 256 * 64, bytes_accessed=count * 400_000, transcendentals=0),
     )(*args)
 
 
@@ -542,16 +541,32 @@
     return [(lax.axis_index(axis).astype(jnp.uint32) // jnp.uint32(k)) & jnp.uint32(1) for axis, k in steps]
 
 
-def total_sum(own, away, steps, bit, lower):
-    got = swap(away, *steps[0])
-    here, code = halve(bit, own, got)
+def total_sum(quarters, steps):
+    own_here, own_there, away_here, away_there = quarters
+    got = swap(away_there, *steps[0])
+    code = add(own_there, got)
+    near = swap(away_here, *steps[0])
     got = swap(code, *steps[1])
-    code = add(here, got)
+    code = add(own_here, near, got)
     for step in steps[2:]:
         got = swap(code, *step)
         code = add(code, got)
+    return code
+
+
+def spread(code, steps, side, bit, lower, high, low):
     other = swap(code, *steps[1])
-    return jnp.where(lower, jnp.concatenate([code, other]), jnp.concatenate([other, code]))
+    if high.shape[0] % 4:
+        both = jnp.where(lower, jnp.concatenate([code, other]), jnp.concatenate([other, code]))
+        away = swap(both, *steps[0])
+        out = final((False, False), 2, side, bit, both, high, low)
+        return final((True, False), 2, side, bit, away, high, low, out)
+    near = swap(code, *steps[0])
+    out = final((False, False), 1, side, bit, code, high, low)
+    out = final((True, False), 1, side, bit, near, high, low, out)
+    far = swap(other, *steps[0])
+    out = final((False, True), 1, side, bit, other, high, low, out)
+    return final((True, True), 1, side, bit, far, high, low, out)
 
 
 def inner(out_grad, prev_state, boundary, angle_code, radius_code, reflect):
@@ -591,15 +606,21 @@
     spaced, head, sent = scan_first(base, count, place, rows, parts[-1], high, low, tab, ktab, keep, [d[1] for d in done])
     entry = entering(sent, (far[0], far[1]), "ctx", early)
     z_last, grad_last = scan_second(base, count, spaced, head, tab, ktab, keep, turned)
-    own, other = merge(half, side, entry, weight, [d[2] for d in done] + [grad_last])
+    quarters = merge(half, side, bit, entry, weight, [d[2] for d in done] + [grad_last])
     z = [d[0] for d in done] + [z_last]
-    grad_input = states(0, half, z, decay, entry, high, low)
-    grad_input = states(half, groups - half, z, decay, entry, high, low, grad_input)
-    own = total_sum(own, other, steps, bit, lower)
-    other = swap(own, *steps[0])
-    grad_transition = final(False, side, own, high, low)
-    grad_transition = final(True, side, other, high, low, grad_transition)
+    grad_input = None
+    for base, count in shares(groups):
+        if count:
+            grad_input = states(base, count, z, decay, entry, high, low, grad_input)
+    grad_transition = spread(total_sum(quarters, steps), steps, side, bit, lower, high, low)
     return grad_input[None], grad_transition
+
+
+def shares(groups):
+    counts = [groups // 4]
+    counts.append((groups - counts[0] + 1) // 2)
+    counts.append(groups - sum(counts))
+    return [(sum(counts[:n]), count) for n, count in enumerate(counts)]
 
 
 def solution(mesh):

time: 57.9 us -> 60 us (1.036)
  Pallas kernels: 17.5 us -> 19.9 us
  waiting for transfers between devices: 19.2 us -> 18.4 us
    pallas_call x2 -> x4, Pallas kernels: 2.6 us -> 4.32 us  [final(): pl.pallas_call(functools.partial(final_kernel, flips, quarters), out_shap...]
    ppermute x10 -> x12, waiting for transfers between devices: 19.2 us -> 18.4 us  [swap(): return lax.ppermute(x, axis, [(i, i ^ k) for i in range(n)])]
    pallas_call x2 -> x3, Pallas kernels: 4.55 us -> 5.16 us  [states(): pl.pallas_call(functools.partial(state_kernel, base, sizes), grid=(count,...]
    ppermute x10 -> x12, starting transfers between devices: 16.3 us -> 16.7 us  [swap(): return lax.ppermute(x, axis, [(i, i ^ k) for i in range(n)])]
  transfers between devices with their start and end apart: 10 -> 12, of which waited for: 8 -> 8; matrix products, arithmetic and copies ran while one was open for 3% -> 3% of each run, Pallas kernels for 25% -> 29%
where the time goes in v5:
time: 60 us; the launch traced here: 59.6 us
  Pallas kernels  19.9 us (33%)
  waiting for transfers between devices  18.4 us (31%)
  starting transfers between devices  16.7 us (28%)
  local copies, waits for them, and re-layouts  2.88 us (5%)
  between operations  0.85 us (1%)
  other arithmetic  0.84 us (1%)
    ppermute x12, waiting for transfers between devices, swap(): return lax.ppermute(x, axis, [(i, i ^ k) for i in range(n)])  18.4 us
    ppermute x12, starting transfers between devices, swap(): return lax.ppermute(x, axis, [(i, i ^ k) for i in range(n)])  16.7 us
    pallas_call x10, Pallas kernels, call(): pl.pallas_call(kernel, out_shape=shapes, in_specs=specs, out_specs=[VMEM]...  10.4 us
    pallas_call x3, Pallas kernels, states(): pl.pallas_call(functools.partial(state_kernel, base, sizes), grid=(count,...  5.16 us
    pallas_call x4, Pallas kernels, final(): pl.pallas_call(functools.partial(final_kernel, flips, quarters), out_shap...  4.32 us
    dynamic_slice x2, local copies, waits for them, and re-layouts, away(): lax.dynamic_slice(rows, (jnp.uint32(0), start), (rows.shape[0], count * G...  2.02 us
  transfers between devices with their start and end apart: 12, of which 8 were waited for; matrix products, arithmetic and copies ran while one was open for 3% of the time, Pallas kernels for 29%

profile of v5, /device:TPU:0, one launch (start us, length us, event | category | flops | bytes accessed | tf_op | source)
XLA Modules:
  0.0 59.6 jit_solution(13913934829275718094)
XLA Ops:
  0.6 0.0 copy-start.3
  0.6 0.0 copy-start.1
  0.7 1.0 %dynamic-slice_bitcast_fusion.1 = bf16[128,768]{1,0:T(8,128)(2,1)S(1)} fusion(bf16[1,128,4096]{2,1,0:T(8,128)(2,1)} %param.6, u32[]{:T(128)S(6)} %add.31), kind=kLoop, calls=%fused_computation.1 | loop fusion | bytes 393220 | tf_op jit(solution)/shard_map/dynamic_slice | solution.py:586
  1.7 3.1 %collective-permute-start = (bf16[128,768]{1,0:T(8,128)(2,1)S(1)}, bf16[128,768]{1,0:T(8,128)(2,1)S(1)}, u32[]{:S(2)}, u32[]{:S(2)}) collective-permute-start(bf16[128,768]{1,0:T(8,128)(2,1)S(1)} %dynamic-slice_bitcast_fusion.1), channel_id=1, source_target_pairs={{0,1},{1,0},{2,3},{3,2},{4,5},{5,4},{6,7},{7,6},{8,9},{9,8},{10,11... | collective-permute-start | bytes 589832 | tf_op jit(solution)/shard_map/ppermute | solution.py:499
  4.8 1.0 %dynamic-slice_bitcast_fusion = bf16[128,1280]{1,0:T(8,128)(2,1)S(1)} fusion(bf16[1,128,4096]{2,1,0:T(8,128)(2,1)} %param.6, u32[]{:T(128)S(6)} %mul.71), kind=kLoop, calls=%fused_computation | loop fusion | bytes 655364 | tf_op jit(solution)/shard_map/dynamic_slice | solution.py:586
  5.7 0.0 copy-start
  5.8 0.1 collective-permute-start.1
  5.8 0.8 %multiply_add_fusion.code_ref = s32[32,32]{1,0:T(8,128)S(1)} fusion(s32[32,32]{1,0:T(8,128)} %param.10, s32[32,32]{1,0:T(8,128)} %param.9), kind=kLoop, calls=%fused_computation.2 | loop fusion | flops 2048 | bytes 12288 | tf_op jit(solution)/shard_map/add | solution.py:598
  6.7 0.0 copy-start.2
  6.7 0.8 %copy-done.2 = f32[32,4,64]{2,1,0:T(4,128)S(1)} copy-done((f32[32,4,64]{2,1,0:T(4,128)S(1)}, f32[32,4,64]{2,1,0:T(4,128)}, u32[]{:S(2)}) %copy-start.2) | copy-done | bytes 32792
  7.5 1.1 %shard_map.77 = (bf16[8,256,256]{2,1,0:T(8,128)(2,1)S(1)}, bf16[8,256,256]{2,1,0:T(8,128)(2,1)S(1)}, f32[8,2,8,128]{3,2,1,0:T(8,128)S(1)}, f32[2,8,128]{2,1,0:T(8,128)S(1)}) custom-call(s32[32,32]{1,0:T(8,128)S(1)} %multiply_add_fusion.code_ref, f32[128,64]{1,0:T(8,128)S(1)} %bitcast.78), custom_call_target="tpu_custom_call" | custom-call | flops 536870912 | bytes 2207744 | tf_op jit(solution)/shard_map/pallas_call | solution.py:204
  8.6 0.0 copy-done.3
  8.6 0.0 copy-done.1
  8.6 3.0 %shard_map.78 = (f32[256,128]{1,0:T(8,128)S(1)}, f32[5,8,128]{2,1,0:T(8,128)S(1)}, bf16[2048,256]{1,0:T(8,128)(2,1)S(1)}, f32[8,2,256,128]{3,2,1,0:T(8,128)S(1)}, f32[8,64,256]{2,1,0:T(8,128)S(1)}) custom-call(s32[1,256]{1,0:T(1,128)S(1)} %copy-done.3, f32[8,2,8,128]{3,2,1,0:T(8,128)S(1)} %get-tuple-element.32.tab_ref.refs_0_, bf16[256,2048]{1,0:T(8,128)(2,1)S(1)} %bitcast.77), custom_call_target="tpu_custom_call" | custom-call | flops 536870912 | bytes 4936704 | tf_op jit(solution)/shard_map/pallas_call | solution.py:204
  11.6 5.1 %collective-permute-done.1.refs_7_ = bf16[128,1280]{1,0:T(8,128)(2,1)S(1)} collective-permute-done((bf16[128,1280]{1,0:T(8,128)(2,1)S(1)}, bf16[128,1280]{1,0:T(8,128)(2,1)S(1)}, u32[]{:S(2)}, u32[]{:S(2)}) %collective-permute-start.1) | collective-permute-done | bytes 327712 | tf_op jit(solution)/shard_map/ppermute | solution.py:499
  16.7 0.0 copy-done
  16.7 3.3 %shard_map.79 = (f32[5,2,256,128]{3,2,1,0:T(8,128)S(1)}, f32[2,5,128]{2,1,0:T(8,128)S(1)}, f32[5,64,256]{2,1,0:T(8,128)S(1)}) custom-call(f32[8,2,8,128]{3,2,1,0:T(8,128)S(1)} %get-tuple-element.32.tab_ref.refs_0_, f32[5,8,128]{2,1,0:T(8,128)S(1)} %get-tuple-element.33.refs_1_, f32[256,128]{1,0:T(8,128)S(1)} %get-tuple-element.34.refs_2_, s32[1]{0:T(128)} %bitcast.1.refs_3_, ...), custom_call_target="tpu_custom_call" | custom-call | flops 671088640 | bytes 6382596 | tf_op jit(solution)/shard_map/pallas_call | solution.py:204
  20.0 0.0 collective-permute-done.refs_7_
  20.0 1.1 %shard_map.80 = (f32[3,2,256,128]{3,2,1,0:T(8,128)S(1)}, f32[3,2,8,128]{3,2,1,0:T(8,128)S(1)}, f32[24,128]{1,0:T(8,128)S(1)}) custom-call(f32[8,2,8,128]{3,2,1,0:T(8,128)S(1)} %get-tuple-element.32.tab_ref.refs_0_, f32[5,8,128]{2,1,0:T(8,128)S(1)} %get-tuple-element.33.refs_1_, f32[256,128]{1,0:T(8,128)S(1)} %get-tuple-element.34.refs_2_, s32[1]{0:T(128)} %bitcast.1.refs_3_, ...), custom_call_target="tpu_custom_call" | custom-call | flops 201326592 | bytes 4387844 | tf_op jit(solution)/shard_map/pallas_call | solution.py:204
  21.1 1.9 %collective-permute-start.2 = (f32[24,128]{1,0:T(8,128)S(1)}, f32[24,128]{1,0:T(8,128)S(1)}, u32[]{:S(2)}, u32[]{:S(2)}) collective-permute-start(f32[24,128]{1,0:T(8,128)S(1)} %get-tuple-element.40), channel_id=1, source_target_pairs={{0,2},{2,0},{4,6},{6,4},{1,3},{3,1},{5,7},{7,5},{8,10},{10,8},{12,... | collective-permute-start | bytes 36872 | tf_op jit(solution)/shard_map/ppermute | solution.py:499
  23.0 1.9 %collective-permute-done.2 = f32[24,128]{1,0:T(8,128)S(1)} collective-permute-done((f32[24,128]{1,0:T(8,128)S(1)}, f32[24,128]{1,0:T(8,128)S(1)}, u32[]{:S(2)}, u32[]{:S(2)}) %collective-permute-start.2) | collective-permute-done | bytes 12320 | tf_op jit(solution)/shard_map/ppermute | solution.py:499
  24.9 2.9 %collective-permute-start.3 = (f32[24,128]{1,0:T(8,128)S(1)}, f32[24,128]{1,0:T(8,128)S(1)}, u32[]{:S(2)}, u32[]{:S(2)}) collective-permute-start(f32[24,128]{1,0:T(8,128)S(1)} %pad_maximum_fusion), channel_id=1, source_target_pairs={{0,4},{2,6},{4,0},{6,2},{1,5},{3,7},{5,1},{7,3},{8,12},{10,14},{12... | collective-permute-start | bytes 36872 | tf_op jit(solution)/shard_map/ppermute | solution.py:499
  27.8 1.4 %shard_map.81 = (f32[3,2,256,128]{3,2,1,0:T(8,128)S(1)}, f32[3,64,256]{2,1,0:T(8,128)S(1)}) custom-call(f32[8,2,8,128]{3,2,1,0:T(8,128)S(1)} %get-tuple-element.32.tab_ref.refs_0_, f32[5,8,128]{2,1,0:T(8,128)S(1)} %get-tuple-element.33.refs_1_, f32[256,128]{1,0:T(8,128)S(1)} %get-tuple-element.34.refs_2_, ...), custom_call_target="tpu_custom_call" | custom-call | flops 201326592 | bytes 3059712 | tf_op jit(solution)/shard_map/pallas_call | solution.py:204
  29.2 0.4 collective-permute-done.3
  29.6 0.2 shard_map.82
  29.9 0.1 collective-permute-start.5
  29.9 0.5 collective-permute-start.4
  30.4 0.8 %collective-permute-done.5.refs_1_ = s16[144,256]{1,0:T(8,128)(2,1)S(1)} collective-permute-done((s16[144,256]{1,0:T(8,128)(2,1)S(1)}, s16[144,256]{1,0:T(8,128)(2,1)S(1)}, u32[]{:S(2)}, u32[]{:S(2)}) %collective-permute-start.5) | collective-permute-done | bytes 73760 | tf_op jit(solution)/shard_map/ppermute | solution.py:499
  31.2 0.1 shard_map.83
  31.3 1.8 %collective-permute-start.6 = (s16[144,256]{1,0:T(8,128)(2,1)S(1)}, s16[144,256]{1,0:T(8,128)(2,1)S(1)}, u32[]{:S(2)}, u32[]{:S(2)}) collective-permute-start(s16[144,256]{1,0:T(8,128)(2,1)S(1)} %shard_map.83), channel_id=1, source_target_pairs={{0,16},{8,24},{16,0},{24,8},{1,17},{9,25},{17,1},{25,9},{2,18},{10... | collective-permute-start | bytes 221192 | tf_op jit(solution)/shard_map/ppermute | solution.py:499
  33.0 0.0 collective-permute-done.4.refs_1_
  33.0 2.6 %collective-permute-done.6.refs_2_ = s16[144,256]{1,0:T(8,128)(2,1)S(1)} collective-permute-done((s16[144,256]{1,0:T(8,128)(2,1)S(1)}, s16[144,256]{1,0:T(8,128)(2,1)S(1)}, u32[]{:S(2)}, u32[]{:S(2)}) %collective-permute-start.6) | collective-permute-done | bytes 73760 | tf_op jit(solution)/shard_map/ppermute | solution.py:499
  35.7 0.1 shard_map.84.refs_0_
  35.8 1.9 %collective-permute-start.7 = (s16[144,256]{1,0:T(8,128)(2,1)S(1)}, s16[144,256]{1,0:T(8,128)(2,1)S(1)}, u32[]{:S(2)}, u32[]{:S(2)}) collective-permute-start(s16[144,256]{1,0:T(8,128)(2,1)S(1)} %shard_map.84.refs_0_), channel_id=1, source_target_pairs={{0,2},{2,0},{4,6},{6,4},{1,3},{3,1},{5,7},{7,5},{8,10},{10,8},{12,... | collective-permute-start | bytes 221192 | tf_op jit(solution)/shard_map/ppermute | solution.py:499
  37.6 2.6 %collective-permute-done.7.refs_1_ = s16[144,256]{1,0:T(8,128)(2,1)S(1)} collective-permute-done((s16[144,256]{1,0:T(8,128)(2,1)S(1)}, s16[144,256]{1,0:T(8,128)(2,1)S(1)}, u32[]{:S(2)}, u32[]{:S(2)}) %collective-permute-start.7) | collective-permute-done | bytes 73760 | tf_op jit(solution)/shard_map/ppermute | solution.py:499
  40.2 0.1 shard_map.85.refs_0_
  40.3 2.9 %collective-permute-start.8 = (s16[144,256]{1,0:T(8,128)(2,1)S(1)}, s16[144,256]{1,0:T(8,128)(2,1)S(1)}, u32[]{:S(2)}, u32[]{:S(2)}) collective-permute-start(s16[144,256]{1,0:T(8,128)(2,1)S(1)} %shard_map.85.refs_0_), channel_id=1, source_target_pairs={{0,4},{2,6},{4,0},{6,2},{1,5},{3,7},{5,1},{7,3},{8,12},{10,14},{12... | collective-permute-start | bytes 221192 | tf_op jit(solution)/shard_map/ppermute | solution.py:499
  43.2 2.4 %collective-permute-done.8.refs_1_ = s16[144,256]{1,0:T(8,128)(2,1)S(1)} collective-permute-done((s16[144,256]{1,0:T(8,128)(2,1)S(1)}, s16[144,256]{1,0:T(8,128)(2,1)S(1)}, u32[]{:S(2)}, u32[]{:S(2)}) %collective-permute-start.8) | collective-permute-done | bytes 73760 | tf_op jit(solution)/shard_map/ppermute | solution.py:499
  45.6 0.1 shard_map.86.x_ref
  45.7 1.8 %collective-permute-start.9 = (s16[144,256]{1,0:T(8,128)(2,1)S(1)}, s16[144,256]{1,0:T(8,128)(2,1)S(1)}, u32[]{:S(2)}, u32[]{:S(2)}) collective-permute-start(s16[144,256]{1,0:T(8,128)(2,1)S(1)} %shard_map.86.x_ref), channel_id=1, source_target_pairs={{0,16},{8,24},{16,0},{24,8},{1,17},{9,25},{17,1},{25,9},{2,18},{10... | collective-permute-start | bytes 221192 | tf_op jit(solution)/shard_map/ppermute | solution.py:499
  47.5 0.0 collective-permute-start.11
  47.5 2.6 %collective-permute-done.9.x_ref = s16[144,256]{1,0:T(8,128)(2,1)S(1)} collective-permute-done((s16[144,256]{1,0:T(8,128)(2,1)S(1)}, s16[144,256]{1,0:T(8,128)(2,1)S(1)}, u32[]{:S(2)}, u32[]{:S(2)}) %collective-permute-start.9) | collective-permute-done | bytes 73760 | tf_op jit(solution)/shard_map/ppermute | solution.py:499
  50.1 0.0 collective-permute-start.10
  50.1 1.3 %states.3.refs_2_ = bf16[256,2048]{1,0:T(8,128)(2,1)} custom-call(f32[2,8,128]{2,1,0:T(8,128)S(1)} %pad_maximum_fusion.1.entry_ref, f32[8,2,256,128]{3,2,1,0:T(8,128)S(1)} %get-tuple-element.42.decay_ref, bf16[8,256,256]{2,1,0:T(8,128)(2,1)S(1)} %get-tuple-element.36.refs_5_.high_ref, bf16[8,256,256]{2,1,0:T(8,128)(2,1)S(1)} %get-tuple-element.37.refs_6_.low_ref, ...), custom_call_target="tpu_custom_call" | custom-call | flops 201326592 | bytes 1800000 | tf_op jit(solution)/shard_map/states/pallas_call | solution.py:380
  51.4 1.9 %states.4.refs_2_ = bf16[256,2048]{1,0:T(8,128)(2,1)} custom-call(f32[2,8,128]{2,1,0:T(8,128)S(1)} %pad_maximum_fusion.1.entry_ref, f32[8,2,256,128]{3,2,1,0:T(8,128)S(1)} %get-tuple-element.42.decay_ref, bf16[8,256,256]{2,1,0:T(8,128)(2,1)S(1)} %get-tuple-element.36.refs_5_.high_ref, ...), custom_call_target="tpu_custom_call", output_to_operand_aliasing={{}: (6, {})} | custom-call | flops 301989888 | bytes 2700000 | tf_op jit(solution)/shard_map/states/pallas_call | solution.py:380
  53.3 1.9 %states.5 = bf16[256,2048]{1,0:T(8,128)(2,1)} custom-call(f32[2,8,128]{2,1,0:T(8,128)S(1)} %pad_maximum_fusion.1.entry_ref, f32[8,2,256,128]{3,2,1,0:T(8,128)S(1)} %get-tuple-element.42.decay_ref, bf16[8,256,256]{2,1,0:T(8,128)(2,1)S(1)} %get-tuple-element.36.refs_5_.high_ref, ...), custom_call_target="tpu_custom_call", output_to_operand_aliasing={{}: (6, {})} | custom-call | flops 301989888 | bytes 2700000 | tf_op jit(solution)/shard_map/states/pallas_call | solution.py:380
  55.3 1.1 %final.4.refs_0_ = f32[32,64,64]{2,1,0:T(8,128)} custom-call(s32[1]{0:T(128)} %bitcast.side_ref, s32[1]{0:T(128)} %bitcast.2.bit_ref, s16[144,256]{1,0:T(8,128)(2,1)S(1)} %shard_map.86.x_ref, bf16[8,256,256]{2,1,0:T(8,128)(2,1)S(1)} %get-tuple-element.36.refs_5_.high_ref, bf16[8,256,256]{2,1,0:T(8,128)(2,1)S(1)} %get-tuple-element.37.refs_6_.low_ref), custom_call_target="tpu_custom_call" | custom-call | flops 50331648 | bytes 800000 | tf_op jit(solution)/shard_map/final/pallas_call | solution.py:484
  56.4 0.0 collective-permute-done.11.x_ref
  56.4 1.1 %final.5.refs_0_ = f32[32,64,64]{2,1,0:T(8,128)} custom-call(s32[1]{0:T(128)} %bitcast.side_ref, s32[1]{0:T(128)} %bitcast.2.bit_ref, s16[144,256]{1,0:T(8,128)(2,1)S(1)} %collective-permute-done.11.x_ref, bf16[8,256,256]{2,1,0:T(8,128)(2,1)S(1)} %get-tuple-element.36.refs_5_.high_ref, ...), custom_call_target="tpu_custom_call", output_to_operand_aliasing={{}: (5, {})} | custom-call | flops 50331648 | bytes 800000 | tf_op jit(solution)/shard_map/final/pallas_call | solution.py:484
  57.5 1.1 %final.6.refs_0_ = f32[32,64,64]{2,1,0:T(8,128)} custom-call(s32[1]{0:T(128)} %bitcast.side_ref, s32[1]{0:T(128)} %bitcast.2.bit_ref, s16[144,256]{1,0:T(8,128)(2,1)S(1)} %collective-permute-done.9.x_ref, bf16[8,256,256]{2,1,0:T(8,128)(2,1)S(1)} %get-tuple-element.36.refs_5_.high_ref, ...), custom_call_target="tpu_custom_call", output_to_operand_aliasing={{}: (5, {})} | custom-call | flops 50331648 | bytes 800000 | tf_op jit(solution)/shard_map/final/pallas_call | solution.py:484
  58.5 0.0 collective-permute-done.10.x_ref
  58.6 1.1 %final.7 = f32[32,64,64]{2,1,0:T(8,128)} custom-call(s32[1]{0:T(128)} %bitcast.side_ref, s32[1]{0:T(128)} %bitcast.2.bit_ref, s16[144,256]{1,0:T(8,128)(2,1)S(1)} %collective-permute-done.10.x_ref, bf16[8,256,256]{2,1,0:T(8,128)(2,1)S(1)} %get-tuple-element.36.refs_5_.high_ref, ...), custom_call_target="tpu_custom_call", output_to_operand_aliasing={{}: (5, {})} | custom-call | flops 50331648 | bytes 800000 | tf_op jit(solution)/shard_map/final/pallas_call | solution.py:484
  (6 shorter events, 0.0 us)
Async XLA Ops:
  0.6 7.9 %copy-start.3 = (s32[1,256]{1,0:T(1,128)S(1)}, s32[1,256]{1,0:T(1,128)}, u32[]{:S(2)}) copy-start(s32[1,256]{1,0:T(1,128)} %boundary_ref.1) | copy-start | bytes 3076
  0.6 7.9 %copy-start.1 = (bf16[1,256,2048]{2,1,0:T(8,128)(2,1)S(1)}, bf16[1,256,2048]{2,1,0:T(8,128)(2,1)}, u32[]{:S(2)}) copy-start(bf16[1,256,2048]{2,1,0:T(8,128)(2,1)} %param.7) | copy-start | bytes 3145732
  1.7 18.3 %collective-permute-start = (bf16[128,768]{1,0:T(8,128)(2,1)S(1)}, bf16[128,768]{1,0:T(8,128)(2,1)S(1)}, u32[]{:S(2)}, u32[]{:S(2)}) collective-permute-start(bf16[128,768]{1,0:T(8,128)(2,1)S(1)} %dynamic-slice_bitcast_fusion.1), channel_id=1, source_target_pairs={{0,1},{1,0},{2,3},{3,2},{4,5},{5,4},{6,7},{7,6},{8,9},{9,8},{10,11... | collective-permute-start | bytes 589832 | tf_op jit(solution)/shard_map/ppermute | solution.py:499
  5.7 10.9 %copy-start = (bf16[1,128,4096]{2,1,0:T(8,128)(2,1)S(1)}, bf16[1,128,4096]{2,1,0:T(8,128)(2,1)}, u32[]{:S(2)}) copy-start(bf16[1,128,4096]{2,1,0:T(8,128)(2,1)} %param.6) | copy-start | bytes 3145732
  5.8 10.9 %collective-permute-start.1 = (bf16[128,1280]{1,0:T(8,128)(2,1)S(1)}, bf16[128,1280]{1,0:T(8,128)(2,1)S(1)}, u32[]{:S(2)}, u32[]{:S(2)}) collective-permute-start(bf16[128,1280]{1,0:T(8,128)(2,1)S(1)} %dynamic-slice_bitcast_fusion), channel_id=1, source_target_pairs={{0,1},{1,0},{2,3},{3,2},{4,5},{5,4},{6,7},{7,6},{8,9},{9,8},{10,11... | collective-permute-start | bytes 983048 | tf_op jit(solution)/shard_map/ppermute | solution.py:499
  6.7 0.8 %copy-start.2 = (f32[32,4,64]{2,1,0:T(4,128)S(1)}, f32[32,4,64]{2,1,0:T(4,128)}, u32[]{:S(2)}) copy-start(f32[32,4,64]{2,1,0:T(4,128)} %param.11) | copy-start | bytes 98308
  21.1 3.8 %collective-permute-start.2 = (f32[24,128]{1,0:T(8,128)S(1)}, f32[24,128]{1,0:T(8,128)S(1)}, u32[]{:S(2)}, u32[]{:S(2)}) collective-permute-start(f32[24,128]{1,0:T(8,128)S(1)} %get-tuple-element.40), channel_id=1, source_target_pairs={{0,2},{2,0},{4,6},{6,4},{1,3},{3,1},{5,7},{7,5},{8,10},{10,8},{12,... | collective-permute-start | bytes 36872 | tf_op jit(solution)/shard_map/ppermute | solution.py:499
  24.9 4.7 %collective-permute-start.3 = (f32[24,128]{1,0:T(8,128)S(1)}, f32[24,128]{1,0:T(8,128)S(1)}, u32[]{:S(2)}, u32[]{:S(2)}) collective-permute-start(f32[24,128]{1,0:T(8,128)S(1)} %pad_maximum_fusion), channel_id=1, source_target_pairs={{0,4},{2,6},{4,0},{6,2},{1,5},{3,7},{5,1},{7,3},{8,12},{10,14},{12... | collective-permute-start | bytes 36872 | tf_op jit(solution)/shard_map/ppermute | solution.py:499
  29.9 1.3 %collective-permute-start.5 = (s16[144,256]{1,0:T(8,128)(2,1)S(1)}, s16[144,256]{1,0:T(8,128)(2,1)S(1)}, u32[]{:S(2)}, u32[]{:S(2)}) collective-permute-start(s16[144,256]{1,0:T(8,128)(2,1)S(1)} %get-tuple-element.55), channel_id=1, source_target_pairs={{0,8},{8,0},{16,24},{24,16},{1,9},{9,1},{17,25},{25,17},{2,10},{10... | collective-permute-start | bytes 221192 | tf_op jit(solution)/shard_map/ppermute | solution.py:499
  29.9 3.1 %collective-permute-start.4 = (s16[144,256]{1,0:T(8,128)(2,1)S(1)}, s16[144,256]{1,0:T(8,128)(2,1)S(1)}, u32[]{:S(2)}, u32[]{:S(2)}) collective-permute-start(s16[144,256]{1,0:T(8,128)(2,1)S(1)} %get-tuple-element.53), channel_id=1, source_target_pairs={{0,8},{8,0},{16,24},{24,16},{1,9},{9,1},{17,25},{25,17},{2,10},{10... | collective-permute-start | bytes 221192 | tf_op jit(solution)/shard_map/ppermute | solution.py:499
  31.3 4.4 %collective-permute-start.6 = (s16[144,256]{1,0:T(8,128)(2,1)S(1)}, s16[144,256]{1,0:T(8,128)(2,1)S(1)}, u32[]{:S(2)}, u32[]{:S(2)}) collective-permute-start(s16[144,256]{1,0:T(8,128)(2,1)S(1)} %shard_map.83), channel_id=1, source_target_pairs={{0,16},{8,24},{16,0},{24,8},{1,17},{9,25},{17,1},{25,9},{2,18},{10... | collective-permute-start | bytes 221192 | tf_op jit(solution)/shard_map/ppermute | solution.py:499
  35.8 4.4 %collective-permute-start.7 = (s16[144,256]{1,0:T(8,128)(2,1)S(1)}, s16[144,256]{1,0:T(8,128)(2,1)S(1)}, u32[]{:S(2)}, u32[]{:S(2)}) collective-permute-start(s16[144,256]{1,0:T(8,128)(2,1)S(1)} %shard_map.84.refs_0_), channel_id=1, source_target_pairs={{0,2},{2,0},{4,6},{6,4},{1,3},{3,1},{5,7},{7,5},{8,10},{10,8},{12,... | collective-permute-start | bytes 221192 | tf_op jit(solution)/shard_map/ppermute | solution.py:499
  40.3 5.3 %collective-permute-start.8 = (s16[144,256]{1,0:T(8,128)(2,1)S(1)}, s16[144,256]{1,0:T(8,128)(2,1)S(1)}, u32[]{:S(2)}, u32[]{:S(2)}) collective-permute-start(s16[144,256]{1,0:T(8,128)(2,1)S(1)} %shard_map.85.refs_0_), channel_id=1, source_target_pairs={{0,4},{2,6},{4,0},{6,2},{1,5},{3,7},{5,1},{7,3},{8,12},{10,14},{12... | collective-permute-start | bytes 221192 | tf_op jit(solution)/shard_map/ppermute | solution.py:499
  45.7 4.4 %collective-permute-start.9 = (s16[144,256]{1,0:T(8,128)(2,1)S(1)}, s16[144,256]{1,0:T(8,128)(2,1)S(1)}, u32[]{:S(2)}, u32[]{:S(2)}) collective-permute-start(s16[144,256]{1,0:T(8,128)(2,1)S(1)} %shard_map.86.x_ref), channel_id=1, source_target_pairs={{0,16},{8,24},{16,0},{24,8},{1,17},{9,25},{17,1},{25,9},{2,18},{10... | collective-permute-start | bytes 221192 | tf_op jit(solution)/shard_map/ppermute | solution.py:499
  47.5 8.9 %collective-permute-start.11 = (s16[144,256]{1,0:T(8,128)(2,1)S(1)}, s16[144,256]{1,0:T(8,128)(2,1)S(1)}, u32[]{:S(2)}, u32[]{:S(2)}) collective-permute-start(s16[144,256]{1,0:T(8,128)(2,1)S(1)} %shard_map.86.x_ref), channel_id=1, source_target_pairs={{0,8},{8,0},{16,24},{24,16},{1,9},{9,1},{17,25},{25,17},{2,10},{10... | collective-permute-start | bytes 221192 | tf_op jit(solution)/shard_map/ppermute | solution.py:499
  50.1 8.4 %collective-permute-start.10 = (s16[144,256]{1,0:T(8,128)(2,1)S(1)}, s16[144,256]{1,0:T(8,128)(2,1)S(1)}, u32[]{:S(2)}, u32[]{:S(2)}) collective-permute-start(s16[144,256]{1,0:T(8,128)(2,1)S(1)} %collective-permute-done.9.x_ref), channel_id=1, source_target_pairs={{0,8},{8,0},{16,24},{24,16},{1,9},{9,1},{17,25},{25,17},{2,10},{10... | collective-permute-start | bytes 221192 | tf_op jit(solution)/shard_map/ppermute | solution.py:499

commit v6 on v5

--- a/solution.py
+++ b/solution.py
@@ -390,23 +390,27 @@
     )(*args)
 
 
-EXTRA = 16
 STEPS = 32000.0
+LEAST = -100
 
 
 def encode(x, code_ref):
-    rows = x.shape[0]
-    most = jnp.maximum(jnp.max(jnp.abs(x), axis=0, keepdims=True), 1e-30)
-    power = jnp.ceil(jnp.log2(most))
-    code = jnp.floor(x * (jnp.exp2(-power) * STEPS) + 0.5)
-    code_ref[:rows, :] = code.astype(jnp.int32).astype(jnp.int16)
-    code_ref[rows:, :] = jnp.broadcast_to(power, (EXTRA, power.shape[1])).astype(jnp.int32).astype(jnp.int16)
+    most = jnp.max(jnp.abs(x), axis=0, keepdims=True)
+    power = jnp.ceil(jnp.log2(jnp.maximum(most, 2.0**LEAST)))
+    code = jnp.floor(x * (jnp.exp2(-power) * STEPS) + 0.5).astype(jnp.int32)
+    row = iota((16, x.shape[1]), 0)
+    bit = ((power - LEAST).astype(jnp.int32) >> row) & 1
+    first = jnp.where(row < 8, (code[:16] & -2) | bit, code[:16])
+    code_ref[:16, :] = first.astype(jnp.int16)
+    code_ref[16:, :] = code[16:].astype(jnp.int16)
 
 
 def decode(code_ref, start=0, rows=None):
-    if rows is None:
-        rows = code_ref.shape[0] - EXTRA
-    power = code_ref[start + rows : start + rows + EXTRA, :].astype(jnp.int32).astype(F32)[:1]
+    rows = code_ref.shape[0] if rows is None else rows
+    first = code_ref[start : start + 16, :].astype(jnp.int32)
+    row = iota(first.shape, 0)
+    bits = jnp.where(row < 8, (first & 1) << row, 0).astype(F32)
+    power = jnp.sum(bits, axis=0, keepdims=True) + float(LEAST)
     return code_ref[start : start + rows, :].astype(jnp.int32).astype(F32) * (jnp.exp2(power) * (1.0 / STEPS))
 
 
@@ -433,7 +437,7 @@
 
 def merge(half, side, bit, entry, weight, parts):
     rows = half * SIZE // 2
-    out = [((rows, GROUP), F32)] * 2 + [((rows + EXTRA, GROUP), jnp.dtype(jnp.int16))] * 2
+    out = [((rows, GROUP), F32)] * 2 + [((rows, GROUP), jnp.dtype(jnp.int16))] * 2
     return call(functools.partial(merge_kernel, half), out, (side, bit, entry, weight, *parts),
                 [SMEM] * 2 + [VMEM] * (2 + len(parts)), [pltpu.VMEM((half * SIZE, GROUP), F32)] * 2)
 
@@ -456,8 +460,8 @@
     count = half * quarters // 2
     side, bit = (1 - ref[0] if flip else ref[0] for ref, flip in zip((side_ref, bit_ref), flips))
     start = side * half + bit * count if quarters == 1 else side * half
-    rows = x_ref.shape[0] // quarters - EXTRA
-    x = jnp.concatenate([decode(x_ref, n * (rows + EXTRA), rows) for n in range(quarters)], axis=0)
+    rows = x_ref.shape[0] // quarters
+    x = jnp.concatenate([decode(x_ref, n * rows, rows) for n in range(quarters)], axis=0)
     copies = []
     for n in range(count):
         at = start + n

time: 60 us -> 58.3 us (0.972)
  waiting for transfers between devices: 18.4 us -> 16.8 us
    ppermute x12, waiting for transfers between devices: 18.4 us -> 16.8 us  [swap(): return lax.ppermute(x, axis, [(i, i ^ k) for i in range(n)])]
  transfers between devices with their start and end apart: 12 -> 12, of which waited for: 8 -> 8; matrix products, arithmetic and copies ran while one was open for 3% -> 3% of each run, Pallas kernels for 29% -> 30%
where the time goes in v6:
time: 58.3 us; the launch traced here: 58 us
  Pallas kernels  20 us (34%)
  waiting for transfers between devices  16.8 us (29%)
  starting transfers between devices  16.7 us (29%)
  local copies, waits for them, and re-layouts  2.88 us (5%)
  between operations  0.85 us (1%)
  other arithmetic  0.84 us (1%)
    ppermute x12, waiting for transfers between devices, swap(): return lax.ppermute(x, axis, [(i, i ^ k) for i in range(n)])  16.8 us
    ppermute x12, starting transfers between devices, swap(): return lax.ppermute(x, axis, [(i, i ^ k) for i in range(n)])  16.7 us
    pallas_call x10, Pallas kernels, call(): pl.pallas_call(kernel, out_shape=shapes, in_specs=specs, out_specs=[VMEM]...  10.5 us
    pallas_call x3, Pallas kernels, states(): pl.pallas_call(functools.partial(state_kernel, base, sizes), grid=(count,...  5.16 us
    pallas_call x4, Pallas kernels, final(): pl.pallas_call(functools.partial(final_kernel, flips, quarters), out_shap...  4.35 us
    dynamic_slice x2, local copies, waits for them, and re-layouts, away(): lax.dynamic_slice(rows, (jnp.uint32(0), start), (rows.shape[0], count * G...  2.02 us
  transfers between devices with their start and end apart: 12, of which 8 were waited for; matrix products, arithmetic and copies ran while one was open for 3% of the time, Pallas kernels for 30%

profile of v6, /device:TPU:0, one launch (start us, length us, event | category | flops | bytes accessed | tf_op | source)
XLA Modules:
  0.0 58.0 jit_solution(1641761658541504827)
XLA Ops:
  0.6 0.0 copy-start.3
  0.6 0.0 copy-start.1
  0.7 1.0 %dynamic-slice_bitcast_fusion.1 = bf16[128,768]{1,0:T(8,128)(2,1)S(1)} fusion(bf16[1,128,4096]{2,1,0:T(8,128)(2,1)} %param.6, u32[]{:T(128)S(6)} %add.31), kind=kLoop, calls=%fused_computation.1 | loop fusion | bytes 393220 | tf_op jit(solution)/shard_map/dynamic_slice | solution.py:590
  1.7 3.1 %collective-permute-start = (bf16[128,768]{1,0:T(8,128)(2,1)S(1)}, bf16[128,768]{1,0:T(8,128)(2,1)S(1)}, u32[]{:S(2)}, u32[]{:S(2)}) collective-permute-start(bf16[128,768]{1,0:T(8,128)(2,1)S(1)} %dynamic-slice_bitcast_fusion.1), channel_id=1, source_target_pairs={{0,1},{1,0},{2,3},{3,2},{4,5},{5,4},{6,7},{7,6},{8,9},{9,8},{10,11... | collective-permute-start | bytes 589832 | tf_op jit(solution)/shard_map/ppermute | solution.py:503
  4.8 1.0 %dynamic-slice_bitcast_fusion = bf16[128,1280]{1,0:T(8,128)(2,1)S(1)} fusion(bf16[1,128,4096]{2,1,0:T(8,128)(2,1)} %param.6, u32[]{:T(128)S(6)} %mul.71), kind=kLoop, calls=%fused_computation | loop fusion | bytes 655364 | tf_op jit(solution)/shard_map/dynamic_slice | solution.py:590
  5.7 0.0 copy-start
  5.8 0.1 collective-permute-start.1
  5.8 0.8 %multiply_add_fusion.code_ref = s32[32,32]{1,0:T(8,128)S(1)} fusion(s32[32,32]{1,0:T(8,128)} %param.10, s32[32,32]{1,0:T(8,128)} %param.9), kind=kLoop, calls=%fused_computation.2 | loop fusion | flops 2048 | bytes 12288 | tf_op jit(solution)/shard_map/add | solution.py:602
  6.7 0.0 copy-start.2
  6.7 0.8 %copy-done.2 = f32[32,4,64]{2,1,0:T(4,128)S(1)} copy-done((f32[32,4,64]{2,1,0:T(4,128)S(1)}, f32[32,4,64]{2,1,0:T(4,128)}, u32[]{:S(2)}) %copy-start.2) | copy-done | bytes 32792
  7.5 1.1 %shard_map.77 = (bf16[8,256,256]{2,1,0:T(8,128)(2,1)S(1)}, bf16[8,256,256]{2,1,0:T(8,128)(2,1)S(1)}, f32[8,2,8,128]{3,2,1,0:T(8,128)S(1)}, f32[2,8,128]{2,1,0:T(8,128)S(1)}) custom-call(s32[32,32]{1,0:T(8,128)S(1)} %multiply_add_fusion.code_ref, f32[128,64]{1,0:T(8,128)S(1)} %bitcast.78), custom_call_target="tpu_custom_call" | custom-call | flops 536870912 | bytes 2207744 | tf_op jit(solution)/shard_map/pallas_call | solution.py:204
  8.6 0.0 copy-done.3
  8.6 0.0 copy-done.1
  8.6 3.0 %shard_map.78 = (f32[256,128]{1,0:T(8,128)S(1)}, f32[5,8,128]{2,1,0:T(8,128)S(1)}, bf16[2048,256]{1,0:T(8,128)(2,1)S(1)}, f32[8,2,256,128]{3,2,1,0:T(8,128)S(1)}, f32[8,64,256]{2,1,0:T(8,128)S(1)}) custom-call(s32[1,256]{1,0:T(1,128)S(1)} %copy-done.3, f32[8,2,8,128]{3,2,1,0:T(8,128)S(1)} %get-tuple-element.32.tab_ref.refs_0_, bf16[256,2048]{1,0:T(8,128)(2,1)S(1)} %bitcast.77), custom_call_target="tpu_custom_call" | custom-call | flops 536870912 | bytes 4936704 | tf_op jit(solution)/shard_map/pallas_call | solution.py:204
  11.6 5.1 %collective-permute-done.1.refs_7_ = bf16[128,1280]{1,0:T(8,128)(2,1)S(1)} collective-permute-done((bf16[128,1280]{1,0:T(8,128)(2,1)S(1)}, bf16[128,1280]{1,0:T(8,128)(2,1)S(1)}, u32[]{:S(2)}, u32[]{:S(2)}) %collective-permute-start.1) | collective-permute-done | bytes 327712 | tf_op jit(solution)/shard_map/ppermute | solution.py:503
  16.7 0.0 copy-done
  16.7 3.3 %shard_map.79 = (f32[5,2,256,128]{3,2,1,0:T(8,128)S(1)}, f32[2,5,128]{2,1,0:T(8,128)S(1)}, f32[5,64,256]{2,1,0:T(8,128)S(1)}) custom-call(f32[8,2,8,128]{3,2,1,0:T(8,128)S(1)} %get-tuple-element.32.tab_ref.refs_0_, f32[5,8,128]{2,1,0:T(8,128)S(1)} %get-tuple-element.33.refs_1_, f32[256,128]{1,0:T(8,128)S(1)} %get-tuple-element.34.refs_2_, s32[1]{0:T(128)} %bitcast.1.refs_3_, ...), custom_call_target="tpu_custom_call" | custom-call | flops 671088640 | bytes 6382596 | tf_op jit(solution)/shard_map/pallas_call | solution.py:204
  20.0 0.0 collective-permute-done.refs_7_
  20.0 1.1 %shard_map.80 = (f32[3,2,256,128]{3,2,1,0:T(8,128)S(1)}, f32[3,2,8,128]{3,2,1,0:T(8,128)S(1)}, f32[24,128]{1,0:T(8,128)S(1)}) custom-call(f32[8,2,8,128]{3,2,1,0:T(8,128)S(1)} %get-tuple-element.32.tab_ref.refs_0_, f32[5,8,128]{2,1,0:T(8,128)S(1)} %get-tuple-element.33.refs_1_, f32[256,128]{1,0:T(8,128)S(1)} %get-tuple-element.34.refs_2_, s32[1]{0:T(128)} %bitcast.1.refs_3_, ...), custom_call_target="tpu_custom_call" | custom-call | flops 201326592 | bytes 4387844 | tf_op jit(solution)/shard_map/pallas_call | solution.py:204
  21.1 1.9 %collective-permute-start.2 = (f32[24,128]{1,0:T(8,128)S(1)}, f32[24,128]{1,0:T(8,128)S(1)}, u32[]{:S(2)}, u32[]{:S(2)}) collective-permute-start(f32[24,128]{1,0:T(8,128)S(1)} %get-tuple-element.40), channel_id=1, source_target_pairs={{0,2},{2,0},{4,6},{6,4},{1,3},{3,1},{5,7},{7,5},{8,10},{10,8},{12,... | collective-permute-start | bytes 36872 | tf_op jit(solution)/shard_map/ppermute | solution.py:503
  23.0 1.9 %collective-permute-done.2 = f32[24,128]{1,0:T(8,128)S(1)} collective-permute-done((f32[24,128]{1,0:T(8,128)S(1)}, f32[24,128]{1,0:T(8,128)S(1)}, u32[]{:S(2)}, u32[]{:S(2)}) %collective-permute-start.2) | collective-permute-done | bytes 12320 | tf_op jit(solution)/shard_map/ppermute | solution.py:503
  24.9 2.9 %collective-permute-start.3 = (f32[24,128]{1,0:T(8,128)S(1)}, f32[24,128]{1,0:T(8,128)S(1)}, u32[]{:S(2)}, u32[]{:S(2)}) collective-permute-start(f32[24,128]{1,0:T(8,128)S(1)} %pad_maximum_fusion), channel_id=1, source_target_pairs={{0,4},{2,6},{4,0},{6,2},{1,5},{3,7},{5,1},{7,3},{8,12},{10,14},{12... | collective-permute-start | bytes 36872 | tf_op jit(solution)/shard_map/ppermute | solution.py:503
  27.8 1.4 %shard_map.81 = (f32[3,2,256,128]{3,2,1,0:T(8,128)S(1)}, f32[3,64,256]{2,1,0:T(8,128)S(1)}) custom-call(f32[8,2,8,128]{3,2,1,0:T(8,128)S(1)} %get-tuple-element.32.tab_ref.refs_0_, f32[5,8,128]{2,1,0:T(8,128)S(1)} %get-tuple-element.33.refs_1_, f32[256,128]{1,0:T(8,128)S(1)} %get-tuple-element.34.refs_2_, ...), custom_call_target="tpu_custom_call" | custom-call | flops 201326592 | bytes 3059712 | tf_op jit(solution)/shard_map/pallas_call | solution.py:204
  29.2 0.4 collective-permute-done.3
  29.6 0.2 shard_map.82
  29.9 0.1 collective-permute-start.5
  29.9 0.5 collective-permute-start.4
  30.4 0.7 %collective-permute-done.5.refs_1_ = s16[128,256]{1,0:T(8,128)(2,1)S(1)} collective-permute-done((s16[128,256]{1,0:T(8,128)(2,1)S(1)}, s16[128,256]{1,0:T(8,128)(2,1)S(1)}, u32[]{:S(2)}, u32[]{:S(2)}) %collective-permute-start.5) | collective-permute-done | bytes 65568 | tf_op jit(solution)/shard_map/ppermute | solution.py:503
  31.2 0.1 shard_map.83
  31.3 1.8 %collective-permute-start.6 = (s16[128,256]{1,0:T(8,128)(2,1)S(1)}, s16[128,256]{1,0:T(8,128)(2,1)S(1)}, u32[]{:S(2)}, u32[]{:S(2)}) collective-permute-start(s16[128,256]{1,0:T(8,128)(2,1)S(1)} %shard_map.83), channel_id=1, source_target_pairs={{0,16},{8,24},{16,0},{24,8},{1,17},{9,25},{17,1},{25,9},{2,18},{10... | collective-permute-start | bytes 196616 | tf_op jit(solution)/shard_map/ppermute | solution.py:503
  33.0 0.0 collective-permute-done.4.refs_1_
  33.0 2.6 %collective-permute-done.6.refs_2_ = s16[128,256]{1,0:T(8,128)(2,1)S(1)} collective-permute-done((s16[128,256]{1,0:T(8,128)(2,1)S(1)}, s16[128,256]{1,0:T(8,128)(2,1)S(1)}, u32[]{:S(2)}, u32[]{:S(2)}) %collective-permute-start.6) | collective-permute-done | bytes 65568 | tf_op jit(solution)/shard_map/ppermute | solution.py:503
  35.6 0.1 shard_map.84.refs_0_
  35.7 1.9 %collective-permute-start.7 = (s16[128,256]{1,0:T(8,128)(2,1)S(1)}, s16[128,256]{1,0:T(8,128)(2,1)S(1)}, u32[]{:S(2)}, u32[]{:S(2)}) collective-permute-start(s16[128,256]{1,0:T(8,128)(2,1)S(1)} %shard_map.84.refs_0_), channel_id=1, source_target_pairs={{0,2},{2,0},{4,6},{6,4},{1,3},{3,1},{5,7},{7,5},{8,10},{10,8},{12,... | collective-permute-start | bytes 196616 | tf_op jit(solution)/shard_map/ppermute | solution.py:503
  37.6 2.5 %collective-permute-done.7.refs_1_ = s16[128,256]{1,0:T(8,128)(2,1)S(1)} collective-permute-done((s16[128,256]{1,0:T(8,128)(2,1)S(1)}, s16[128,256]{1,0:T(8,128)(2,1)S(1)}, u32[]{:S(2)}, u32[]{:S(2)}) %collective-permute-start.7) | collective-permute-done | bytes 65568 | tf_op jit(solution)/shard_map/ppermute | solution.py:503
  40.0 0.1 shard_map.85.refs_0_
  40.1 2.9 %collective-permute-start.8 = (s16[128,256]{1,0:T(8,128)(2,1)S(1)}, s16[128,256]{1,0:T(8,128)(2,1)S(1)}, u32[]{:S(2)}, u32[]{:S(2)}) collective-permute-start(s16[128,256]{1,0:T(8,128)(2,1)S(1)} %shard_map.85.refs_0_), channel_id=1, source_target_pairs={{0,4},{2,6},{4,0},{6,2},{1,5},{3,7},{5,1},{7,3},{8,12},{10,14},{12... | collective-permute-start | bytes 196616 | tf_op jit(solution)/shard_map/ppermute | solution.py:503
  43.0 2.4 %collective-permute-done.8.refs_1_ = s16[128,256]{1,0:T(8,128)(2,1)S(1)} collective-permute-done((s16[128,256]{1,0:T(8,128)(2,1)S(1)}, s16[128,256]{1,0:T(8,128)(2,1)S(1)}, u32[]{:S(2)}, u32[]{:S(2)}) %collective-permute-start.8) | collective-permute-done | bytes 65568 | tf_op jit(solution)/shard_map/ppermute | solution.py:503
  45.4 0.1 shard_map.86.x_ref
  45.4 1.8 %collective-permute-start.9 = (s16[128,256]{1,0:T(8,128)(2,1)S(1)}, s16[128,256]{1,0:T(8,128)(2,1)S(1)}, u32[]{:S(2)}, u32[]{:S(2)}) collective-permute-start(s16[128,256]{1,0:T(8,128)(2,1)S(1)} %shard_map.86.x_ref), channel_id=1, source_target_pairs={{0,16},{8,24},{16,0},{24,8},{1,17},{9,25},{17,1},{25,9},{2,18},{10... | collective-permute-start | bytes 196616 | tf_op jit(solution)/shard_map/ppermute | solution.py:503
  47.2 0.0 collective-permute-start.11
  47.2 1.3 %states.3.refs_2_ = bf16[256,2048]{1,0:T(8,128)(2,1)} custom-call(f32[2,8,128]{2,1,0:T(8,128)S(1)} %pad_maximum_fusion.1.entry_ref, f32[8,2,256,128]{3,2,1,0:T(8,128)S(1)} %get-tuple-element.42.decay_ref, bf16[8,256,256]{2,1,0:T(8,128)(2,1)S(1)} %get-tuple-element.36.refs_5_.high_ref, bf16[8,256,256]{2,1,0:T(8,128)(2,1)S(1)} %get-tuple-element.37.refs_6_.low_ref, ...), custom_call_target="tpu_custom_call" | custom-call | flops 201326592 | bytes 1800000 | tf_op jit(solution)/shard_map/states/pallas_call | solution.py:380
  48.5 1.3 %collective-permute-done.9.x_ref = s16[128,256]{1,0:T(8,128)(2,1)S(1)} collective-permute-done((s16[128,256]{1,0:T(8,128)(2,1)S(1)}, s16[128,256]{1,0:T(8,128)(2,1)S(1)}, u32[]{:S(2)}, u32[]{:S(2)}) %collective-permute-start.9) | collective-permute-done | bytes 65568 | tf_op jit(solution)/shard_map/ppermute | solution.py:503
  49.8 0.0 collective-permute-start.10
  49.8 1.9 %states.4.refs_2_ = bf16[256,2048]{1,0:T(8,128)(2,1)} custom-call(f32[2,8,128]{2,1,0:T(8,128)S(1)} %pad_maximum_fusion.1.entry_ref, f32[8,2,256,128]{3,2,1,0:T(8,128)S(1)} %get-tuple-element.42.decay_ref, bf16[8,256,256]{2,1,0:T(8,128)(2,1)S(1)} %get-tuple-element.36.refs_5_.high_ref, ...), custom_call_target="tpu_custom_call", output_to_operand_aliasing={{}: (6, {})} | custom-call | flops 301989888 | bytes 2700000 | tf_op jit(solution)/shard_map/states/pallas_call | solution.py:380
  51.7 1.9 %states.5 = bf16[256,2048]{1,0:T(8,128)(2,1)} custom-call(f32[2,8,128]{2,1,0:T(8,128)S(1)} %pad_maximum_fusion.1.entry_ref, f32[8,2,256,128]{3,2,1,0:T(8,128)S(1)} %get-tuple-element.42.decay_ref, bf16[8,256,256]{2,1,0:T(8,128)(2,1)S(1)} %get-tuple-element.36.refs_5_.high_ref, ...), custom_call_target="tpu_custom_call", output_to_operand_aliasing={{}: (6, {})} | custom-call | flops 301989888 | bytes 2700000 | tf_op jit(solution)/shard_map/states/pallas_call | solution.py:380
  53.6 1.1 %final.4.refs_0_ = f32[32,64,64]{2,1,0:T(8,128)} custom-call(s32[1]{0:T(128)} %bitcast.side_ref, s32[1]{0:T(128)} %bitcast.2.bit_ref, s16[128,256]{1,0:T(8,128)(2,1)S(1)} %shard_map.86.x_ref, bf16[8,256,256]{2,1,0:T(8,128)(2,1)S(1)} %get-tuple-element.36.refs_5_.high_ref, bf16[8,256,256]{2,1,0:T(8,128)(2,1)S(1)} %get-tuple-element.37.refs_6_.low_ref), custom_call_target="tpu_custom_call" | custom-call | flops 50331648 | bytes 800000 | tf_op jit(solution)/shard_map/final/pallas_call | solution.py:488
  54.7 0.0 collective-permute-done.11.x_ref
  54.8 1.1 %final.5.refs_0_ = f32[32,64,64]{2,1,0:T(8,128)} custom-call(s32[1]{0:T(128)} %bitcast.side_ref, s32[1]{0:T(128)} %bitcast.2.bit_ref, s16[128,256]{1,0:T(8,128)(2,1)S(1)} %collective-permute-done.11.x_ref, bf16[8,256,256]{2,1,0:T(8,128)(2,1)S(1)} %get-tuple-element.36.refs_5_.high_ref, ...), custom_call_target="tpu_custom_call", output_to_operand_aliasing={{}: (5, {})} | custom-call | flops 50331648 | bytes 800000 | tf_op jit(solution)/shard_map/final/pallas_call | solution.py:488
  55.9 1.1 %final.6.refs_0_ = f32[32,64,64]{2,1,0:T(8,128)} custom-call(s32[1]{0:T(128)} %bitcast.side_ref, s32[1]{0:T(128)} %bitcast.2.bit_ref, s16[128,256]{1,0:T(8,128)(2,1)S(1)} %collective-permute-done.9.x_ref, bf16[8,256,256]{2,1,0:T(8,128)(2,1)S(1)} %get-tuple-element.36.refs_5_.high_ref, ...), custom_call_target="tpu_custom_call", output_to_operand_aliasing={{}: (5, {})} | custom-call | flops 50331648 | bytes 800000 | tf_op jit(solution)/shard_map/final/pallas_call | solution.py:488
  56.9 0.0 collective-permute-done.10.x_ref
  57.0 1.1 %final.7 = f32[32,64,64]{2,1,0:T(8,128)} custom-call(s32[1]{0:T(128)} %bitcast.side_ref, s32[1]{0:T(128)} %bitcast.2.bit_ref, s16[128,256]{1,0:T(8,128)(2,1)S(1)} %collective-permute-done.10.x_ref, bf16[8,256,256]{2,1,0:T(8,128)(2,1)S(1)} %get-tuple-element.36.refs_5_.high_ref, ...), custom_call_target="tpu_custom_call", output_to_operand_aliasing={{}: (5, {})} | custom-call | flops 50331648 | bytes 800000 | tf_op jit(solution)/shard_map/final/pallas_call | solution.py:488
  (6 shorter events, 0.0 us)
Async XLA Ops:
  0.6 7.9 %copy-start.3 = (s32[1,256]{1,0:T(1,128)S(1)}, s32[1,256]{1,0:T(1,128)}, u32[]{:S(2)}) copy-start(s32[1,256]{1,0:T(1,128)} %boundary_ref.1) | copy-start | bytes 3076
  0.6 7.9 %copy-start.1 = (bf16[1,256,2048]{2,1,0:T(8,128)(2,1)S(1)}, bf16[1,256,2048]{2,1,0:T(8,128)(2,1)}, u32[]{:S(2)}) copy-start(bf16[1,256,2048]{2,1,0:T(8,128)(2,1)} %param.7) | copy-start | bytes 3145732
  1.7 18.3 %collective-permute-start = (bf16[128,768]{1,0:T(8,128)(2,1)S(1)}, bf16[128,768]{1,0:T(8,128)(2,1)S(1)}, u32[]{:S(2)}, u32[]{:S(2)}) collective-permute-start(bf16[128,768]{1,0:T(8,128)(2,1)S(1)} %dynamic-slice_bitcast_fusion.1), channel_id=1, source_target_pairs={{0,1},{1,0},{2,3},{3,2},{4,5},{5,4},{6,7},{7,6},{8,9},{9,8},{10,11... | collective-permute-start | bytes 589832 | tf_op jit(solution)/shard_map/ppermute | solution.py:503
  5.7 10.9 %copy-start = (bf16[1,128,4096]{2,1,0:T(8,128)(2,1)S(1)}, bf16[1,128,4096]{2,1,0:T(8,128)(2,1)}, u32[]{:S(2)}) copy-start(bf16[1,128,4096]{2,1,0:T(8,128)(2,1)} %param.6) | copy-start | bytes 3145732
  5.8 10.9 %collective-permute-start.1 = (bf16[128,1280]{1,0:T(8,128)(2,1)S(1)}, bf16[128,1280]{1,0:T(8,128)(2,1)S(1)}, u32[]{:S(2)}, u32[]{:S(2)}) collective-permute-start(bf16[128,1280]{1,0:T(8,128)(2,1)S(1)} %dynamic-slice_bitcast_fusion), channel_id=1, source_target_pairs={{0,1},{1,0},{2,3},{3,2},{4,5},{5,4},{6,7},{7,6},{8,9},{9,8},{10,11... | collective-permute-start | bytes 983048 | tf_op jit(solution)/shard_map/ppermute | solution.py:503
  6.7 0.8 %copy-start.2 = (f32[32,4,64]{2,1,0:T(4,128)S(1)}, f32[32,4,64]{2,1,0:T(4,128)}, u32[]{:S(2)}) copy-start(f32[32,4,64]{2,1,0:T(4,128)} %param.11) | copy-start | bytes 98308
  21.1 3.8 %collective-permute-start.2 = (f32[24,128]{1,0:T(8,128)S(1)}, f32[24,128]{1,0:T(8,128)S(1)}, u32[]{:S(2)}, u32[]{:S(2)}) collective-permute-start(f32[24,128]{1,0:T(8,128)S(1)} %get-tuple-element.40), channel_id=1, source_target_pairs={{0,2},{2,0},{4,6},{6,4},{1,3},{3,1},{5,7},{7,5},{8,10},{10,8},{12,... | collective-permute-start | bytes 36872 | tf_op jit(solution)/shard_map/ppermute | solution.py:503
  24.9 4.7 %collective-permute-start.3 = (f32[24,128]{1,0:T(8,128)S(1)}, f32[24,128]{1,0:T(8,128)S(1)}, u32[]{:S(2)}, u32[]{:S(2)}) collective-permute-start(f32[24,128]{1,0:T(8,128)S(1)} %pad_maximum_fusion), channel_id=1, source_target_pairs={{0,4},{2,6},{4,0},{6,2},{1,5},{3,7},{5,1},{7,3},{8,12},{10,14},{12... | collective-permute-start | bytes 36872 | tf_op jit(solution)/shard_map/ppermute | solution.py:503
  29.9 1.3 %collective-permute-start.5 = (s16[128,256]{1,0:T(8,128)(2,1)S(1)}, s16[128,256]{1,0:T(8,128)(2,1)S(1)}, u32[]{:S(2)}, u32[]{:S(2)}) collective-permute-start(s16[128,256]{1,0:T(8,128)(2,1)S(1)} %get-tuple-element.55), channel_id=1, source_target_pairs={{0,8},{8,0},{16,24},{24,16},{1,9},{9,1},{17,25},{25,17},{2,10},{10... | collective-permute-start | bytes 196616 | tf_op jit(solution)/shard_map/ppermute | solution.py:503
  29.9 3.1 %collective-permute-start.4 = (s16[128,256]{1,0:T(8,128)(2,1)S(1)}, s16[128,256]{1,0:T(8,128)(2,1)S(1)}, u32[]{:S(2)}, u32[]{:S(2)}) collective-permute-start(s16[128,256]{1,0:T(8,128)(2,1)S(1)} %get-tuple-element.53), channel_id=1, source_target_pairs={{0,8},{8,0},{16,24},{24,16},{1,9},{9,1},{17,25},{25,17},{2,10},{10... | collective-permute-start | bytes 196616 | tf_op jit(solution)/shard_map/ppermute | solution.py:503
  31.3 4.3 %collective-permute-start.6 = (s16[128,256]{1,0:T(8,128)(2,1)S(1)}, s16[128,256]{1,0:T(8,128)(2,1)S(1)}, u32[]{:S(2)}, u32[]{:S(2)}) collective-permute-start(s16[128,256]{1,0:T(8,128)(2,1)S(1)} %shard_map.83), channel_id=1, source_target_pairs={{0,16},{8,24},{16,0},{24,8},{1,17},{9,25},{17,1},{25,9},{2,18},{10... | collective-permute-start | bytes 196616 | tf_op jit(solution)/shard_map/ppermute | solution.py:503
  35.7 4.3 %collective-permute-start.7 = (s16[128,256]{1,0:T(8,128)(2,1)S(1)}, s16[128,256]{1,0:T(8,128)(2,1)S(1)}, u32[]{:S(2)}, u32[]{:S(2)}) collective-permute-start(s16[128,256]{1,0:T(8,128)(2,1)S(1)} %shard_map.84.refs_0_), channel_id=1, source_target_pairs={{0,2},{2,0},{4,6},{6,4},{1,3},{3,1},{5,7},{7,5},{8,10},{10,8},{12,... | collective-permute-start | bytes 196616 | tf_op jit(solution)/shard_map/ppermute | solution.py:503
  40.1 5.2 %collective-permute-start.8 = (s16[128,256]{1,0:T(8,128)(2,1)S(1)}, s16[128,256]{1,0:T(8,128)(2,1)S(1)}, u32[]{:S(2)}, u32[]{:S(2)}) collective-permute-start(s16[128,256]{1,0:T(8,128)(2,1)S(1)} %shard_map.85.refs_0_), channel_id=1, source_target_pairs={{0,4},{2,6},{4,0},{6,2},{1,5},{3,7},{5,1},{7,3},{8,12},{10,14},{12... | collective-permute-start | bytes 196616 | tf_op jit(solution)/shard_map/ppermute | solution.py:503
  45.4 4.3 %collective-permute-start.9 = (s16[128,256]{1,0:T(8,128)(2,1)S(1)}, s16[128,256]{1,0:T(8,128)(2,1)S(1)}, u32[]{:S(2)}, u32[]{:S(2)}) collective-permute-start(s16[128,256]{1,0:T(8,128)(2,1)S(1)} %shard_map.86.x_ref), channel_id=1, source_target_pairs={{0,16},{8,24},{16,0},{24,8},{1,17},{9,25},{17,1},{25,9},{2,18},{10... | collective-permute-start | bytes 196616 | tf_op jit(solution)/shard_map/ppermute | solution.py:503
  47.2 7.5 %collective-permute-start.11 = (s16[128,256]{1,0:T(8,128)(2,1)S(1)}, s16[128,256]{1,0:T(8,128)(2,1)S(1)}, u32[]{:S(2)}, u32[]{:S(2)}) collective-permute-start(s16[128,256]{1,0:T(8,128)(2,1)S(1)} %shard_map.86.x_ref), channel_id=1, source_target_pairs={{0,8},{8,0},{16,24},{24,16},{1,9},{9,1},{17,25},{25,17},{2,10},{10... | collective-permute-start | bytes 196616 | tf_op jit(solution)/shard_map/ppermute | solution.py:503
  49.8 7.2 %collective-permute-start.10 = (s16[128,256]{1,0:T(8,128)(2,1)S(1)}, s16[128,256]{1,0:T(8,128)(2,1)S(1)}, u32[]{:S(2)}, u32[]{:S(2)}) collective-permute-start(s16[128,256]{1,0:T(8,128)(2,1)S(1)} %collective-permute-done.9.x_ref), channel_id=1, source_target_pairs={{0,8},{8,0},{16,24},{24,16},{1,9},{9,1},{17,25},{25,17},{2,10},{10... | collective-permute-start | bytes 196616 | tf_op jit(solution)/shard_map/ppermute | solution.py:503

commit v7 on v6

--- a/solution.py
+++ b/solution.py
@@ -258,21 +258,33 @@
         (grad_ref,) = take(1)
     heads = []
     if begin:
-        rows_ref, = take(1)
-        spaced_ref = take(1)[0] if finish else out_ref
-        size = own_ref.shape[0]
-        width = count * GROUP
         place = place_ref[0]
-        channels = high_ref.shape[0] * GROUP
-        at = pl.ds(pl.multiple_of(place * size, size), size)
-        rows_ref[at, :] = own_ref[:, pl.ds(pl.multiple_of(place * channels + base * GROUP, GROUP), width)]
-        for k in range(1, peers):
-            rows_ref[pl.ds(pl.multiple_of((place ^ k) * size, size), size), :] = others[k - 1][...]
-        for n in range(count):
-            rows = rows_ref[:, n * GROUP : (n + 1) * GROUP]
-            out = matmul(rows, high_ref[base + n]) + matmul(rows, low_ref[base + n])
-            spaced_ref[n, 0] = out[:, :LANES]
-            spaced_ref[n, 1] = out[:, LANES:]
+        if finish:
+            rows_ref, spaced_ref = take(2)
+            size = own_ref.shape[0]
+            width = count * GROUP
+            channels = high_ref.shape[0] * GROUP
+            at = [pl.ds(pl.multiple_of((place ^ k) * size, size), size) for k in range(peers)]
+            rows_ref[at[0], :] = own_ref[:, pl.ds(pl.multiple_of(place * channels + base * GROUP, GROUP), width)]
+            for k in range(1, peers):
+                rows_ref[at[k], :] = others[k - 1][...]
+            for n in range(count):
+                rows = rows_ref[:, n * GROUP : (n + 1) * GROUP]
+                out = matmul(rows, high_ref[base + n]) + matmul(rows, low_ref[base + n])
+                spaced_ref[n, 0] = out[:, :LANES]
+                spaced_ref[n, 1] = out[:, LANES:]
+        else:
+            spaced_ref = out_ref
+            size = own_ref.shape[2]
+            at = [pl.ds(pl.multiple_of((place ^ k) * size, size), size) for k in range(peers)]
+            for n in range(count):
+                for c in range(2):
+                    spaced_ref[n, c, at[0], :] = own_ref[n, c]
+                for k in range(1, peers):
+                    rows = others[k - 1][:, n * GROUP : (n + 1) * GROUP]
+                    out = matmul(rows, high_ref[base + n]) + matmul(rows, low_ref[base + n])
+                    spaced_ref[n, 0, at[k], :] = out[:, :LANES]
+                    spaced_ref[n, 1, at[k], :] = out[:, LANES:]
     else:
         spaced_ref = in_ref
     load = lambda n, at: (spaced_ref[n, 0, at, :], spaced_ref[n, 1, at, :])
@@ -318,6 +330,20 @@
             grad_ref[n] = fold(matmul(turned, high) + matmul(turned, low))
 
 
+def ahead_kernel(base, place_ref, own_ref, high_ref, low_ref, out_ref):
+    start = place_ref[0] * (high_ref.shape[0] * GROUP) + base * GROUP
+    for n in range(out_ref.shape[0]):
+        rows = own_ref[:, pl.ds(pl.multiple_of(start + n * GROUP, GROUP), GROUP)]
+        out = matmul(rows, high_ref[base + n]) + matmul(rows, low_ref[base + n])
+        out_ref[n, 0] = out[:, :LANES]
+        out_ref[n, 1] = out[:, LANES:]
+
+
+def ahead_rows(base, count, place, rows, high, low):
+    return call(functools.partial(ahead_kernel, base), [((count, 2, rows.shape[0], LANES), F32)], (place, rows, high, low),
+                [SMEM] + [VMEM] * 3, (), count * 2 * 256**3)[0]
+
+
 def scan_both(base, count, place, rows, parts, high, low, tab, ktab, keep, turned):
     tokens = keep.shape[0]
     peers = len(parts) + 1
@@ -333,7 +359,7 @@
     out = [((count, 2, tokens, LANES), F32), ((count, 2) + TILE, F32), ((2 * (base + count) + CHUNKS, LANES), F32)]
     return call(functools.partial(scan_kernel, tokens // CHUNKS, base, count, peers, True, False, len(ahead)), out,
                 (tab, ktab, keep, place, rows, high, low, *parts, *ahead), [VMEM] * 3 + [SMEM] + [VMEM] * (peers + 2 + len(ahead)),
-                [pltpu.VMEM((tokens, count * GROUP), BF16)], count * 2 * 2 * 256**3)
+                (), count * 2 * 2 * 256**3)
 
 
 def scan_second(base, count, spaced, head, tab, ktab, keep, turned):
@@ -603,11 +629,12 @@
     code, side, place, bit, lower, early = lax.optimization_barrier((code, side, place, bit, lower, early))
     high, low, tab, far = basis(code, reflect, tokens // CHUNKS)
     keep, ktab, turned, decay, weight = weights(boundary, tab, prev_state[0])
+    ahead = ahead_rows(bases[-1], counts[-1], place, rows, high, low)
     done = []
     for base, count, part in zip(bases[:-1], counts[:-1], parts[:-1]):
         done.append(scan_both(base, count, place, rows, part, high, low, tab, ktab, keep, turned))
     base, count = bases[-1], counts[-1]
-    spaced, head, sent = scan_first(base, count, place, rows, parts[-1], high, low, tab, ktab, keep, [d[1] for d in done])
+    spaced, head, sent = scan_first(base, count, place, ahead, parts[-1], high, low, tab, ktab, keep, [d[1] for d in done])
     entry = entering(sent, (far[0], far[1]), "ctx", early)
     z_last, grad_last = scan_second(base, count, spaced, head, tab, ktab, keep, turned)
     quarters = merge(half, side, bit, entry, weight, [d[2] for d in done] + [grad_last])

time: 58.3 us -> 58.1 us (level)
  waiting for transfers between devices: 16.8 us -> 15.5 us
  local copies, waits for them, and re-layouts: 2.88 us -> 3.79 us
    ppermute x12, waiting for transfers between devices: 16.8 us -> 15.5 us  [swap(): return lax.ppermute(x, axis, [(i, i ^ k) for i in range(n)])]
    unnamed x8, local copies, waits for them, and re-layouts: 0.85 us -> 1.77 us
    pallas_call x10 -> x11, Pallas kernels: 10.5 us -> 10.5 us  [call(): pl.pallas_call(kernel, out_shape=shapes, in_specs=specs, out_specs=[VMEM]...]
where the time goes in v7:
time: 58.1 us; the launch traced here: 57.7 us
  Pallas kernels  20 us (34%)
  starting transfers between devices  16.8 us (29%)
  waiting for transfers between devices  15.5 us (27%)
  local copies, waits for them, and re-layouts  3.79 us (7%)
  between operations  0.84 us (1%)
  other arithmetic  0.77 us (1%)
    ppermute x12, starting transfers between devices, swap(): return lax.ppermute(x, axis, [(i, i ^ k) for i in range(n)])  16.8 us
    ppermute x12, waiting for transfers between devices, swap(): return lax.ppermute(x, axis, [(i, i ^ k) for i in range(n)])  15.5 us
    pallas_call x11, Pallas kernels, call(): pl.pallas_call(kernel, out_shape=shapes, in_specs=specs, out_specs=[VMEM]...  10.5 us
    pallas_call x3, Pallas kernels, states(): pl.pallas_call(functools.partial(state_kernel, base, sizes), grid=(count,...  5.16 us
    pallas_call x4, Pallas kernels, final(): pl.pallas_call(functools.partial(final_kernel, flips, quarters), out_shap...  4.34 us
    dynamic_slice x2, local copies, waits for them, and re-layouts, away(): lax.dynamic_slice(rows, (jnp.uint32(0), start), (rows.shape[0], count * G...  2.02 us
    unnamed x8, local copies, waits for them, and re-layouts  1.77 us
  transfers between devices with their start and end apart: 12, of which 8 were waited for; matrix products, arithmetic and copies ran while one was open for 3% of the time, Pallas kernels for 30%

profile of v7, /device:TPU:0, one launch (start us, length us, event | category | flops | bytes accessed | tf_op | source)
XLA Modules:
  0.0 57.7 jit_solution(12747377504242694312)
XLA Ops:
  0.6 0.0 copy-start
  0.6 1.0 %dynamic-slice_bitcast_fusion.1 = bf16[128,768]{1,0:T(8,128)(2,1)S(1)} fusion(bf16[1,128,4096]{2,1,0:T(8,128)(2,1)} %param.6, u32[]{:T(128)S(6)} %add.31), kind=kLoop, calls=%fused_computation.1 | loop fusion | bytes 393220 | tf_op jit(solution)/shard_map/dynamic_slice | solution.py:616
  1.7 3.1 %collective-permute-start = (bf16[128,768]{1,0:T(8,128)(2,1)S(1)}, bf16[128,768]{1,0:T(8,128)(2,1)S(1)}, u32[]{:S(2)}, u32[]{:S(2)}) collective-permute-start(bf16[128,768]{1,0:T(8,128)(2,1)S(1)} %dynamic-slice_bitcast_fusion.1), channel_id=1, source_target_pairs={{0,1},{1,0},{2,3},{3,2},{4,5},{5,4},{6,7},{7,6},{8,9},{9,8},{10,11... | collective-permute-start | bytes 589832 | tf_op jit(solution)/shard_map/ppermute | solution.py:529
  4.7 1.0 %dynamic-slice_bitcast_fusion = bf16[128,1280]{1,0:T(8,128)(2,1)S(1)} fusion(bf16[1,128,4096]{2,1,0:T(8,128)(2,1)} %param.6, u32[]{:T(128)S(6)} %mul.71), kind=kLoop, calls=%fused_computation | loop fusion | bytes 655364 | tf_op jit(solution)/shard_map/dynamic_slice | solution.py:616
  5.7 0.1 collective-permute-start.1
  5.8 0.7 %multiply_add_fusion.code_ref = s32[32,32]{1,0:T(8,128)S(1)} fusion(s32[32,32]{1,0:T(8,128)} %param.10, s32[32,32]{1,0:T(8,128)} %param.9), kind=kLoop, calls=%fused_computation.2 | loop fusion | flops 2048 | bytes 12288 | tf_op jit(solution)/shard_map/add | solution.py:628
  6.6 0.0 copy-start.2
  6.6 0.8 %copy-done.2 = f32[32,4,64]{2,1,0:T(4,128)S(1)} copy-done((f32[32,4,64]{2,1,0:T(4,128)S(1)}, f32[32,4,64]{2,1,0:T(4,128)}, u32[]{:S(2)}) %copy-start.2) | copy-done | bytes 32792
  7.4 1.1 %shard_map.77 = (bf16[8,256,256]{2,1,0:T(8,128)(2,1)S(1)}, bf16[8,256,256]{2,1,0:T(8,128)(2,1)S(1)}, f32[8,2,8,128]{3,2,1,0:T(8,128)S(1)}, f32[2,8,128]{2,1,0:T(8,128)S(1)}) custom-call(s32[32,32]{1,0:T(8,128)S(1)} %multiply_add_fusion.code_ref, f32[128,64]{1,0:T(8,128)S(1)} %bitcast.78), custom_call_target="tpu_custom_call" | custom-call | flops 536870912 | bytes 2207744 | tf_op jit(solution)/shard_map/pallas_call | solution.py:204
  8.5 0.0 copy-start.1
  8.5 0.0 copy-start.3
  8.5 0.0 copy-done
  8.5 0.3 shard_map.79.refs_4_
  8.8 0.9 %copy-done.1 = bf16[1,256,2048]{2,1,0:T(8,128)(2,1)S(1)} copy-done((bf16[1,256,2048]{2,1,0:T(8,128)(2,1)S(1)}, bf16[1,256,2048]{2,1,0:T(8,128)(2,1)}, u32[]{:S(2)}) %copy-start.1) | copy-done | bytes 1048600
  9.7 0.0 copy-done.3
  9.7 3.1 %shard_map.78 = (f32[256,128]{1,0:T(8,128)S(1)}, f32[5,8,128]{2,1,0:T(8,128)S(1)}, bf16[2048,256]{1,0:T(8,128)(2,1)S(1)}, f32[8,2,256,128]{3,2,1,0:T(8,128)S(1)}, f32[8,64,256]{2,1,0:T(8,128)S(1)}) custom-call(s32[1,256]{1,0:T(1,128)S(1)} %copy-done.3, f32[8,2,8,128]{3,2,1,0:T(8,128)S(1)} %get-tuple-element.32.tab_ref.refs_0_, bf16[256,2048]{1,0:T(8,128)(2,1)S(1)} %bitcast.77), custom_call_target="tpu_custom_call" | custom-call | flops 536870912 | bytes 4936704 | tf_op jit(solution)/shard_map/pallas_call | solution.py:204
  12.8 3.9 %collective-permute-done.1.refs_7_ = bf16[128,1280]{1,0:T(8,128)(2,1)S(1)} collective-permute-done((bf16[128,1280]{1,0:T(8,128)(2,1)S(1)}, bf16[128,1280]{1,0:T(8,128)(2,1)S(1)}, u32[]{:S(2)}, u32[]{:S(2)}) %collective-permute-start.1) | collective-permute-done | bytes 327712 | tf_op jit(solution)/shard_map/ppermute | solution.py:529
  16.7 3.3 %shard_map.80 = (f32[5,2,256,128]{3,2,1,0:T(8,128)S(1)}, f32[2,5,128]{2,1,0:T(8,128)S(1)}, f32[5,64,256]{2,1,0:T(8,128)S(1)}) custom-call(f32[8,2,8,128]{3,2,1,0:T(8,128)S(1)} %get-tuple-element.32.tab_ref.refs_0_, f32[5,8,128]{2,1,0:T(8,128)S(1)} %get-tuple-element.33.refs_1_, f32[256,128]{1,0:T(8,128)S(1)} %get-tuple-element.34.refs_2_, ...), custom_call_target="tpu_custom_call" | custom-call | flops 671088640 | bytes 6382596 | tf_op jit(solution)/shard_map/pallas_call | solution.py:204
  20.0 0.0 collective-permute-done.refs_7_
  20.0 0.8 %shard_map.81 = (f32[3,2,256,128]{3,2,1,0:T(8,128)S(1)}, f32[3,2,8,128]{3,2,1,0:T(8,128)S(1)}, f32[24,128]{1,0:T(8,128)S(1)}) custom-call(f32[8,2,8,128]{3,2,1,0:T(8,128)S(1)} %get-tuple-element.32.tab_ref.refs_0_, f32[5,8,128]{2,1,0:T(8,128)S(1)} %get-tuple-element.33.refs_1_, f32[256,128]{1,0:T(8,128)S(1)} %get-tuple-element.34.refs_2_, ...), custom_call_target="tpu_custom_call" | custom-call | flops 201326592 | bytes 3732484 | tf_op jit(solution)/shard_map/pallas_call | solution.py:204
  20.8 1.9 %collective-permute-start.2 = (f32[24,128]{1,0:T(8,128)S(1)}, f32[24,128]{1,0:T(8,128)S(1)}, u32[]{:S(2)}, u32[]{:S(2)}) collective-permute-start(f32[24,128]{1,0:T(8,128)S(1)} %get-tuple-element.40), channel_id=1, source_target_pairs={{0,2},{2,0},{4,6},{6,4},{1,3},{3,1},{5,7},{7,5},{8,10},{10,8},{12,... | collective-permute-start | bytes 36872 | tf_op jit(solution)/shard_map/ppermute | solution.py:529
  22.7 1.9 %collective-permute-done.2 = f32[24,128]{1,0:T(8,128)S(1)} collective-permute-done((f32[24,128]{1,0:T(8,128)S(1)}, f32[24,128]{1,0:T(8,128)S(1)}, u32[]{:S(2)}, u32[]{:S(2)}) %collective-permute-start.2) | collective-permute-done | bytes 12320 | tf_op jit(solution)/shard_map/ppermute | solution.py:529
  24.6 2.9 %collective-permute-start.3 = (f32[24,128]{1,0:T(8,128)S(1)}, f32[24,128]{1,0:T(8,128)S(1)}, u32[]{:S(2)}, u32[]{:S(2)}) collective-permute-start(f32[24,128]{1,0:T(8,128)S(1)} %pad_maximum_fusion), channel_id=1, source_target_pairs={{0,4},{2,6},{4,0},{6,2},{1,5},{3,7},{5,1},{7,3},{8,12},{10,14},{12... | collective-permute-start | bytes 36872 | tf_op jit(solution)/shard_map/ppermute | solution.py:529
  27.5 1.4 %shard_map.82 = (f32[3,2,256,128]{3,2,1,0:T(8,128)S(1)}, f32[3,64,256]{2,1,0:T(8,128)S(1)}) custom-call(f32[8,2,8,128]{3,2,1,0:T(8,128)S(1)} %get-tuple-element.32.tab_ref.refs_0_, f32[5,8,128]{2,1,0:T(8,128)S(1)} %get-tuple-element.33.refs_1_, f32[256,128]{1,0:T(8,128)S(1)} %get-tuple-element.34.refs_2_, ...), custom_call_target="tpu_custom_call" | custom-call | flops 201326592 | bytes 3059712 | tf_op jit(solution)/shard_map/pallas_call | solution.py:204
  28.9 0.4 collective-permute-done.3
  29.3 0.2 shard_map.83
  29.5 0.1 collective-permute-start.5
  29.6 0.5 collective-permute-start.4
  30.1 0.7 %collective-permute-done.5.refs_1_ = s16[128,256]{1,0:T(8,128)(2,1)S(1)} collective-permute-done((s16[128,256]{1,0:T(8,128)(2,1)S(1)}, s16[128,256]{1,0:T(8,128)(2,1)S(1)}, u32[]{:S(2)}, u32[]{:S(2)}) %collective-permute-start.5) | collective-permute-done | bytes 65568 | tf_op jit(solution)/shard_map/ppermute | solution.py:529
  30.8 0.1 shard_map.84
  30.9 1.8 %collective-permute-start.6 = (s16[128,256]{1,0:T(8,128)(2,1)S(1)}, s16[128,256]{1,0:T(8,128)(2,1)S(1)}, u32[]{:S(2)}, u32[]{:S(2)}) collective-permute-start(s16[128,256]{1,0:T(8,128)(2,1)S(1)} %shard_map.84), channel_id=1, source_target_pairs={{0,16},{8,24},{16,0},{24,8},{1,17},{9,25},{17,1},{25,9},{2,18},{10... | collective-permute-start | bytes 196616 | tf_op jit(solution)/shard_map/ppermute | solution.py:529
  32.7 0.0 collective-permute-done.4.refs_1_
  32.7 2.5 %collective-permute-done.6.refs_2_ = s16[128,256]{1,0:T(8,128)(2,1)S(1)} collective-permute-done((s16[128,256]{1,0:T(8,128)(2,1)S(1)}, s16[128,256]{1,0:T(8,128)(2,1)S(1)}, u32[]{:S(2)}, u32[]{:S(2)}) %collective-permute-start.6) | collective-permute-done | bytes 65568 | tf_op jit(solution)/shard_map/ppermute | solution.py:529
  35.2 0.1 shard_map.85.refs_0_
  35.3 1.9 %collective-permute-start.7 = (s16[128,256]{1,0:T(8,128)(2,1)S(1)}, s16[128,256]{1,0:T(8,128)(2,1)S(1)}, u32[]{:S(2)}, u32[]{:S(2)}) collective-permute-start(s16[128,256]{1,0:T(8,128)(2,1)S(1)} %shard_map.85.refs_0_), channel_id=1, source_target_pairs={{0,2},{2,0},{4,6},{6,4},{1,3},{3,1},{5,7},{7,5},{8,10},{10,8},{12,... | collective-permute-start | bytes 196616 | tf_op jit(solution)/shard_map/ppermute | solution.py:529
  37.2 2.5 %collective-permute-done.7.refs_1_ = s16[128,256]{1,0:T(8,128)(2,1)S(1)} collective-permute-done((s16[128,256]{1,0:T(8,128)(2,1)S(1)}, s16[128,256]{1,0:T(8,128)(2,1)S(1)}, u32[]{:S(2)}, u32[]{:S(2)}) %collective-permute-start.7) | collective-permute-done | bytes 65568 | tf_op jit(solution)/shard_map/ppermute | solution.py:529
  39.7 0.1 shard_map.86.refs_0_
  39.8 2.9 %collective-permute-start.8 = (s16[128,256]{1,0:T(8,128)(2,1)S(1)}, s16[128,256]{1,0:T(8,128)(2,1)S(1)}, u32[]{:S(2)}, u32[]{:S(2)}) collective-permute-start(s16[128,256]{1,0:T(8,128)(2,1)S(1)} %shard_map.86.refs_0_), channel_id=1, source_target_pairs={{0,4},{2,6},{4,0},{6,2},{1,5},{3,7},{5,1},{7,3},{8,12},{10,14},{12... | collective-permute-start | bytes 196616 | tf_op jit(solution)/shard_map/ppermute | solution.py:529
  42.6 2.4 %collective-permute-done.8.refs_1_ = s16[128,256]{1,0:T(8,128)(2,1)S(1)} collective-permute-done((s16[128,256]{1,0:T(8,128)(2,1)S(1)}, s16[128,256]{1,0:T(8,128)(2,1)S(1)}, u32[]{:S(2)}, u32[]{:S(2)}) %collective-permute-start.8) | collective-permute-done | bytes 65568 | tf_op jit(solution)/shard_map/ppermute | solution.py:529
  45.0 0.1 shard_map.87.x_ref
  45.1 1.8 %collective-permute-start.9 = (s16[128,256]{1,0:T(8,128)(2,1)S(1)}, s16[128,256]{1,0:T(8,128)(2,1)S(1)}, u32[]{:S(2)}, u32[]{:S(2)}) collective-permute-start(s16[128,256]{1,0:T(8,128)(2,1)S(1)} %shard_map.87.x_ref), channel_id=1, source_target_pairs={{0,16},{8,24},{16,0},{24,8},{1,17},{9,25},{17,1},{25,9},{2,18},{10... | collective-permute-start | bytes 196616 | tf_op jit(solution)/shard_map/ppermute | solution.py:529
  46.9 0.0 collective-permute-start.11
  46.9 1.3 %states.3.refs_2_ = bf16[256,2048]{1,0:T(8,128)(2,1)} custom-call(f32[2,8,128]{2,1,0:T(8,128)S(1)} %pad_maximum_fusion.1.entry_ref, f32[8,2,256,128]{3,2,1,0:T(8,128)S(1)} %get-tuple-element.42.decay_ref, bf16[8,256,256]{2,1,0:T(8,128)(2,1)S(1)} %get-tuple-element.36.high_ref.refs_5_, bf16[8,256,256]{2,1,0:T(8,128)(2,1)S(1)} %get-tuple-element.37.low_ref.refs_6_, ...), custom_call_target="tpu_custom_call" | custom-call | flops 201326592 | bytes 1800000 | tf_op jit(solution)/shard_map/states/pallas_call | solution.py:406
  48.2 1.3 %collective-permute-done.9.x_ref = s16[128,256]{1,0:T(8,128)(2,1)S(1)} collective-permute-done((s16[128,256]{1,0:T(8,128)(2,1)S(1)}, s16[128,256]{1,0:T(8,128)(2,1)S(1)}, u32[]{:S(2)}, u32[]{:S(2)}) %collective-permute-start.9) | collective-permute-done | bytes 65568 | tf_op jit(solution)/shard_map/ppermute | solution.py:529
  49.4 0.0 collective-permute-start.10
  49.4 1.9 %states.4.refs_2_ = bf16[256,2048]{1,0:T(8,128)(2,1)} custom-call(f32[2,8,128]{2,1,0:T(8,128)S(1)} %pad_maximum_fusion.1.entry_ref, f32[8,2,256,128]{3,2,1,0:T(8,128)S(1)} %get-tuple-element.42.decay_ref, bf16[8,256,256]{2,1,0:T(8,128)(2,1)S(1)} %get-tuple-element.36.high_ref.refs_5_, ...), custom_call_target="tpu_custom_call", output_to_operand_aliasing={{}: (6, {})} | custom-call | flops 301989888 | bytes 2700000 | tf_op jit(solution)/shard_map/states/pallas_call | solution.py:406
  51.4 1.9 %states.5 = bf16[256,2048]{1,0:T(8,128)(2,1)} custom-call(f32[2,8,128]{2,1,0:T(8,128)S(1)} %pad_maximum_fusion.1.entry_ref, f32[8,2,256,128]{3,2,1,0:T(8,128)S(1)} %get-tuple-element.42.decay_ref, bf16[8,256,256]{2,1,0:T(8,128)(2,1)S(1)} %get-tuple-element.36.high_ref.refs_5_, ...), custom_call_target="tpu_custom_call", output_to_operand_aliasing={{}: (6, {})} | custom-call | flops 301989888 | bytes 2700000 | tf_op jit(solution)/shard_map/states/pallas_call | solution.py:406
  53.3 1.1 %final.4.refs_0_ = f32[32,64,64]{2,1,0:T(8,128)} custom-call(s32[1]{0:T(128)} %bitcast.side_ref, s32[1]{0:T(128)} %bitcast.2.bit_ref, s16[128,256]{1,0:T(8,128)(2,1)S(1)} %shard_map.87.x_ref, bf16[8,256,256]{2,1,0:T(8,128)(2,1)S(1)} %get-tuple-element.36.high_ref.refs_5_, bf16[8,256,256]{2,1,0:T(8,128)(2,1)S(1)} %get-tuple-element.37.low_ref.refs_6_), custom_call_target="tpu_custom_call" | custom-call | flops 50331648 | bytes 800000 | tf_op jit(solution)/shard_map/final/pallas_call | solution.py:514
  54.4 0.0 collective-permute-done.11.x_ref
  54.4 1.1 %final.5.refs_0_ = f32[32,64,64]{2,1,0:T(8,128)} custom-call(s32[1]{0:T(128)} %bitcast.side_ref, s32[1]{0:T(128)} %bitcast.2.bit_ref, s16[128,256]{1,0:T(8,128)(2,1)S(1)} %collective-permute-done.11.x_ref, bf16[8,256,256]{2,1,0:T(8,128)(2,1)S(1)} %get-tuple-element.36.high_ref.refs_5_, ...), custom_call_target="tpu_custom_call", output_to_operand_aliasing={{}: (5, {})} | custom-call | flops 50331648 | bytes 800000 | tf_op jit(solution)/shard_map/final/pallas_call | solution.py:514
  55.5 1.1 %final.6.refs_0_ = f32[32,64,64]{2,1,0:T(8,128)} custom-call(s32[1]{0:T(128)} %bitcast.side_ref, s32[1]{0:T(128)} %bitcast.2.bit_ref, s16[128,256]{1,0:T(8,128)(2,1)S(1)} %collective-permute-done.9.x_ref, bf16[8,256,256]{2,1,0:T(8,128)(2,1)S(1)} %get-tuple-element.36.high_ref.refs_5_, ...), custom_call_target="tpu_custom_call", output_to_operand_aliasing={{}: (5, {})} | custom-call | flops 50331648 | bytes 800000 | tf_op jit(solution)/shard_map/final/pallas_call | solution.py:514
  56.6 0.0 collective-permute-done.10.x_ref
  56.6 1.1 %final.7 = f32[32,64,64]{2,1,0:T(8,128)} custom-call(s32[1]{0:T(128)} %bitcast.side_ref, s32[1]{0:T(128)} %bitcast.2.bit_ref, s16[128,256]{1,0:T(8,128)(2,1)S(1)} %collective-permute-done.10.x_ref, bf16[8,256,256]{2,1,0:T(8,128)(2,1)S(1)} %get-tuple-element.36.high_ref.refs_5_, ...), custom_call_target="tpu_custom_call", output_to_operand_aliasing={{}: (5, {})} | custom-call | flops 50331648 | bytes 800000 | tf_op jit(solution)/shard_map/final/pallas_call | solution.py:514
  (6 shorter events, 0.0 us)
Async XLA Ops:
  0.6 7.9 %copy-start = (bf16[1,128,4096]{2,1,0:T(8,128)(2,1)S(1)}, bf16[1,128,4096]{2,1,0:T(8,128)(2,1)}, u32[]{:S(2)}) copy-start(bf16[1,128,4096]{2,1,0:T(8,128)(2,1)} %param.6) | copy-start | bytes 3145732
  1.7 18.3 %collective-permute-start = (bf16[128,768]{1,0:T(8,128)(2,1)S(1)}, bf16[128,768]{1,0:T(8,128)(2,1)S(1)}, u32[]{:S(2)}, u32[]{:S(2)}) collective-permute-start(bf16[128,768]{1,0:T(8,128)(2,1)S(1)} %dynamic-slice_bitcast_fusion.1), channel_id=1, source_target_pairs={{0,1},{1,0},{2,3},{3,2},{4,5},{5,4},{6,7},{7,6},{8,9},{9,8},{10,11... | collective-permute-start | bytes 589832 | tf_op jit(solution)/shard_map/ppermute | solution.py:529
  5.7 10.9 %collective-permute-start.1 = (bf16[128,1280]{1,0:T(8,128)(2,1)S(1)}, bf16[128,1280]{1,0:T(8,128)(2,1)S(1)}, u32[]{:S(2)}, u32[]{:S(2)}) collective-permute-start(bf16[128,1280]{1,0:T(8,128)(2,1)S(1)} %dynamic-slice_bitcast_fusion), channel_id=1, source_target_pairs={{0,1},{1,0},{2,3},{3,2},{4,5},{5,4},{6,7},{7,6},{8,9},{9,8},{10,11... | collective-permute-start | bytes 983048 | tf_op jit(solution)/shard_map/ppermute | solution.py:529
  6.6 0.8 %copy-start.2 = (f32[32,4,64]{2,1,0:T(4,128)S(1)}, f32[32,4,64]{2,1,0:T(4,128)}, u32[]{:S(2)}) copy-start(f32[32,4,64]{2,1,0:T(4,128)} %param.11) | copy-start | bytes 98308
  8.5 1.2 %copy-start.1 = (bf16[1,256,2048]{2,1,0:T(8,128)(2,1)S(1)}, bf16[1,256,2048]{2,1,0:T(8,128)(2,1)}, u32[]{:S(2)}) copy-start(bf16[1,256,2048]{2,1,0:T(8,128)(2,1)} %param.7) | copy-start | bytes 3145732
  8.5 1.2 %copy-start.3 = (s32[1,256]{1,0:T(1,128)S(1)}, s32[1,256]{1,0:T(1,128)}, u32[]{:S(2)}) copy-start(s32[1,256]{1,0:T(1,128)} %boundary_ref.1) | copy-start | bytes 3076
  20.8 3.8 %collective-permute-start.2 = (f32[24,128]{1,0:T(8,128)S(1)}, f32[24,128]{1,0:T(8,128)S(1)}, u32[]{:S(2)}, u32[]{:S(2)}) collective-permute-start(f32[24,128]{1,0:T(8,128)S(1)} %get-tuple-element.40), channel_id=1, source_target_pairs={{0,2},{2,0},{4,6},{6,4},{1,3},{3,1},{5,7},{7,5},{8,10},{10,8},{12,... | collective-permute-start | bytes 36872 | tf_op jit(solution)/shard_map/ppermute | solution.py:529
  24.6 4.7 %collective-permute-start.3 = (f32[24,128]{1,0:T(8,128)S(1)}, f32[24,128]{1,0:T(8,128)S(1)}, u32[]{:S(2)}, u32[]{:S(2)}) collective-permute-start(f32[24,128]{1,0:T(8,128)S(1)} %pad_maximum_fusion), channel_id=1, source_target_pairs={{0,4},{2,6},{4,0},{6,2},{1,5},{3,7},{5,1},{7,3},{8,12},{10,14},{12... | collective-permute-start | bytes 36872 | tf_op jit(solution)/shard_map/ppermute | solution.py:529
  29.5 1.3 %collective-permute-start.5 = (s16[128,256]{1,0:T(8,128)(2,1)S(1)}, s16[128,256]{1,0:T(8,128)(2,1)S(1)}, u32[]{:S(2)}, u32[]{:S(2)}) collective-permute-start(s16[128,256]{1,0:T(8,128)(2,1)S(1)} %get-tuple-element.55), channel_id=1, source_target_pairs={{0,8},{8,0},{16,24},{24,16},{1,9},{9,1},{17,25},{25,17},{2,10},{10... | collective-permute-start | bytes 196616 | tf_op jit(solution)/shard_map/ppermute | solution.py:529
  29.6 3.1 %collective-permute-start.4 = (s16[128,256]{1,0:T(8,128)(2,1)S(1)}, s16[128,256]{1,0:T(8,128)(2,1)S(1)}, u32[]{:S(2)}, u32[]{:S(2)}) collective-permute-start(s16[128,256]{1,0:T(8,128)(2,1)S(1)} %get-tuple-element.53), channel_id=1, source_target_pairs={{0,8},{8,0},{16,24},{24,16},{1,9},{9,1},{17,25},{25,17},{2,10},{10... | collective-permute-start | bytes 196616 | tf_op jit(solution)/shard_map/ppermute | solution.py:529
  30.9 4.3 %collective-permute-start.6 = (s16[128,256]{1,0:T(8,128)(2,1)S(1)}, s16[128,256]{1,0:T(8,128)(2,1)S(1)}, u32[]{:S(2)}, u32[]{:S(2)}) collective-permute-start(s16[128,256]{1,0:T(8,128)(2,1)S(1)} %shard_map.84), channel_id=1, source_target_pairs={{0,16},{8,24},{16,0},{24,8},{1,17},{9,25},{17,1},{25,9},{2,18},{10... | collective-permute-start | bytes 196616 | tf_op jit(solution)/shard_map/ppermute | solution.py:529
  35.3 4.3 %collective-permute-start.7 = (s16[128,256]{1,0:T(8,128)(2,1)S(1)}, s16[128,256]{1,0:T(8,128)(2,1)S(1)}, u32[]{:S(2)}, u32[]{:S(2)}) collective-permute-start(s16[128,256]{1,0:T(8,128)(2,1)S(1)} %shard_map.85.refs_0_), channel_id=1, source_target_pairs={{0,2},{2,0},{4,6},{6,4},{1,3},{3,1},{5,7},{7,5},{8,10},{10,8},{12,... | collective-permute-start | bytes 196616 | tf_op jit(solution)/shard_map/ppermute | solution.py:529
  39.8 5.2 %collective-permute-start.8 = (s16[128,256]{1,0:T(8,128)(2,1)S(1)}, s16[128,256]{1,0:T(8,128)(2,1)S(1)}, u32[]{:S(2)}, u32[]{:S(2)}) collective-permute-start(s16[128,256]{1,0:T(8,128)(2,1)S(1)} %shard_map.86.refs_0_), channel_id=1, source_target_pairs={{0,4},{2,6},{4,0},{6,2},{1,5},{3,7},{5,1},{7,3},{8,12},{10,14},{12... | collective-permute-start | bytes 196616 | tf_op jit(solution)/shard_map/ppermute | solution.py:529
  45.1 4.3 %collective-permute-start.9 = (s16[128,256]{1,0:T(8,128)(2,1)S(1)}, s16[128,256]{1,0:T(8,128)(2,1)S(1)}, u32[]{:S(2)}, u32[]{:S(2)}) collective-permute-start(s16[128,256]{1,0:T(8,128)(2,1)S(1)} %shard_map.87.x_ref), channel_id=1, source_target_pairs={{0,16},{8,24},{16,0},{24,8},{1,17},{9,25},{17,1},{25,9},{2,18},{10... | collective-permute-start | bytes 196616 | tf_op jit(solution)/shard_map/ppermute | solution.py:529
  46.9 7.5 %collective-permute-start.11 = (s16[128,256]{1,0:T(8,128)(2,1)S(1)}, s16[128,256]{1,0:T(8,128)(2,1)S(1)}, u32[]{:S(2)}, u32[]{:S(2)}) collective-permute-start(s16[128,256]{1,0:T(8,128)(2,1)S(1)} %shard_map.87.x_ref), channel_id=1, source_target_pairs={{0,8},{8,0},{16,24},{24,16},{1,9},{9,1},{17,25},{25,17},{2,10},{10... | collective-permute-start | bytes 196616 | tf_op jit(solution)/shard_map/ppermute | solution.py:529
  49.4 7.2 %collective-permute-start.10 = (s16[128,256]{1,0:T(8,128)(2,1)S(1)}, s16[128,256]{1,0:T(8,128)(2,1)S(1)}, u32[]{:S(2)}, u32[]{:S(2)}) collective-permute-start(s16[128,256]{1,0:T(8,128)(2,1)S(1)} %collective-permute-done.9.x_ref), channel_id=1, source_target_pairs={{0,8},{8,0},{16,24},{24,16},{1,9},{9,1},{17,25},{25,17},{2,10},{10... | collective-permute-start | bytes 196616 | tf_op jit(solution)/shard_map/ppermute | solution.py:529
